TPU v7x, 32 devices: a whole 2x2x4 slice. The times are simulated.
32 devices in a mesh: dp: 8 (over z, x), tensor: 4 (over y, core).
Axes of the slice: x: 2, y: 2, z: 4, core: 2. Of those that a mesh axis runs over, the one named last changes fastest.
Arguments:
- layer_input: float32 [16384, 1024], P(('dp', 'tensor')), may hold values from -6 to 6
- segment_ids: int32 [8, 1024], P('dp'), may hold values from 0 to 3, never falling along the last dimension, each value on 1 to 512 neighbouring positions
- ln_attn_gain: float32 [2, 1024], replicated, may hold values from 0.5 to 1.5
- w_query: float32 [2, 1024, 1024], P(None, 'dp', 'tensor'), may hold values from -0.1875 to 0.1875
- w_key: float32 [2, 1024, 1024], P(None, 'dp', 'tensor'), may hold values from -0.1875 to 0.1875
- w_value: float32 [2, 1024, 1024], P(None, 'dp', 'tensor'), may hold values from -0.1875 to 0.1875
- head_scale: float32 [2, 16], replicated, may hold values from 0.5 to 1.5
- w_out: float32 [2, 1024, 1024], P(None, 'tensor', 'dp'), may hold values from -0.1875 to 0.1875
- ln_post_gain: float32 [2, 1024], replicated, may hold values from 0.5 to 1.5
- ln_ffn_gain: float32 [2, 1024], replicated, may hold values from 0.5 to 1.5
- w_up: float32 [2, 1024, 4096], P(None, 'dp', 'tensor'), may hold values from -0.1875 to 0.1875
- ln_mid_gain: float32 [2, 4096], replicated, may hold values from 0.5 to 1.5
- w_down: float32 [2, 4096, 1024], P(None, 'tensor', 'dp'), may hold values from -0.09375 to 0.09375
- out_cotangent: float32 [16384, 1024], P(('dp', 'tensor')), may hold values from -6 to 6
Outputs:
- block_output: float32 [16384, 1024], P(('dp', 'tensor'))
- input_grad: float32 [16384, 1024], P(('dp', 'tensor'))
- grad_ln_attn_gain: float32 [2, 1024], replicated
- grad_w_query: float32 [2, 1024, 1024], P(None, 'dp', 'tensor')
- grad_w_key: float32 [2, 1024, 1024], P(None, 'dp', 'tensor')
- grad_w_value: float32 [2, 1024, 1024], P(None, 'dp', 'tensor')
- grad_head_scale: float32 [2, 16], replicated
- grad_w_out: float32 [2, 1024, 1024], P(None, 'tensor', 'dp')
- grad_ln_post_gain: float32 [2, 1024], replicated
- grad_ln_ffn_gain: float32 [2, 1024], replicated
- grad_w_up: float32 [2, 1024, 4096], P(None, 'dp', 'tensor')
- grad_ln_mid_gain: float32 [2, 4096], replicated
- grad_w_down: float32 [2, 4096, 1024], P(None, 'tensor', 'dp')
Inputs may be any that keep to these rules, and one draw needn't show every extreme that they name: `segment_ids`: along each row numbers never fall; each of the 4 continuations has 1 to 512 positions, and one has exactly 512.
All inputs are finite; a program needn't handle non-finite values.
Results may differ from a plain program's by a relative error of at most 0.017.
The roundings to bfloat16 on the way count: a program that leaves them out, or rounds other values in their place, can miss the bound.
Values may be sent and summed in bfloat16 or wider, within the bound.
A program may use at most 256 MiB of HBM per device.

v0:
```python
import jax
import jax.numpy as jnp
from jax import lax
from jax.sharding import PartitionSpec as P

H = 16
HD = 64
FF = 4096
LAYERS = 2
PROMPT = 1024


NORM_EPSILON = 1e-05
MASKED_SCORE = -1e30


def in_blocks(array, dim, length):
    dims = array.shape
    parts = array.reshape(*dims[:dim], length, dims[dim] // length, *dims[dim + 1 :])
    return jnp.moveaxis(parts, dim, 0)


def sum_at_owner(array, axis, dim):
    parts = in_blocks(array, dim, lax.axis_size(axis))
    arrived = lax.all_to_all(parts, axis, split_axis=0, concat_axis=0, tiled=True)
    return arrived.astype(jnp.float32).sum(axis=0)


def side_by_side(arrays, axis, dim, along):
    both = jnp.concatenate(arrays, axis=along)
    filled, at, finished = (sum_at_owner(both, axis, dim), 0, [])
    for a in arrays:
        finished.append(lax.slice_in_dim(filled, at, at + a.shape[along], axis=along))
        at += a.shape[along]
    return tuple(finished)


def tanh_gelu(inputs):
    return (
        0.5
        * inputs
        * (1.0 + jnp.tanh(0.7978845608028654 * (inputs + 0.044715 * inputs * inputs * inputs)))
    )


def normalize(values):
    center = values - jnp.mean(values, -1, keepdims=True)
    factor = lax.rsqrt(jnp.mean(center * center, -1, keepdims=True) + NORM_EPSILON)
    return (center * factor, factor)


def norm_back(grad_norm, normed, factor):
    return factor * (
        grad_norm
        - jnp.mean(grad_norm, -1, keepdims=True)
        - normed * jnp.mean(grad_norm * normed, -1, keepdims=True)
    )


def outer_sum(left, right):
    return lax.dot_general(
        left, right, (((0,), (0,)), ((), ())), preferred_element_type=jnp.float32
    )


def times_transpose(left, right):
    return lax.dot_general(
        left, right, (((1,), (1,)), ((), ())), preferred_element_type=jnp.float32
    )


def visible(offset, block_size, seg_full):
    length = seg_full.shape[0]
    query_pos = offset + jnp.arange(block_size, dtype=jnp.int32)
    key_pos = jnp.arange(length, dtype=jnp.int32)
    query_seg = lax.dynamic_slice_in_dim(seg_full, offset, block_size)
    same_doc = query_seg[:, None] == seg_full[None, :]
    return (key_pos[None, :] <= query_pos[:, None]) & ((key_pos[None, :] < PROMPT) | same_doc)


def block_scores(query_block, all_keys, offset, seg_full):
    scores = (
        jnp.einsum("qhd,khd->hqk", query_block, all_keys, preferred_element_type=jnp.float32)
        * 0.125
    )
    return jnp.where(visible(offset, query_block.shape[0], seg_full)[None], scores, MASKED_SCORE)


def attend_forward(queries, all_keys, values, seg_full):
    length, head_count, head_width = queries.shape
    block_size = min(512, length)
    blocks = length // block_size

    def one_block(block_item):
        query_block, offset = block_item
        scores = block_scores(query_block, all_keys, offset, seg_full)
        highest = jnp.max(scores, -1, keepdims=True)
        exponents = jnp.exp(scores - highest)
        denominator = jnp.sum(exponents, -1, keepdims=True)
        weights_low = (exponents / denominator).astype(jnp.bfloat16)
        mixture = jnp.einsum(
            "hqk,khd->qhd", weights_low, values, preferred_element_type=jnp.float32
        )
        return (mixture, (highest + jnp.log(denominator))[..., 0])

    offsets = jnp.arange(blocks, dtype=jnp.int32) * block_size
    mixture, logsum = lax.map(
        one_block, (queries.reshape(blocks, block_size, head_count, head_width), offsets)
    )
    return (mixture.reshape(length, head_count * head_width), logsum)


def attend_backward(queries, all_keys, values, grad_mixture, logsum, seg_full):
    length, head_count, head_width = queries.shape
    block_size = min(512, length)
    blocks = length // block_size

    def one_block(carry, block_item):
        grad_keys, grad_values = carry
        query_block, grad_block, logsum_block, offset = block_item
        scores = block_scores(query_block, all_keys, offset, seg_full)
        softmax_rows = jnp.exp(scores - logsum_block[..., None])
        grad_probs = jnp.einsum(
            "qhd,khd->hqk", grad_block, values, preferred_element_type=jnp.float32
        )
        inner = jnp.sum(softmax_rows * grad_probs, -1, keepdims=True)
        grad_scores = (softmax_rows * (grad_probs - inner)).astype(jnp.bfloat16)
        grad_query = (
            jnp.einsum("hqk,khd->qhd", grad_scores, all_keys, preferred_element_type=jnp.float32)
            * 0.125
        )
        grad_keys = (
            grad_keys
            + jnp.einsum(
                "hqk,qhd->khd", grad_scores, query_block, preferred_element_type=jnp.float32
            )
            * 0.125
        )
        grad_values = grad_values + jnp.einsum(
            "hqk,qhd->khd",
            softmax_rows.astype(jnp.bfloat16),
            grad_block,
            preferred_element_type=jnp.float32,
        )
        return ((grad_keys, grad_values), grad_query)

    offsets = jnp.arange(blocks, dtype=jnp.int32) * block_size
    zeros = jnp.zeros(all_keys.shape, jnp.float32)
    block_shape = (blocks, block_size, head_count, head_width)
    (grad_keys, grad_values), grad_queries = lax.scan(
        one_block,
        (zeros, zeros),
        (queries.reshape(block_shape), grad_mixture.reshape(block_shape), logsum, offsets),
    )
    flat_shape = (length, head_count * head_width)
    return (
        grad_queries.reshape(flat_shape).astype(jnp.bfloat16),
        grad_keys.reshape(flat_shape).astype(jnp.bfloat16),
        grad_values.reshape(flat_shape).astype(jnp.bfloat16),
    )


def gather_rows(values):
    return lax.all_gather(values, "tensor", axis=0, tiled=True)


def gather_grads(values):
    return lax.all_gather(values, "tensor", axis=0, tiled=True)


def sum_rows(values):
    return lax.psum_scatter(values, "tensor", scatter_dimension=0, tiled=True)


def sum_grads(values):
    return lax.psum_scatter(values, "tensor", scatter_dimension=0, tiled=True)


def local(
    layer_input,
    segment_ids,
    ln_attn_gain,
    w_query,
    w_key,
    w_value,
    head_scale,
    w_out,
    ln_post_gain,
    ln_ffn_gain,
    w_up,
    ln_mid_gain,
    w_down,
    out_cotangent,
):
    tensor_size = lax.axis_size("tensor")
    tensor_index = lax.axis_index("tensor")
    local_heads = H // tensor_size
    local_hidden = FF // tensor_size
    seg_full = jnp.concatenate([jnp.full((PROMPT,), -1, dtype=jnp.int32), segment_ids[0]])
    stream = layer_input
    saved = []
    for layer_index in range(LAYERS):
        normed_one, factor_one = normalize(stream)
        h_attn = (normed_one * ln_attn_gain[layer_index]).astype(jnp.bfloat16)
        gathered_attn = gather_rows(h_attn)
        attn_set = (
            lax.all_gather(w_query[layer_index].astype(jnp.bfloat16), "dp", axis=0, tiled=True),
            lax.all_gather(w_key[layer_index].astype(jnp.bfloat16), "dp", axis=0, tiled=True),
            lax.all_gather(w_value[layer_index].astype(jnp.bfloat16), "dp", axis=0, tiled=True),
            lax.all_gather(w_out[layer_index].astype(jnp.bfloat16), "dp", axis=1, tiled=True),
        )
        length = gathered_attn.shape[0]
        head_shape = (length, local_heads, HD)
        queries = (
            jnp.dot(gathered_attn, attn_set[0], preferred_element_type=jnp.float32)
            .astype(jnp.bfloat16)
            .reshape(head_shape)
        )
        all_keys = (
            jnp.dot(gathered_attn, attn_set[1], preferred_element_type=jnp.float32)
            .astype(jnp.bfloat16)
            .reshape(head_shape)
        )
        values = (
            jnp.dot(gathered_attn, attn_set[2], preferred_element_type=jnp.float32)
            .astype(jnp.bfloat16)
            .reshape(head_shape)
        )
        mixture, logsum = attend_forward(queries, all_keys, values, seg_full)
        scale_local = jnp.repeat(
            lax.dynamic_slice_in_dim(
                head_scale[layer_index], tensor_index * local_heads, local_heads
            ),
            HD,
        )
        scaled = (mixture * scale_local).astype(jnp.bfloat16)
        attn_sum = sum_rows(jnp.dot(scaled, attn_set[3], preferred_element_type=jnp.float32))
        normed_two, factor_two = normalize(attn_sum)
        middle = stream + normed_two * ln_post_gain[layer_index]
        normed_three, factor_three = normalize(middle)
        h_ffn = (normed_three * ln_ffn_gain[layer_index]).astype(jnp.bfloat16)
        gathered_ffn = gather_rows(h_ffn)
        ffn_set = (
            lax.all_gather(w_up[layer_index].astype(jnp.bfloat16), "dp", axis=0, tiled=True),
            lax.all_gather(w_down[layer_index].astype(jnp.bfloat16), "dp", axis=1, tiled=True),
        )
        hidden_pre = jnp.dot(gathered_ffn, ffn_set[0], preferred_element_type=jnp.float32)
        activated = tanh_gelu(hidden_pre)
        row_stats = lax.psum((jnp.sum(activated, -1), jnp.sum(activated * activated, -1)), "tensor")
        hidden_mean = (row_stats[0] / FF)[:, None]
        hidden_factor = lax.rsqrt(
            row_stats[1][:, None] / FF - hidden_mean * hidden_mean + NORM_EPSILON
        )
        normed_four = (activated - hidden_mean) * hidden_factor
        gain_mid = lax.dynamic_slice_in_dim(
            ln_mid_gain[layer_index], tensor_index * local_hidden, local_hidden
        )
        hidden_out = (normed_four * gain_mid).astype(jnp.bfloat16)
        stream = middle + sum_rows(
            jnp.dot(hidden_out, ffn_set[1], preferred_element_type=jnp.float32)
        )
        saved.append(
            (
                normed_one,
                factor_one,
                gathered_attn,
                attn_set,
                queries,
                all_keys,
                values,
                mixture,
                logsum,
                scale_local,
                scaled,
                normed_two,
                factor_two,
                normed_three,
                factor_three,
                gathered_ffn,
                ffn_set,
                hidden_pre,
                normed_four,
                hidden_factor,
                gain_mid,
                hidden_out,
            )
        )
    grad_stream = out_cotangent
    matrix_grads = [None] * LAYERS
    attn_gain_grads = [None] * LAYERS
    post_gain_grads = [None] * LAYERS
    ffn_gain_grads = [None] * LAYERS
    head_grads = [None] * LAYERS
    mid_grads = [None] * LAYERS
    for layer_index in reversed(range(LAYERS)):
        (
            normed_one,
            factor_one,
            gathered_attn,
            attn_set,
            queries,
            all_keys,
            values,
            mixture,
            logsum,
            scale_local,
            scaled,
            normed_two,
            factor_two,
            normed_three,
            factor_three,
            gathered_ffn,
            ffn_set,
            hidden_pre,
            normed_four,
            hidden_factor,
            gain_mid,
            hidden_out,
        ) = saved[layer_index]
        attn_set = (
            lax.all_gather(w_query[layer_index].astype(jnp.bfloat16), "dp", axis=0, tiled=True),
            lax.all_gather(w_key[layer_index].astype(jnp.bfloat16), "dp", axis=0, tiled=True),
            lax.all_gather(w_value[layer_index].astype(jnp.bfloat16), "dp", axis=0, tiled=True),
            lax.all_gather(w_out[layer_index].astype(jnp.bfloat16), "dp", axis=1, tiled=True),
        )
        ffn_set = (
            lax.all_gather(w_up[layer_index].astype(jnp.bfloat16), "dp", axis=0, tiled=True),
            lax.all_gather(w_down[layer_index].astype(jnp.bfloat16), "dp", axis=1, tiled=True),
        )
        length = gathered_attn.shape[0]
        head_shape = (length, local_heads, HD)
        grad_down_in = gather_grads(grad_stream.astype(jnp.bfloat16))
        grad_down = outer_sum(hidden_out, grad_down_in)
        grad_hidden = times_transpose(grad_down_in, ffn_set[1])
        mid_grads[layer_index] = jnp.sum(grad_hidden * normed_four, 0)
        grad_normed = grad_hidden * gain_mid
        back_stats = lax.psum(
            (jnp.sum(grad_normed, -1), jnp.sum(grad_normed * normed_four, -1)), "tensor"
        )
        grad_active = hidden_factor * (
            grad_normed
            - (back_stats[0] / FF)[:, None]
            - normed_four * (back_stats[1] / FF)[:, None]
        )
        _, gelu_back = jax.vjp(tanh_gelu, hidden_pre)
        grad_pre = gelu_back(grad_active)[0].astype(jnp.bfloat16)
        grad_upper = outer_sum(gathered_ffn, grad_pre)
        grad_ffn_in = sum_grads(times_transpose(grad_pre, ffn_set[0]))
        ffn_gain_grads[layer_index] = jnp.sum(grad_ffn_in * normed_three, 0)
        grad_middle = grad_stream + norm_back(
            grad_ffn_in * ln_ffn_gain[layer_index], normed_three, factor_three
        )
        ffn_pair = (
            lax.psum_scatter(grad_upper, "dp", scatter_dimension=0, tiled=True),
            lax.psum_scatter(grad_down, "dp", scatter_dimension=1, tiled=True),
        )
        post_gain_grads[layer_index] = jnp.sum(grad_middle * normed_two, 0)
        grad_attn_out = norm_back(
            grad_middle * ln_post_gain[layer_index], normed_two, factor_two
        ).astype(jnp.bfloat16)
        grad_out_in = gather_grads(grad_attn_out)
        grad_w_outer = outer_sum(scaled, grad_out_in)
        grad_scaled = times_transpose(grad_out_in, attn_set[3])
        head_grads[layer_index] = jnp.sum((grad_scaled * mixture).reshape(head_shape), (0, 2))
        grad_mixture = (grad_scaled * scale_local).astype(jnp.bfloat16)
        grad_queries, grad_keys, grad_values = attend_backward(
            queries, all_keys, values, grad_mixture.reshape(head_shape), logsum, seg_full
        )
        grad_wq = outer_sum(gathered_attn, grad_queries)
        grad_wk = outer_sum(gathered_attn, grad_keys)
        grad_wv = outer_sum(gathered_attn, grad_values)
        grad_attn_local = (
            times_transpose(grad_queries, attn_set[0])
            + times_transpose(grad_keys, attn_set[1])
            + times_transpose(grad_values, attn_set[2])
        )
        grad_attn_in = sum_grads(grad_attn_local)
        attn_gain_grads[layer_index] = jnp.sum(grad_attn_in * normed_one, 0)
        grad_stream = grad_middle + norm_back(
            grad_attn_in * ln_attn_gain[layer_index], normed_one, factor_one
        )
        attn_four = (
            *side_by_side(
                (
                    grad_wq.astype(jnp.bfloat16),
                    grad_wk.astype(jnp.bfloat16),
                    grad_wv.astype(jnp.bfloat16),
                ),
                "dp",
                0,
                1,
            ),
            sum_at_owner(grad_w_outer.astype(jnp.bfloat16), "dp", 1),
        )
        matrix_grads[layer_index] = (
            attn_four[0],
            attn_four[1],
            attn_four[2],
            attn_four[3],
            ffn_pair[0],
            ffn_pair[1],
        )
    stacked = [
        jnp.stack([matrix_grads[index][member] for index in range(LAYERS)]) for member in range(6)
    ]
    head_full = jnp.stack(
        [
            lax.dynamic_update_slice_in_dim(
                jnp.zeros((H,), jnp.float32), head_grads[index], tensor_index * local_heads, 0
            )
            for index in range(LAYERS)
        ]
    )
    mid_full = jnp.stack(
        [
            lax.dynamic_update_slice_in_dim(
                jnp.zeros((FF,), jnp.float32), mid_grads[index], tensor_index * local_hidden, 0
            )
            for index in range(LAYERS)
        ]
    )
    small_sums = lax.psum(
        (
            jnp.stack(attn_gain_grads),
            head_full,
            jnp.stack(post_gain_grads),
            jnp.stack(ffn_gain_grads),
            mid_full,
        ),
        ("dp", "tensor"),
    )
    return (
        stream,
        grad_stream,
        small_sums[0],
        stacked[0],
        stacked[1],
        stacked[2],
        small_sums[1],
        stacked[3],
        small_sums[2],
        small_sums[3],
        stacked[4],
        small_sums[4],
        stacked[5],
    )


def solution(mesh):
    in_specs = (
        P(("dp", "tensor"), None),
        P("dp", None),
        P(),
        P(None, "dp", "tensor"),
        P(None, "dp", "tensor"),
        P(None, "dp", "tensor"),
        P(),
        P(None, "tensor", "dp"),
        P(),
        P(),
        P(None, "dp", "tensor"),
        P(),
        P(None, "tensor", "dp"),
        P(("dp", "tensor"), None),
    )
    out_specs = (
        P(("dp", "tensor"), None),
        P(("dp", "tensor"), None),
        P(),
        P(None, "dp", "tensor"),
        P(None, "dp", "tensor"),
        P(None, "dp", "tensor"),
        P(),
        P(None, "tensor", "dp"),
        P(),
        P(),
        P(None, "dp", "tensor"),
        P(),
        P(None, "tensor", "dp"),
    )
    return jax.shard_map(local, mesh=mesh, in_specs=in_specs, out_specs=out_specs, check_vma=False)
```

profile of v0, /device:TPU:0, one launch (start us, length us, event | category | flops | bytes accessed | tf_op | source)
XLA Modules:
  0.0 2211.7 jit_solution(11137312576364839278)
XLA Ops:
  18.7 30.7 %all-gather.3 = bf16[1,256,1024]{2,1,0:T(8,128)(2,1)} all-gather(bf16[1,256,128]{2,1,0:T(8,128)(2,1)S(1)} %get-tuple-element.636), channel_id=5, replica_groups=mesh['dp'=8,'tensor'=4] {'dp'}, dimensions={2}, use_global_device_ids=true | all-gather | bytes 589824 | tf_op jit(solution)/shard_map/all_gather | solution.py:210
  49.4 33.5 %all-gather.2 = bf16[1,1024,256]{2,1,0:T(8,128)(2,1)} all-gather(bf16[1,128,256]{2,1,0:T(8,128)(2,1)S(1)} %get-tuple-element.630), channel_id=4, replica_groups=mesh['dp'=8,'tensor'=4] {'dp'}, dimensions={1}, use_global_device_ids=true | all-gather | bytes 589824 | tf_op jit(solution)/shard_map/all_gather | solution.py:209
  82.9 33.4 %all-gather.1 = bf16[1,1024,256]{2,1,0:T(8,128)(2,1)} all-gather(bf16[1,128,256]{2,1,0:T(8,128)(2,1)S(1)} %get-tuple-element.632), channel_id=3, replica_groups=mesh['dp'=8,'tensor'=4] {'dp'}, dimensions={1}, use_global_device_ids=true | all-gather | bytes 589824 | tf_op jit(solution)/shard_map/all_gather | solution.py:208
  116.3 31.3 %all-gather = bf16[1,1024,256]{2,1,0:T(8,128)(2,1)S(1)} all-gather(bf16[1,128,256]{2,1,0:T(8,128)(2,1)S(1)} %get-tuple-element.634), channel_id=2, replica_groups=mesh['dp'=8,'tensor'=4] {'dp'}, dimensions={1}, use_global_device_ids=true | all-gather | bytes 589824 | tf_op jit(solution)/shard_map/all_gather | solution.py:207
  160.8 70.5 %while.54 = (s32[]{:T(128)}, f32[4,512,4,64]{1,3,2,0:T(8,128)}, f32[4,4,512]{2,1,0:T(4,128)S(1)}, s32[4]{0:T(128)S(1)}, s32[2048]{0:T(1024)S(1)}, /*index=5*/bf1...) while((s32[]{:T(128)}, f32[4,512,4,64]{1,3,2,0:T(8,128)}, ...), condition=%wide.region_5.6_spmd, body=%wide.region_2.5_spmd.sunk | while | flops 1128268288 | bytes 57497784 | solution.py:107
  252.1 67.3 %reduce-scatter.13.cloned.1.call-done = f32[512,1024]{1,0:T(8,128)} async-done(((f32[2048,1024]{1,0:T(8,128)}), f32[512,1024]{1,0:T(8,128)}) %reduce-scatter.13.cloned.1.call-update) | async-done | bytes 2097168 | tf_op jit(solution)/shard_map/reduce_scatter | solution.py:172
  329.8 32.7 %all-gather.27.cloned.1.call-done = bf16[2048,1024]{1,0:T(8,128)(2,1)} async-done(((bf16[512,1024]{1,0:T(8,128)(2,1)}), bf16[2048,1024]{1,0:T(8,128)(2,1)}) %all-gather.27.cloned.1.call-update) | async-done | bytes 4194320 | tf_op jit(solution)/shard_map/all_gather | solution.py:164
  385.3 30.5 %all-gather.43.cloned.1.call-done = bf16[1,1024,1024]{2,1,0:T(8,128)(2,1)} async-done(((bf16[1,1024,128]{2,1,0:T(8,128)(2,1)}), bf16[1,1024,1024]{2,1,0:T(8,128)(2,1)}) %all-gather.43.cloned.1.call-update) | async-done | bytes 2097168 | tf_op jit(solution)/shard_map/all_gather | solution.py:245
  427.5 69.9 %reduce-scatter.15.cloned.1.call-done = f32[512,1024]{1,0:T(8,128)} async-done(((f32[2048,1024]{1,0:T(8,128)}), f32[512,1024]{1,0:T(8,128)}) %reduce-scatter.15.cloned.1.call-update) | async-done | bytes 2097168 | tf_op jit(solution)/shard_map/reduce_scatter | solution.py:172
  502.7 29.0 %all-gather.9 = bf16[1,256,1024]{2,1,0:T(8,128)(2,1)} all-gather(bf16[1,256,128]{2,1,0:T(8,128)(2,1)S(1)} %copy-done.69), channel_id=11, replica_groups=mesh['dp'=8,'tensor'=4] {'dp'}, dimensions={2}, use_global_device_ids=true | all-gather | bytes 589824 | tf_op jit(solution)/shard_map/all_gather | solution.py:210
  531.7 31.7 %all-gather.8 = bf16[1,1024,256]{2,1,0:T(8,128)(2,1)S(1)} all-gather(bf16[1,128,256]{2,1,0:T(8,128)(2,1)S(1)} %copy-done.68), channel_id=10, replica_groups=mesh['dp'=8,'tensor'=4] {'dp'}, dimensions={1}, use_global_device_ids=true | all-gather | bytes 589824 | tf_op jit(solution)/shard_map/all_gather | solution.py:209
  563.4 33.5 %all-gather.7 = bf16[1,1024,256]{2,1,0:T(8,128)(2,1)} all-gather(bf16[1,128,256]{2,1,0:T(8,128)(2,1)S(1)} %copy-done.67), channel_id=9, replica_groups=mesh['dp'=8,'tensor'=4] {'dp'}, dimensions={1}, use_global_device_ids=true | all-gather | bytes 589824 | tf_op jit(solution)/shard_map/all_gather | solution.py:208
  596.9 31.2 %all-gather.6 = bf16[1,1024,256]{2,1,0:T(8,128)(2,1)S(1)} all-gather(bf16[1,128,256]{2,1,0:T(8,128)(2,1)S(1)} %copy-done.66), channel_id=8, replica_groups=mesh['dp'=8,'tensor'=4] {'dp'}, dimensions={1}, use_global_device_ids=true | all-gather | bytes 589824 | tf_op jit(solution)/shard_map/all_gather | solution.py:207
  643.2 70.7 %while.55 = (s32[]{:T(128)}, f32[4,512,4,64]{1,3,2,0:T(8,128)}, f32[4,4,512]{2,1,0:T(4,128)S(1)}, s32[4]{0:T(128)S(1)}, s32[2048]{0:T(1024)S(1)}, /*index=5*/bf1...) while((s32[]{:T(128)}, f32[4,512,4,64]{1,3,2,0:T(8,128)}, ...), condition=%wide.region_21.22_spmd, body=%wide.region_18.21_spmd.sunk | while | flops 1128268288 | bytes 57497784 | solution.py:107
  731.6 69.2 %reduce-scatter.17.cloned.1.call-done = f32[512,1024]{1,0:T(8,128)} async-done(((f32[2048,1024]{1,0:T(8,128)}), f32[512,1024]{1,0:T(8,128)}) %reduce-scatter.17.cloned.1.call-update) | async-done | bytes 2097168 | tf_op jit(solution)/shard_map/reduce_scatter | solution.py:172
  811.8 31.8 %all-gather.31.cloned.1.call-done = bf16[2048,1024]{1,0:T(8,128)(2,1)} async-done(((bf16[512,1024]{1,0:T(8,128)(2,1)}), bf16[2048,1024]{1,0:T(8,128)(2,1)}) %all-gather.31.cloned.1.call-update) | async-done | bytes 4194320 | tf_op jit(solution)/shard_map/all_gather | solution.py:164
  866.9 30.0 %all-gather.47.cloned.1.call-done = bf16[1,1024,1024]{2,1,0:T(8,128)(2,1)} async-done(((bf16[1,1024,128]{2,1,0:T(8,128)(2,1)}), bf16[1,1024,1024]{2,1,0:T(8,128)(2,1)}) %all-gather.47.cloned.1.call-update) | async-done | bytes 2097168 | tf_op jit(solution)/shard_map/all_gather | solution.py:245
  896.9 34.6 %all-gather.33.cloned.1.call-done = bf16[2048,1024]{1,0:T(8,128)(2,1)} async-done(((bf16[512,1024]{1,0:T(8,128)(2,1)}), bf16[2048,1024]{1,0:T(8,128)(2,1)}) %all-gather.33.cloned.1.call-update) | async-done | bytes 4194320 | tf_op jit(solution)/shard_map/all_gather | solution.py:168
  990.6 59.7 %reduce-scatter.21.cloned.1.call-done = f32[512,1024]{1,0:T(8,128)} async-done(((f32[2048,1024]{1,0:T(8,128)}), f32[512,1024]{1,0:T(8,128)}) %reduce-scatter.21.cloned.1.call-update) | async-done | bytes 2097168 | tf_op jit(solution)/shard_map/reduce_scatter | solution.py:176
  1053.9 70.6 %reduce-scatter.19.cloned.1.call-done = f32[512,1024]{1,0:T(8,128)} async-done(((f32[2048,1024]{1,0:T(8,128)}), f32[512,1024]{1,0:T(8,128)}) %reduce-scatter.19.cloned.1.call-update) | async-done | bytes 2097168 | tf_op jit(solution)/shard_map/reduce_scatter | solution.py:172
  1135.5 32.3 %all-gather.35.cloned.1.call-done = bf16[2048,1024]{1,0:T(8,128)(2,1)} async-done(((bf16[512,1024]{1,0:T(8,128)(2,1)}), bf16[2048,1024]{1,0:T(8,128)(2,1)}) %all-gather.35.cloned.1.call-update) | async-done | bytes 4194320 | tf_op jit(solution)/shard_map/all_gather | solution.py:168
  1178.6 199.7 %while.56 = (s32[]{:T(128)}, f32[2048,4,64]{0,2,1:T(8,128)}, f32[2048,4,64]{0,2,1:T(8,128)}, bf16[4,512,4,64]{1,3,2,0:T(8,128)(2,1)}, bf16[4,512,4,64]{1,3,2,0:T...) while((s32[]{:T(128)}, f32[2048,4,64]{0,2,1:T(8,128)}, ...), condition=%wide.region_43.44_spmd.clone, body=%wide.region_41.43_spmd.clone.sunk | while | flops 2754216448 | bytes 181254496 | solution.py:150
  1390.8 71.7 %reduce-scatter.23.cloned.1.call-done = f32[512,1024]{1,0:T(8,128)} async-done(((f32[2048,1024]{1,0:T(8,128)}), f32[512,1024]{1,0:T(8,128)}) %reduce-scatter.23.cloned.1.call-update) | async-done | bytes 2097168 | tf_op jit(solution)/shard_map/reduce_scatter | solution.py:176
  1468.2 34.4 %all-gather.37.cloned.1.call-done = bf16[2048,1024]{1,0:T(8,128)(2,1)} async-done(((bf16[512,1024]{1,0:T(8,128)(2,1)}), bf16[2048,1024]{1,0:T(8,128)(2,1)}) %all-gather.37.cloned.1.call-update) | async-done | bytes 4194320 | tf_op jit(solution)/shard_map/all_gather | solution.py:168
  1548.9 72.8 %reduce-scatter.25.cloned.1.call-done = f32[512,1024]{1,0:T(8,128)} async-done(((f32[2048,1024]{1,0:T(8,128)}), f32[512,1024]{1,0:T(8,128)}) %reduce-scatter.25.cloned.1.call-update) | async-done | bytes 2097168 | tf_op jit(solution)/shard_map/reduce_scatter | solution.py:176
  1687.4 203.2 %while.57 = (s32[]{:T(128)}, f32[2048,4,64]{0,2,1:T(8,128)}, f32[2048,4,64]{0,2,1:T(8,128)}, bf16[4,512,4,64]{1,3,2,0:T(8,128)(2,1)}, bf16[4,512,4,64]{1,3,2,0:T...) while((s32[]{:T(128)}, f32[2048,4,64]{0,2,1:T(8,128)}, ...), condition=%wide.region_58.59_spmd.clone, body=%wide.region_56.58_spmd.clone.sunk | while | flops 2754216448 | bytes 180992304 | solution.py:150
  1922.5 14.7 all-to-all-done.3
  1947.7 50.6 %all-to-all-done.1 = bf16[8,128,768]{1,2,0:T(8,128)(2,1)} async-done(((bf16[8,128,768]{1,2,0:T(8,128)(2,1)}), bf16[8,128,768]{1,2,0:T(8,128)(2,1)}, u32[]{:S(2)}, u32[]{:S(2)}) %all-to-all-start.1) | async-done | bytes 1572896 | tf_op jit(solution)/shard_map/all_to_all | solution.py:25
  2009.9 15.2 all-to-all-done.2
  2035.1 49.0 %reduce-scatter.29.cloned.1.call-done = f32[128,1024]{1,0:T(8,128)} async-done(((f32[1024,1024]{1,0:T(8,128)}), f32[128,1024]{1,0:T(8,128)}) %reduce-scatter.29.cloned.1.call-update) | async-done | bytes 524304 | tf_op jit(solution)/shard_map/reduce_scatter | solution.py:354
  2093.1 63.5 %reduce-scatter.27.cloned.1.call-done = f32[512,1024]{1,0:T(8,128)} async-done(((f32[2048,1024]{1,0:T(8,128)}), f32[512,1024]{1,0:T(8,128)}) %reduce-scatter.27.cloned.1.call-update) | async-done | bytes 2097168 | tf_op jit(solution)/shard_map/reduce_scatter | solution.py:176
  2159.1 40.5 %all-reduce.1 = (f32[2,1024]{1,0:T(2,128)}, f32[2,16]{1,0:T(2,128)}, f32[2,1024]{1,0:T(2,128)}, f32[2,1024]{1,0:T(2,128)}, f32[2,4096]{1,0:T(2,128)}) all-reduce(f32[2,1024]{1,0:T(2,128)S(1)} %pad_maximum_fusion.7, f32[2,16]{1,0:T(2,128)S(1)} %pad_maximum_fusion.10, ...), channel_id=1, replica_groups=mesh['dp'=8,'tensor'=4] {'dp','tensor'}, use_global_device_ids=true, to_apply=%region_64.65 | all-reduce | flops 14368 | bytes 114944 | tf_op jit(solution)/shard_map/psum | solution.py:422
  (748 shorter events, 965.5 us)
Async XLA Ops:
  8.1 139.5 %all-gather.25.cloned.1.call-start = ((), (), s32[]{:S(2)}) async-start(), calls=%async_computation.16 | async-start | bytes 5242880 | tf_op jit(solution)/shard_map/all_gather | solution.py:164
  14.6 304.8 %reduce-scatter.13.cloned.1.call-start = ((), (), s32[]{:S(2)}) async-start(), calls=%async_computation.17 | async-start | bytes 10485760 | tf_op jit(solution)/shard_map/reduce_scatter | solution.py:172
  248.5 81.3 %all-gather.41.cloned.1.call-start = ((), (), s32[]{:S(2)}) async-start(), calls=%async_computation.36 | async-start | bytes 2359296 | tf_op jit(solution)/shard_map/all_gather | solution.py:244
  250.8 111.7 %all-gather.27.cloned.1.call-start = ((), (), s32[]{:S(2)}) async-start(), calls=%async_computation.18 | async-start | bytes 5242880 | tf_op jit(solution)/shard_map/all_gather | solution.py:164
  328.1 87.6 %all-gather.43.cloned.1.call-start = ((), (), s32[]{:S(2)}) async-start(), calls=%async_computation.37 | async-start | bytes 2359296 | tf_op jit(solution)/shard_map/all_gather | solution.py:245
  329.1 168.3 %reduce-scatter.15.cloned.1.call-start = ((), (), s32[]{:S(2)}) async-start(), calls=%async_computation.19 | async-start | bytes 10485760 | tf_op jit(solution)/shard_map/reduce_scatter | solution.py:172
  427.5 200.6 %all-gather.29.cloned.1.call-start = ((), (), s32[]{:S(2)}) async-start(), calls=%async_computation.20 | async-start | bytes 5242880 | tf_op jit(solution)/shard_map/all_gather | solution.py:164
  499.4 128.7 %copy-start.85 = (f32[512]{0:T(512)}, f32[512]{0:T(512)S(1)}, u32[]{:S(2)}) copy-start(f32[512]{0:T(512)S(1)} %broadcast_multiply_fusion.20) | copy-start | bytes 6148
  499.7 131.9 %copy-start.93 = (f32[512]{0:T(512)}, f32[512]{0:T(512)S(1)}, u32[]{:S(2)}) copy-start(f32[512]{0:T(512)S(1)} %add_rsqrt_fusion.4) | copy-start | bytes 6148
  502.0 298.8 %reduce-scatter.17.cloned.1.call-start = ((), (), s32[]{:S(2)}) async-start(), calls=%async_computation.21 | async-start | bytes 10485760 | tf_op jit(solution)/shard_map/reduce_scatter | solution.py:172
  730.8 81.0 %all-gather.45.cloned.1.call-start = ((), (), s32[]{:S(2)}) async-start(), calls=%async_computation.38 | async-start | bytes 2359296 | tf_op jit(solution)/shard_map/all_gather | solution.py:244
  731.5 112.1 %all-gather.31.cloned.1.call-start = ((), (), s32[]{:S(2)}) async-start(), calls=%async_computation.22 | async-start | bytes 5242880 | tf_op jit(solution)/shard_map/all_gather | solution.py:164
  809.3 87.6 %all-gather.47.cloned.1.call-start = ((), (), s32[]{:S(2)}) async-start(), calls=%async_computation.39 | async-start | bytes 2359296 | tf_op jit(solution)/shard_map/all_gather | solution.py:245
  809.9 121.7 %all-gather.33.cloned.1.call-start = ((), (), s32[]{:S(2)}) async-start(), calls=%async_computation.24 | async-start | bytes 5242880 | tf_op jit(solution)/shard_map/all_gather | solution.py:168
  811.1 239.2 %reduce-scatter.21.cloned.1.call-start = ((), (), s32[]{:S(2)}) async-start(), calls=%async_computation.25 | async-start | bytes 10485760 | tf_op jit(solution)/shard_map/reduce_scatter | solution.py:176
  811.8 165.6 %copy-start.115 = (f32[1,1024]{1,0:T(1,128)}, f32[1,1024]{1,0:T(1,128)S(1)}, u32[]{:S(2)}) copy-start(f32[1,1024]{1,0:T(1,128)S(1)} %constant_dynamic-slice_fusion) | copy-start | bytes 12292
  977.4 147.1 %reduce-scatter.19.cloned.1.call-start = ((), (), s32[]{:S(2)}) async-start(), calls=%async_computation.23 | async-start | bytes 10485760 | tf_op jit(solution)/shard_map/reduce_scatter | solution.py:172
  990.5 134.0 %copy-start.18 = (f32[512,1024]{1,0:T(8,128)S(1)}, f32[512,1024]{1,0:T(8,128)}, u32[]{:S(2)}) copy-start(f32[512,1024]{1,0:T(8,128)} %reduce-scatter.17.cloned.1.call-done) | copy-start | bytes 6291460
  990.5 177.2 %all-gather.35.cloned.1.call-start = ((), (), s32[]{:S(2)}) async-start(), calls=%async_computation.26 | async-start | bytes 5242880 | tf_op jit(solution)/shard_map/all_gather | solution.py:168
  1133.3 329.1 %reduce-scatter.23.cloned.1.call-start = ((), (), s32[]{:S(2)}) async-start(), calls=%async_computation.27 | async-start | bytes 10485760 | tf_op jit(solution)/shard_map/reduce_scatter | solution.py:176
  1390.7 111.8 %all-gather.37.cloned.1.call-start = ((), (), s32[]{:S(2)}) async-start(), calls=%async_computation.28 | async-start | bytes 5242880 | tf_op jit(solution)/shard_map/all_gather | solution.py:168
  1468.1 153.6 %reduce-scatter.25.cloned.1.call-start = ((), (), s32[]{:S(2)}) async-start(), calls=%async_computation.29 | async-start | bytes 10485760 | tf_op jit(solution)/shard_map/reduce_scatter | solution.py:176
  1548.8 125.9 %all-gather.39.cloned.1.call-start = ((), (), s32[]{:S(2)}) async-start(), calls=%async_computation.30 | async-start | bytes 5242880 | tf_op jit(solution)/shard_map/all_gather | solution.py:168
  1631.8 401.0 %reduce-scatter.35.cloned.1.call-start = ((), (), s32[]{:S(2)}) async-start(), calls=%async_computation.35 | async-start | bytes 4718592 | tf_op jit(solution)/shard_map/reduce_scatter | solution.py:355
  1642.9 390.0 %reduce-scatter.33.cloned.1.call-start = ((), (), s32[]{:S(2)}) async-start(), calls=%async_computation.34 | async-start | bytes 4718592 | tf_op jit(solution)/shard_map/reduce_scatter | solution.py:355
  1654.4 380.7 %reduce-scatter.31.cloned.1.call-start = ((), (), s32[]{:S(2)}) async-start(), calls=%async_computation.33 | async-start | bytes 4718592 | tf_op jit(solution)/shard_map/reduce_scatter | solution.py:354
  1664.5 419.6 %reduce-scatter.29.cloned.1.call-start = ((), (), s32[]{:S(2)}) async-start(), calls=%async_computation.32 | async-start | bytes 4718592 | tf_op jit(solution)/shard_map/reduce_scatter | solution.py:354
  1674.7 482.0 %reduce-scatter.27.cloned.1.call-start = ((), (), s32[]{:S(2)}) async-start(), calls=%async_computation.31 | async-start | bytes 10485760 | tf_op jit(solution)/shard_map/reduce_scatter | solution.py:176
  1908.8 28.4 %all-to-all-start.3 = ((bf16[8,256,128]{2,1,0:T(8,128)(2,1)}), bf16[8,256,128]{2,1,0:T(8,128)(2,1)}, u32[]{:S(2)}, u32[]{:S(2)}) async-start(bf16[8,256,128]{2,1,0:T(8,128)(2,1)} %bitcast.294), calls=%async_computation.11 | async-start | bytes 1048576 | tf_op jit(solution)/shard_map/all_to_all | solution.py:25
  1937.2 61.1 %all-to-all-start.1 = ((bf16[8,128,768]{1,2,0:T(8,128)(2,1)}), bf16[8,128,768]{1,2,0:T(8,128)(2,1)}, u32[]{:S(2)}, u32[]{:S(2)}) async-start(bf16[8,128,768]{1,2,0:T(8,128)(2,1)} %copy_bitcast_fusion), calls=%async_computation.9 | async-start | bytes 3145728 | tf_op jit(solution)/shard_map/all_to_all | solution.py:25
  1998.3 26.8 %all-to-all-start.2 = ((bf16[8,256,128]{2,1,0:T(8,128)(2,1)}), bf16[8,256,128]{2,1,0:T(8,128)(2,1)S(1)}, u32[]{:S(2)}, u32[]{:S(2)}) async-start(bf16[8,256,128]{2,1,0:T(8,128)(2,1)} %bitcast.296), calls=%async_computation.10 | async-start | bytes 1048576 | tf_op jit(solution)/shard_map/all_to_all | solution.py:25
  2025.1 63.7 %all-to-all-start = ((bf16[8,128,768]{1,2,0:T(8,128)(2,1)}), bf16[8,128,768]{1,2,0:T(8,128)(2,1)}, u32[]{:S(2)}, u32[]{:S(2)}) async-start(bf16[8,128,768]{1,2,0:T(8,128)(2,1)} %copy_bitcast_fusion.1), calls=%async_computation.8 | async-start | bytes 3145728 | tf_op jit(solution)/shard_map/all_to_all | solution.py:25
  (160 other events, 3425.3 us)
Sparse Core Ops, SparseCore 0:
  14.7 37.1 all-gather.24
  248.6 70.7 reduce-scatter.12
  502.1 34.4 all-gather.28
  730.9 69.8 reduce-scatter.16
  977.5 72.7 reduce-scatter.20
  1052.7 71.7 reduce-scatter.18
  1548.9 72.7 reduce-scatter.24
Sparse Core Ops, SparseCore 1:
  251.9 48.3 all-gather.40
  328.2 34.2 all-gather.26
  365.2 50.5 all-gather.42
  427.5 69.8 reduce-scatter.14
  734.5 47.4 all-gather.44
  809.4 34.2 all-gather.30
  846.3 50.5 all-gather.46
  899.0 32.5 all-gather.32
  1133.4 34.3 all-gather.34
  1390.8 71.6 reduce-scatter.22
  1468.2 34.3 all-gather.36
  1631.9 34.3 all-gather.38
  1670.2 88.2 reduce-scatter.34
  1762.1 87.9 reduce-scatter.32
  1854.1 94.7 reduce-scatter.30
  1952.6 131.5 reduce-scatter.28
  2086.9 69.7 reduce-scatter.26
where the time goes:
time: 2220 us; the launch traced here: 2210 us
  waiting for transfers between devices  902 us (41%)
  matrix products  549 us (25%)
  blocking collectives  338 us (15%)
  other arithmetic  257 us (12%)
  local copies, waits for them, and re-layouts  94.1 us (4%)
  loops' own time  32.7 us (1%)
    reduce_scatter x4, waiting for transfers between devices, sum_rows(): return lax.psum_scatter(values, 'tensor', scatter_dimension=0, tiled=True)  277 us
    reduce_scatter x4, waiting for transfers between devices, sum_grads(): return lax.psum_scatter(values, 'tensor', scatter_dimension=0, tiled=True)  268 us
    all_gather x4, waiting for transfers between devices, gather_grads(): return lax.all_gather(values, 'tensor', axis=0, tiled=True)  101 us
    dot_general x8, matrix products, one_block(): jnp.einsum('qhd,khd->hqk', grad_block, values, preferred_element_type=jnp...  93 us
    convert_element_type x8, other arithmetic, one_block(): grad_scores = (softmax_rows * (grad_probs - inner)).astype(jnp.bfloat16)  88.3 us
    all_to_all x4, waiting for transfers between devices, sum_at_owner(): lax.all_to_all(parts, axis, split_axis=0, concat_axis=0, tiled=True)  80.6 us
    dot_general x12, matrix products, times_transpose(): lax.dot_general(left, right, (((1,), (1,)), ((), ())), preferred_element_...  67 us
    all_gather x2, blocking collectives, local(): lax.all_gather(w_key[layer_index].astype(jnp.bfloat16), 'dp', axis=0, til...  66.9 us
  transfers between devices with their start and end apart: 28, of which 19 were waited for; matrix products, arithmetic and copies ran while one was open for 17% of the time, Pallas kernels for 0%

commit v1 on v0

v1 whole, which is shorter than its diff:
```python
import functools

import jax
import jax.numpy as jnp
from jax import lax
from jax.experimental import pallas as pl
from jax.experimental.pallas import tpu as pltpu
from jax.sharding import PartitionSpec as P

H = 16
HD = 64
LAYERS = 2
PROMPT = 1024
BLOCK = 512

NORM_EPSILON = 1e-05
MASKED_SCORE = -1e30
F32 = jnp.float32
BF16 = jnp.bfloat16
VMEM_LIMIT = 67_000_000


def tanh_gelu(inputs):
    return (
        0.5
        * inputs
        * (1.0 + jnp.tanh(0.7978845608028654 * (inputs + 0.044715 * inputs * inputs * inputs)))
    )


def normalize(values):
    center = values - jnp.mean(values, -1, keepdims=True)
    factor = lax.rsqrt(jnp.mean(center * center, -1, keepdims=True) + NORM_EPSILON)
    return (center * factor, factor)


def norm_back(grad_norm, normed, factor):
    return factor * (
        grad_norm
        - jnp.mean(grad_norm, -1, keepdims=True)
        - normed * jnp.mean(grad_norm * normed, -1, keepdims=True)
    )


def dot_nn(left, right):
    return lax.dot_general(left, right, (((1,), (0,)), ((), ())), preferred_element_type=F32)


def dot_tn(left, right):
    return lax.dot_general(left, right, (((0,), (0,)), ((), ())), preferred_element_type=F32)


def dot_nt(left, right):
    return lax.dot_general(left, right, (((1,), (1,)), ((), ())), preferred_element_type=F32)


def bit_masks(size):
    masks = []
    while size > 1:
        size //= 2
        masks.append(size)
    return masks


def relative_order(masks):
    order = [0]
    for mask in masks:
        order = order + [mask | other for other in order]
    return order


def swap(array, axis, mask):
    size = lax.axis_size(axis)
    return lax.ppermute(array, axis, [(i, i ^ mask) for i in range(size)])


class Places:
    def __init__(self):
        self.dp_size = lax.axis_size("dp")
        self.tensor_size = lax.axis_size("tensor")
        dp_index = lax.axis_index("dp").astype(jnp.int32)
        self.tensor_index = lax.axis_index("tensor").astype(jnp.int32)
        self.tensor_masks = bit_masks(self.tensor_size)
        masks = bit_masks(self.dp_size)
        self.far_masks = relative_order(masks[:-1])
        self.near_mask = masks[-1]
        dp_order = self.far_masks + [mask | self.near_mask for mask in self.far_masks]
        self.tensor_order = relative_order(self.tensor_masks)
        tensor_inverse = [self.tensor_order.index(i) for i in range(self.tensor_size)]
        self.dp_places = jnp.array(dp_order, jnp.int32) ^ dp_index
        self.tensor_places = jnp.array(self.tensor_order, jnp.int32) ^ self.tensor_index
        spots = jnp.arange(self.tensor_size, dtype=jnp.int32) ^ self.tensor_index
        self.tensor_sources = jnp.array(tensor_inverse, jnp.int32)[spots]


def gather_far(shard, places):
    others = [swap(shard, "dp", mask) for mask in places.far_masks[1:]]
    return jnp.stack([shard] + others)


def gather_near(part, places):
    return [part, swap(part, "dp", places.near_mask)]


def gather_tensor(parts, masks):
    for mask in masks:
        parts = parts + [jax.tree.map(lambda x, m=mask: swap(x, "tensor", m), p) for p in parts]
    return parts


def gather_late_tensor(shard, places):
    pieces = gather_near(gather_far(shard, places), places)
    return gather_tensor([pieces], places.tensor_masks)


def gather_late_near(shard, places):
    parts = gather_tensor([gather_far(shard, places)], places.tensor_masks[:-1])
    pieces = [gather_near(part, places) for part in parts]
    return gather_tensor(pieces, places.tensor_masks[-1:])


def add_low(kept, arrived):
    return (kept.astype(F32) + arrived.astype(F32)).astype(BF16)


def add_halves(kept, arrived):
    return add_low(kept[0], arrived[0]), add_low(kept[1], arrived[1])


def sum_far(kept, arrived, places):
    blocks = [add_low(kept[i], arrived[i]) for i in range(kept.shape[0])]
    return sum_blocks(blocks, places)


def sum_blocks(blocks, places):
    total = blocks[0].astype(F32)
    for block, mask in zip(blocks[1:], places.far_masks[1:]):
        total = total + swap(block, "dp", mask).astype(F32)
    return total


def scatter_pair(kept, sent, hops, places):
    arrived = swap(sent, *hops[0])
    for hop in hops[1:]:
        kept, sent = add_halves(kept, arrived)
        arrived = swap(sent, *hop)
    return sum_far(kept, arrived, places)


def sum_everywhere(vector):
    for axis in ("tensor", "dp"):
        for mask in reversed(bit_masks(lax.axis_size(axis))):
            vector = vector + swap(vector, axis, mask)
    return vector


def block_rows(place_ref, at, rows):
    return pl.ds(pl.multiple_of(place_ref[at] * rows, rows), rows)


def start_rows(spot, blocks, columns, target, semaphore):
    count, _, rows, _ = blocks.shape
    for at in range(count):
        pltpu.make_async_copy(
            blocks.at[at, spot, :, columns], target.at[at * rows : (at + 1) * rows, :], semaphore
        ).start()


def wait_whole(target, semaphore):
    pltpu.make_async_copy(target, target, semaphore).wait()


def each_rows(total, chunk, body):
    def step(at, carry):
        body(pl.ds(pl.multiple_of(at * chunk, chunk), chunk))
        return carry

    lax.fori_loop(0, total // chunk, step, 0)


def fold_lanes(values):
    total = values[:, :128]
    for lane in range(128, values.shape[1], 128):
        total = total + values[:, lane : lane + 128]
    return total


def fold_rows(values):
    return jnp.sum(values.reshape(values.shape[0] // 8, 8, values.shape[1]), axis=0)


CHUNK = 16


def ffn_forward_kernel(parts, last, place_ref, *refs):
    refs = list(refs)

    def take(count):
        taken = refs[:count]
        del refs[:count]
        return taken

    (stream_ref,) = take(1)
    a_refs = take(parts)
    (matrix_ref,) = take(1)
    post_ref, ffn_ref, mid_ref, next_ref = take(4)
    out_ref, middle_ref, next_stream_ref, h_ffn_ref, mean_ref, factor_ref = take(6)
    pre_ref, h_mid_ref = take(2)
    h_next_ref = None if last else take(1)[0]
    w_up, w_out, w_down, active, pre_buf, mid_buf, sums, squares = take(8)
    up_sem, out_sem, down_sem, pre_sem, mid_sem = take(5)
    rows, depth = stream_ref.shape
    wide = w_up.shape[2]
    narrow = w_out.shape[2]
    hidden = parts * wide

    up_columns, down_columns = pl.ds(0, wide), pl.ds(wide, wide)
    out_columns = pl.ds(2 * wide, narrow)
    for at in range(parts):
        start_rows(place_ref[at], matrix_ref, out_columns, w_out.at[at], out_sem)
    for at in range(parts):
        start_rows(place_ref[at], matrix_ref, up_columns, w_up.at[at], up_sem.at[at])
    for at in range(parts):
        start_rows(place_ref[at], matrix_ref, down_columns, w_down.at[at], down_sem.at[at])
    wait_whole(w_out, out_sem)
    out_ref[...] = sum(dot_nt(a_refs[at][...], w_out[at]) for at in range(parts))

    def middle_rows(here):
        normed, _ = normalize(out_ref[here, :])
        middle = stream_ref[here, :] + normed * post_ref[...]
        middle_ref[here, :] = middle
        normed, _ = normalize(middle)
        h_ffn_ref[here, :] = (normed * ffn_ref[...]).astype(BF16)

    each_rows(rows, CHUNK, middle_rows)
    sums[...] = jnp.zeros_like(sums)
    squares[...] = jnp.zeros_like(squares)
    for at in range(parts):
        slot = at % 2
        wait_whole(w_up.at[at], up_sem.at[at])
        if at >= 2:
            pltpu.make_async_copy(
                pre_buf.at[slot], pre_ref.at[at - 2], pre_sem.at[slot]
            ).wait()
        pre_buf[slot] = dot_nn(h_ffn_ref[...], w_up[at])
        pltpu.make_async_copy(pre_buf.at[slot], pre_ref.at[at], pre_sem.at[slot]).start()

        def active_rows(here, at=at, slot=slot):
            value = tanh_gelu(pre_buf[slot, here, :])
            active[at, here, :] = value
            sums[here, :] += fold_lanes(value)
            squares[here, :] += fold_lanes(value * value)

        each_rows(rows, CHUNK, active_rows)
    mean = jnp.sum(sums[...], axis=1, keepdims=True) / hidden
    spread = jnp.sum(squares[...], axis=1, keepdims=True) / hidden - mean * mean
    mean_ref[...] = jnp.broadcast_to(mean, mean_ref.shape)
    factor_ref[...] = jnp.broadcast_to(lax.rsqrt(spread + NORM_EPSILON), factor_ref.shape)
    for at in range(parts):
        slot = at % 2
        if at >= 2:
            pltpu.make_async_copy(
                mid_buf.at[slot], h_mid_ref.at[at - 2], mid_sem.at[slot]
            ).wait()

        def mid_rows(here, at=at, slot=slot):
            normed = (active[at, here, :] - mean_ref[here, :1]) * factor_ref[here, :1]
            mid_buf[slot, here, :] = (normed * mid_ref[at : at + 1, :]).astype(BF16)

        each_rows(rows, CHUNK, mid_rows)
        pltpu.make_async_copy(mid_buf.at[slot], h_mid_ref.at[at], mid_sem.at[slot]).start()
        wait_whole(w_down.at[at], down_sem.at[at])
        product = dot_nt(mid_buf[slot], w_down[at])
        if at == 0:
            next_stream_ref[...] = middle_ref[...] + product
        else:
            next_stream_ref[...] += product
    if not last:

        def next_rows(here):
            normed, _ = normalize(next_stream_ref[here, :])
            h_next_ref[here, :] = (normed * next_ref[...]).astype(BF16)

        each_rows(rows, CHUNK, next_rows)
    for at in range(max(parts - 2, 0), parts):
        slot = at % 2
        pltpu.make_async_copy(pre_buf.at[slot], pre_ref.at[at], pre_sem.at[slot]).wait()
        pltpu.make_async_copy(mid_buf.at[slot], h_mid_ref.at[at], mid_sem.at[slot]).wait()


def ffn_forward(places, stream, a_parts, matrices, post, ffn, mid, following, last):
    rows, depth = stream.shape
    parts, wide = mid.shape
    narrow = a_parts[0].shape[1]
    vmem = pl.BlockSpec(memory_space=pltpu.VMEM)
    hbm = pl.BlockSpec(memory_space=pl.ANY)
    full = jax.ShapeDtypeStruct((rows, depth), F32)
    low = jax.ShapeDtypeStruct((rows, depth), BF16)
    stat = jax.ShapeDtypeStruct((rows, 128), F32)
    outs = [full, full, full, low, stat, stat] + [
        jax.ShapeDtypeStruct((parts, rows, wide), F32),
        jax.ShapeDtypeStruct((parts, rows, wide), BF16),
    ]
    out_specs = [vmem] * 6 + [hbm] * 2
    if not last:
        outs, out_specs = outs + [low], out_specs + [vmem]
    dma = pltpu.SemaphoreType.DMA
    return pl.pallas_call(
        functools.partial(ffn_forward_kernel, parts, last),
        in_specs=[pl.BlockSpec(memory_space=pltpu.SMEM)]
        + [vmem] * (1 + parts)
        + [hbm]
        + [vmem] * 4,
        out_specs=out_specs,
        out_shape=outs,
        scratch_shapes=[
            pltpu.VMEM((parts, depth, wide), BF16),
            pltpu.VMEM((parts, depth, narrow), BF16),
            pltpu.VMEM((parts, depth, wide), BF16),
            pltpu.VMEM((parts, rows, wide), F32),
            pltpu.VMEM((2, rows, wide), F32),
            pltpu.VMEM((2, rows, wide), BF16),
            pltpu.VMEM((rows, 128), F32),
            pltpu.VMEM((rows, 128), F32),
            dma((parts,)),
            dma,
            dma((parts,)),
            dma((2,)),
            dma((2,)),
        ],
        compiler_params=pltpu.CompilerParams(vmem_limit_bytes=VMEM_LIMIT),
        cost_estimate=pl.CostEstimate(
            flops=2 * rows * depth * parts * (2 * wide + narrow),
            bytes_accessed=40 << 20,
            transcendentals=rows * parts * wide,
        ),
        name="ffn_forward",
    )(
        places.tensor_places,
        stream,
        *a_parts,
        matrices,
        post[None],
        ffn[None],
        mid,
        following[None],
    )


def ffn_backward_kernel(parts, place_ref, *refs):
    refs = list(refs)

    def take(count):
        taken = refs[:count]
        del refs[:count]
        return taken

    grad_ref, out_ref, middle_ref, mean_ref, factor_ref, pre_ref = take(6)
    (matrix_ref,) = take(1)
    post_ref, ffn_ref, mid_ref, scale_ref = take(4)
    low_ref, grad_middle_ref, grad_out_ref = take(3)
    dout_refs = take(parts)
    grad_pre_ref, mid_sum_ref, ffn_sum_ref, post_sum_ref = take(4)
    weights, w_out, grad_normed, normed_four, slope, pre_buf, product, low_buf = take(8)
    first, second = take(2)
    weight_sem, out_sem, pre_sem, low_sem = take(4)
    rows, depth = grad_ref.shape
    wide = weights.shape[2]
    narrow = w_out.shape[2]
    hidden = parts * wide

    def read_pre(at):
        return pltpu.make_async_copy(pre_ref.at[at], pre_buf.at[at % 2], pre_sem.at[at % 2])

    up_columns, down_columns = pl.ds(0, wide), pl.ds(wide, wide)
    out_columns = pl.ds(2 * wide, narrow)
    for at in range(parts):
        start_rows(place_ref[at], matrix_ref, down_columns, weights.at[at], weight_sem.at[at])
        if at < 2:
            read_pre(at).start()
    for at in range(parts):
        start_rows(place_ref[at], matrix_ref, out_columns, w_out.at[at], out_sem)
    low_ref[...] = grad_ref[...].astype(BF16)
    first[...] = jnp.zeros_like(first)
    second[...] = jnp.zeros_like(second)
    mid_sum_ref[...] = jnp.zeros_like(mid_sum_ref)
    ffn_sum_ref[...] = jnp.zeros_like(ffn_sum_ref)
    post_sum_ref[...] = jnp.zeros_like(post_sum_ref)
    for at in range(parts):
        wait_whole(weights.at[at], weight_sem.at[at])
        product[...] = dot_nn(low_ref[...], weights[at])
        start_rows(place_ref[at], matrix_ref, up_columns, weights.at[at], weight_sem.at[at])
        read_pre(at).wait()

        def hidden_rows(here, at=at):
            value = pre_buf[at % 2, here, :]
            squared = value * value
            bend = jnp.tanh(0.7978845608028654 * (value + 0.044715 * squared * value))
            raised = 0.5 * (1.0 + bend)
            normed = (value * raised - mean_ref[here, :1]) * factor_ref[here, :1]
            steep = 0.7978845608028654 * (1.0 + 0.134145 * squared)
            slope[at, here, :] = raised + 0.5 * value * (1.0 - bend * bend) * steep
            normed_four[at, here, :] = normed
            grad = product[here, :]
            mid_sum_ref[at] += fold_rows(grad * normed)
            grad = grad * mid_ref[at : at + 1, :]
            grad_normed[at, here, :] = grad
            first[here, :] += fold_lanes(grad)
            second[here, :] += fold_lanes(grad * normed)

        each_rows(rows, CHUNK, hidden_rows)
        if at + 2 < parts:
            read_pre(at + 2).start()
    first[...] = jnp.broadcast_to(
        jnp.sum(first[...], axis=1, keepdims=True) / hidden, first.shape
    )
    second[...] = jnp.broadcast_to(
        jnp.sum(second[...], axis=1, keepdims=True) / hidden, second.shape
    )

    def write_low(at):
        return pltpu.make_async_copy(low_buf.at[at % 2], grad_pre_ref.at[at], low_sem.at[at % 2])

    for at in range(parts):
        if at >= 2:
            write_low(at - 2).wait()

        def pre_rows(here, at=at):
            grad = grad_normed[at, here, :] - first[here, :1]
            grad = factor_ref[here, :1] * (grad - normed_four[at, here, :] * second[here, :1])
            low_buf[at % 2, here, :] = (grad * slope[at, here, :]).astype(BF16)

        each_rows(rows, CHUNK, pre_rows)
        write_low(at).start()
        wait_whole(weights.at[at], weight_sem.at[at])
        part = dot_nt(low_buf[at % 2], weights[at])
        if at == 0:
            product[...] = part
        else:
            product[...] += part

    def middle_rows(here):
        grad = product[here, :]
        normed, factor = normalize(middle_ref[here, :])
        ffn_sum_ref[...] += fold_rows(grad * normed)
        grad = grad_ref[here, :] + norm_back(grad * ffn_ref[...], normed, factor)
        grad_middle_ref[here, :] = grad
        normed, factor = normalize(out_ref[here, :])
        post_sum_ref[...] += fold_rows(grad * normed)
        grad_out_ref[here, :] = norm_back(grad * post_ref[...], normed, factor).astype(BF16)

    each_rows(rows, CHUNK, middle_rows)
    wait_whole(w_out, out_sem)
    for at in range(parts):
        grad = dot_nn(grad_out_ref[...], w_out[at])
        dout_refs[at][...] = (grad * scale_ref[at : at + 1, :]).astype(BF16)
    for at in range(max(parts - 2, 0), parts):
        write_low(at).wait()


def ffn_backward(places, grad, out, middle, mean, factor, pre, matrices, post, ffn, mid, scale):
    rows, depth = grad.shape
    parts, wide = mid.shape
    narrow = scale.shape[1]
    vmem = pl.BlockSpec(memory_space=pltpu.VMEM)
    hbm = pl.BlockSpec(memory_space=pl.ANY)
    low = jax.ShapeDtypeStruct((rows, depth), BF16)
    sums = jax.ShapeDtypeStruct((8, depth), F32)
    dma = pltpu.SemaphoreType.DMA
    return pl.pallas_call(
        functools.partial(ffn_backward_kernel, parts),
        in_specs=[pl.BlockSpec(memory_space=pltpu.SMEM)]
        + [vmem] * 5
        + [hbm] * 2
        + [vmem] * 4,
        out_specs=[vmem] * (3 + parts) + [hbm] + [vmem] * 3,
        out_shape=[low, jax.ShapeDtypeStruct((rows, depth), F32), low]
        + [jax.ShapeDtypeStruct((rows, narrow), BF16)] * parts
        + [
            jax.ShapeDtypeStruct((parts, rows, wide), BF16),
            jax.ShapeDtypeStruct((parts, 8, wide), F32),
            sums,
            sums,
        ],
        scratch_shapes=[
            pltpu.VMEM((parts, depth, wide), BF16),
            pltpu.VMEM((parts, depth, narrow), BF16),
            pltpu.VMEM((parts, rows, wide), F32),
            pltpu.VMEM((parts, rows, wide), F32),
            pltpu.VMEM((parts, rows, wide), F32),
            pltpu.VMEM((2, rows, wide), F32),
            pltpu.VMEM((rows, depth), F32),
            pltpu.VMEM((2, rows, wide), BF16),
            pltpu.VMEM((rows, 128), F32),
            pltpu.VMEM((rows, 128), F32),
            dma((parts,)),
            dma,
            dma((2,)),
            dma((2,)),
        ],
        compiler_params=pltpu.CompilerParams(vmem_limit_bytes=VMEM_LIMIT),
        cost_estimate=pl.CostEstimate(
            flops=2 * rows * depth * parts * (2 * wide + narrow),
            bytes_accessed=44 << 20,
            transcendentals=rows * parts * wide,
        ),
        name="ffn_backward",
    )(
        places.tensor_places,
        grad,
        out,
        middle,
        mean,
        factor,
        pre,
        matrices,
        post[None],
        ffn[None],
        mid,
        scale,
    )


def turned(place_ref, source, plain, target, rows):
    plain[...] = source[...].astype(F32).T.astype(BF16)
    for at in range(target.shape[0] // rows):
        target[at * rows : (at + 1) * rows, :] = plain[block_rows(place_ref, at, rows), :]


def matrix_grads_kernel(parts, place_ref, *refs):
    low_ref, h_ffn_ref, grad_out_ref = refs[:3]
    grad_pre_ref, h_mid_ref, a_ref = refs[3:6]
    up_keep, up_send, down_keep, down_send = refs[6:10]
    low_turned, h_turned, out_turned, low_plain, h_plain, out_plain = refs[10:]
    step = pl.program_id(0)
    depth = low_turned.shape[0]
    count, rows = up_keep.shape[2:4]
    wide = h_mid_ref.shape[2]

    @pl.when(step == 0)
    def _():
        turned(place_ref, low_ref, low_plain, low_turned, rows)
        turned(place_ref, h_ffn_ref, h_plain, h_turned, rows)
        turned(place_ref, grad_out_ref, out_plain, out_turned, rows)

    def fill(up_ref, down_ref):
        shape = (2, count, rows, -1)
        grad = dot_nn(h_turned[...], grad_pre_ref[0]).astype(BF16)
        up_ref[0, :, :, :, :wide] = grad.reshape(shape)
        grad = dot_nn(out_turned[...], a_ref[0]).astype(BF16)
        up_ref[0, :, :, :, wide:] = grad.reshape(shape)
        grad = dot_nn(low_turned[...], h_mid_ref[0]).astype(BF16)
        down_ref[:, 0] = grad.reshape(shape)

    @pl.when(step < parts // 2)
    def _():
        fill(up_keep, down_keep)

    @pl.when(step >= parts // 2)
    def _():
        fill(up_send, down_send)


def matrix_grads_of(places, low, h_ffn, grad_out, grad_pre, h_mid, a_parts):
    rows, depth = low.shape
    parts, _, wide = h_mid.shape
    narrow = a_parts[0].shape[1]
    half = parts // 2
    count = places.dp_size // 2
    block = depth // places.dp_size
    a_all = jnp.stack(a_parts)
    whole = pl.BlockSpec((rows, depth), lambda i, place: (0, 0))
    each = pl.BlockSpec((1, rows, wide), lambda i, place: (i, 0, 0))
    up = (half, 2, count, block, wide + narrow)
    down = (2, half, count, block, wide)
    up_block = (1, 2, count, block, wide + narrow)
    down_block = (2, 1, count, block, wide)
    return pl.pallas_call(
        functools.partial(matrix_grads_kernel, parts),
        grid_spec=pltpu.PrefetchScalarGridSpec(
            num_scalar_prefetch=1,
            grid=(parts,),
            in_specs=[whole] * 3
            + [each] * 2
            + [pl.BlockSpec((1, rows, narrow), lambda i, place: (i, 0, 0))],
            out_specs=[
                pl.BlockSpec(up_block, lambda i, p: (jnp.minimum(i, half - 1), 0, 0, 0, 0)),
                pl.BlockSpec(up_block, lambda i, p: (jnp.maximum(i - half, 0), 0, 0, 0, 0)),
                pl.BlockSpec(down_block, lambda i, p: (0, jnp.minimum(i, half - 1), 0, 0, 0)),
                pl.BlockSpec(down_block, lambda i, p: (0, jnp.maximum(i - half, 0), 0, 0, 0)),
            ],
            scratch_shapes=[pltpu.VMEM((depth, rows), BF16)] * 6,
        ),
        out_shape=[
            jax.ShapeDtypeStruct(up, BF16),
            jax.ShapeDtypeStruct(up, BF16),
            jax.ShapeDtypeStruct(down, BF16),
            jax.ShapeDtypeStruct(down, BF16),
        ],
        compiler_params=pltpu.CompilerParams(vmem_limit_bytes=VMEM_LIMIT),
        cost_estimate=pl.CostEstimate(
            flops=2 * rows * depth * parts * (2 * wide + narrow),
            bytes_accessed=30 << 20,
            transcendentals=0,
        ),
        name="matrix_grads",
    )(places.dp_places, low, h_ffn, grad_out, grad_pre, h_mid, a_all)


def whole_grads_kernel(parts, place_ref, *refs):
    del place_ref
    low_ref, h_ffn_ref, grad_out_ref, grad_pre_ref, h_mid_ref, a_ref, matrix_ref = refs[:7]
    low_turned, h_turned, out_turned = refs[7:]
    wide = h_mid_ref.shape[2]
    shape = matrix_ref.shape[:3] + (-1,)

    @pl.when(pl.program_id(0) == 0)
    def _():
        for source, target in (
            (low_ref, low_turned), (h_ffn_ref, h_turned), (grad_out_ref, out_turned)
        ):
            target[...] = source[...].astype(F32).T.astype(BF16)

    grad = dot_nn(h_turned[...], grad_pre_ref[0]).astype(BF16)
    matrix_ref[:, :, :, :wide] = grad.reshape(shape)
    grad = dot_nn(low_turned[...], h_mid_ref[0]).astype(BF16)
    matrix_ref[:, :, :, wide : 2 * wide] = grad.reshape(shape)
    grad = dot_nn(out_turned[...], a_ref[0]).astype(BF16)
    matrix_ref[:, :, :, 2 * wide :] = grad.reshape(shape)


def whole_grads(places, low, h_ffn, grad_out, grad_pre, h_mid, a_parts):
    rows, depth = low.shape
    parts, _, wide = h_mid.shape
    narrow = a_parts[0].shape[1]
    block = depth // places.dp_size
    columns = 2 * wide + narrow
    whole = pl.BlockSpec((rows, depth), lambda i, place: (0, 0))
    each = pl.BlockSpec((1, rows, wide), lambda i, place: (i, 0, 0))
    return pl.pallas_call(
        functools.partial(whole_grads_kernel, parts),
        grid_spec=pltpu.PrefetchScalarGridSpec(
            num_scalar_prefetch=1,
            grid=(parts,),
            in_specs=[whole] * 3
            + [each] * 2
            + [pl.BlockSpec((1, rows, narrow), lambda i, place: (i, 0, 0))],
            out_specs=pl.BlockSpec(
                (places.dp_size, 1, block, columns), lambda i, place: (0, place[i], 0, 0)
            ),
            scratch_shapes=[pltpu.VMEM((depth, rows), BF16)] * 3,
        ),
        out_shape=jax.ShapeDtypeStruct((places.dp_size, parts, block, columns), BF16),
        compiler_params=pltpu.CompilerParams(vmem_limit_bytes=VMEM_LIMIT),
        cost_estimate=pl.CostEstimate(
            flops=2 * rows * depth * parts * columns,
            bytes_accessed=30 << 20,
            transcendentals=0,
        ),
        name="whole_grads",
    )(places.tensor_places, low, h_ffn, grad_out, grad_pre, h_mid, jnp.stack(a_parts))


def attn_grads_kernel(parts, place_ref, *refs):
    h_refs = refs[:parts]
    packed_ref, keep_ref, send_ref, total = refs[parts:]
    count, rows, _ = keep_ref.shape
    tokens = packed_ref.shape[0] // parts
    for part in range(parts):
        flipped = h_refs[part][...].astype(F32).T.astype(BF16)
        grad = dot_nn(flipped, packed_ref[part * tokens : (part + 1) * tokens, :])
        if part == 0:
            total[...] = grad
        else:
            total[...] += grad
    for at in range(count):
        keep_ref[at] = total[block_rows(place_ref, at, rows), :].astype(BF16)
        send_ref[at] = total[block_rows(place_ref, count + at, rows), :].astype(BF16)


def attn_grads(places, h_parts, packed):
    parts = len(h_parts)
    tokens, depth = h_parts[0].shape
    columns = packed.shape[1]
    count = places.dp_size // 2
    block = depth // places.dp_size
    vmem = pl.BlockSpec(memory_space=pltpu.VMEM)
    return pl.pallas_call(
        functools.partial(attn_grads_kernel, parts),
        in_specs=[pl.BlockSpec(memory_space=pltpu.SMEM)] + [vmem] * (parts + 1),
        out_specs=[vmem] * 2,
        out_shape=[jax.ShapeDtypeStruct((count, block, columns), BF16)] * 2,
        scratch_shapes=[
            pltpu.VMEM((depth, columns), F32),
        ],
        compiler_params=pltpu.CompilerParams(vmem_limit_bytes=VMEM_LIMIT),
        cost_estimate=pl.CostEstimate(
            flops=2 * tokens * parts * depth * columns,
            bytes_accessed=8 << 20,
            transcendentals=0,
        ),
        name="attn_grads",
    )(places.dp_places, *h_parts, packed)


def half_mask(shape, head):
    lane = lax.broadcasted_iota(jnp.int32, shape, len(shape) - 1)
    return (lane // HD) == (head % 2)


def place_rows(place_ref, pieces, target):
    for half, piece in enumerate(pieces):
        count, rows, _ = piece.shape
        for at in range(count):
            target[block_rows(place_ref, half * count + at, rows), :] = piece[at]


def forward_kernel(block_ref, place_ref, *refs):
    parts = block_ref.shape[0]
    rows_refs = refs[:parts]
    pieces = refs[parts : parts + 2]
    column_ref, row_ref, scale_ref = refs[parts + 2 : parts + 5]
    query_ref, key_ref, value_ref, mixture_ref, logsum_ref = refs[parts + 5 : parts + 10]
    scaled_refs = refs[parts + 10 : -2]
    score_ref, weight_ref = refs[-2:]
    width = query_ref.shape[1]
    length = query_ref.shape[0]
    rows = length // parts

    place_rows(place_ref, pieces, weight_ref)
    for part in range(parts):
        at = pl.ds(pl.multiple_of(block_ref[part] * rows, rows), rows)
        packed = dot_nn(rows_refs[part][...], weight_ref[...])
        query_ref[at, :] = packed[:, :width].astype(BF16) * jnp.asarray(0.125, BF16)
        key_ref[at, :] = packed[:, width : 2 * width].astype(BF16)
        value_ref[at, :] = packed[:, 2 * width :].astype(BF16)

    for query_block in range(length // BLOCK):
        here = pl.ds(query_block * BLOCK, BLOCK)

        def one_head(head, logsums, query_block=query_block, here=here):
            lanes = pl.ds(pl.multiple_of((head // 2) * 128, 128), 128)
            own = half_mask((BLOCK, 128), head)
            query = jnp.where(own, query_ref[here, lanes], jnp.asarray(0, BF16))
            highest = jnp.full((BLOCK, 128), MASKED_SCORE, F32)
            for key_block in range(query_block + 1):
                there = pl.ds(key_block * BLOCK, BLOCK)
                scores = dot_nt(query, key_ref[there, lanes])
                if key_block == query_block or key_block * BLOCK >= PROMPT:
                    first = lax.broadcasted_iota(jnp.int32, (BLOCK, BLOCK), 0)
                    second = lax.broadcasted_iota(jnp.int32, (BLOCK, BLOCK), 1)
                    seen = None
                    if key_block == query_block:
                        seen = second <= first
                    if key_block * BLOCK >= PROMPT:
                        query_at = pl.ds(query_block * BLOCK - PROMPT, BLOCK)
                        key_at = pl.ds(key_block * BLOCK - PROMPT, BLOCK)
                        same = column_ref[query_at, :] == row_ref[:, key_at]
                        seen = same if seen is None else seen & same
                    scores = jnp.where(seen, scores, MASKED_SCORE)
                score_ref[:, there] = scores
                for lane in range(0, BLOCK, 128):
                    highest = jnp.maximum(highest, scores[:, lane : lane + 128])
            top = jnp.max(highest, axis=1, keepdims=True)
            total = jnp.zeros((BLOCK, 128), F32)
            mixed = jnp.zeros((BLOCK, 128), F32)
            for key_block in range(query_block + 1):
                there = pl.ds(key_block * BLOCK, BLOCK)
                weights = jnp.exp(score_ref[:, there] - top)
                for lane in range(0, BLOCK, 128):
                    total = total + weights[:, lane : lane + 128]
                mixed = mixed + dot_nn(weights.astype(BF16), value_ref[there, lanes])
            denominator = jnp.sum(total, axis=1, keepdims=True)
            mixed = mixed / denominator
            mixture_ref[here, lanes] = jnp.where(own, mixed, mixture_ref[here, lanes])
            lane = lax.broadcasted_iota(jnp.int32, (BLOCK, 128), 1)
            return jnp.where(lane == head, top + jnp.log(denominator), logsums)

        logsums = lax.fori_loop(0, width // HD, one_head, jnp.zeros((BLOCK, 128), F32))
        logsum_ref[:, here] = logsums.T[: logsum_ref.shape[0], :]

    for part in range(parts):
        at = pl.ds(pl.multiple_of(block_ref[part] * rows, rows), rows)
        scaled_refs[part][...] = (mixture_ref[at, :] * scale_ref[...]).astype(BF16)


def attend_forward(places, rows, pieces, seg_column, seg_row, scale):
    parts = len(rows)
    length = parts * rows[0].shape[0]
    width = pieces[0].shape[2] // 3
    depth = rows[0].shape[1]
    heads = width // HD
    pairs = length * length * 5 // 8
    whole = pl.BlockSpec(memory_space=pltpu.VMEM)
    return pl.pallas_call(
        forward_kernel,
        in_specs=[pl.BlockSpec(memory_space=pltpu.SMEM)] * 2 + [whole] * (parts + 5),
        out_specs=[whole] * (5 + parts),
        out_shape=[jax.ShapeDtypeStruct((length, width), BF16)] * 3
        + [
            jax.ShapeDtypeStruct((length, width), F32),
            jax.ShapeDtypeStruct((8, length), F32),
        ]
        + [jax.ShapeDtypeStruct((length // parts, width), BF16)] * parts,
        scratch_shapes=[
            pltpu.VMEM((BLOCK, length), F32),
            pltpu.VMEM((depth, 3 * width), BF16),
        ],
        compiler_params=pltpu.CompilerParams(vmem_limit_bytes=VMEM_LIMIT),
        cost_estimate=pl.CostEstimate(
            flops=2 * length * depth * 3 * width + heads * pairs * 4 * 256,
            bytes_accessed=20 << 20,
            transcendentals=heads * pairs,
        ),
        name="attend_forward",
    )(places.tensor_places, places.dp_places, *rows, *pieces, seg_column, seg_row, scale)


def backward_kernel(block_ref, place_ref, open_ref, edge_ref, *refs):
    parts = block_ref.shape[0]
    grad_refs = refs[:parts]
    query_ref, key_ref, value_ref, mixture_ref, logsum_ref = refs[parts : parts + 5]
    column_ref, row_ref = refs[parts + 5 : parts + 7]
    pieces = refs[parts + 7 : parts + 9]
    packed_ref, inner_sum_ref, keep_ref, send_ref = refs[parts + 9 : parts + 13]
    dout_ref, inner_ref, dq_ref, dk_ref, dv_ref, weight_ref = refs[parts + 13 :]
    length, width = query_ref.shape
    rows = length // parts

    for part in range(parts):
        at = pl.ds(pl.multiple_of(block_ref[part] * rows, rows), rows)
        dout_ref[at, :] = grad_refs[part][...]
    picks = lax.broadcasted_iota(jnp.int32, (8, width), 1) // HD == lax.broadcasted_iota(
        jnp.int32, (8, width), 0
    )
    picks = jnp.where(picks, 1.0, 0.0)
    inner_sum = jnp.zeros((8, 128), F32)
    for part in range(length // BLOCK):
        at = pl.ds(part * BLOCK, BLOCK)
        product = dout_ref[at, :].astype(F32) * mixture_ref[at, :]
        inner = lax.dot_general(
            picks,
            product,
            (((1,), (1,)), ((), ())),
            precision=lax.Precision.HIGHEST,
            preferred_element_type=F32,
        )
        inner_ref[:, at] = inner
        for lane in range(0, BLOCK, 128):
            inner_sum = inner_sum + inner[:, lane : lane + 128]
    inner_sum_ref[...] = inner_sum
    dq_ref[...] = jnp.zeros_like(dq_ref)
    dk_ref[...] = jnp.zeros_like(dk_ref)
    dv_ref[...] = jnp.zeros_like(dv_ref)

    def one_pair(head, key_block, query_block, edge):
        lanes = pl.ds(pl.multiple_of((head // 2) * 128, 128), 128)
        there = pl.ds(pl.multiple_of(key_block * BLOCK, BLOCK), BLOCK)
        here = pl.ds(pl.multiple_of(query_block * BLOCK, BLOCK), BLOCK)
        own = half_mask((BLOCK, 128), head)
        none = jnp.asarray(0, BF16)
        query = jnp.where(own, query_ref[here, lanes], none)
        dout = jnp.where(own, dout_ref[here, lanes], none)
        key = key_ref[there, lanes]
        scores = dot_nt(key, query)
        weights = jnp.exp(scores - logsum_ref[pl.ds(head, 1), here])
        if edge:
            key_at = key_block * BLOCK + lax.broadcasted_iota(jnp.int32, (BLOCK, BLOCK), 0)
            query_at = query_block * BLOCK + lax.broadcasted_iota(jnp.int32, (BLOCK, BLOCK), 1)
            same = column_ref[there, :] == row_ref[:, here]
            weights = jnp.where((key_at <= query_at) & same, weights, 0.0)
        dv_ref[there, lanes] += dot_nn(weights.astype(BF16), dout)
        grad = dot_nt(value_ref[there, lanes], dout)
        grad = (weights * (grad - inner_ref[pl.ds(head, 1), here])).astype(BF16)
        dk_ref[there, lanes] += dot_nn(grad, query)
        dq_ref[here, lanes] += dot_tn(grad, jnp.where(own, key, none))

    def one_head(head, carry):
        def open_pair(at, inside):
            one_pair(head, open_ref[2 * at], open_ref[2 * at + 1], False)
            return inside

        def edge_pair(at, inside):
            one_pair(head, edge_ref[2 * at], edge_ref[2 * at + 1], True)
            return inside

        lax.fori_loop(0, open_ref.shape[0] // 2, open_pair, 0)
        lax.fori_loop(0, edge_ref.shape[0] // 2, edge_pair, 0)
        return carry

    lax.fori_loop(0, width // HD, one_head, 0)
    for part in range(parts):
        at = pl.ds(pl.multiple_of(block_ref[part] * rows, rows), rows)
        to = pl.ds(part * rows, rows)
        packed_ref[to, :width] = (dq_ref[at, :] * 0.125).astype(BF16)
        packed_ref[to, width : 2 * width] = dk_ref[at, :].astype(BF16)
        packed_ref[to, 2 * width :] = dv_ref[at, :].astype(BF16)
    place_rows(place_ref, pieces, weight_ref)
    for part in range(parts):
        grad = dot_nt(packed_ref[part * rows : (part + 1) * rows, :], weight_ref[...])
        half = parts // 2
        target = keep_ref if part < half else send_ref
        target[part % half] = grad.astype(BF16)


def attend_backward(
    places, grads, queries, keys, values, mixture, logsum, seg_column, seg_row, pieces
):
    parts = len(grads)
    length, width = queries.shape
    heads = width // HD
    depth = pieces[0].shape[0] * pieces[0].shape[1] * 2
    opened, edges = [], []
    for query_block in range(length // BLOCK):
        for key_block in range(query_block + 1):
            if key_block == query_block or key_block * BLOCK >= PROMPT:
                edges += [key_block, query_block]
            else:
                opened += [key_block, query_block]
    whole = pl.BlockSpec(memory_space=pltpu.VMEM)
    scalars = pl.BlockSpec(memory_space=pltpu.SMEM)
    pairs = length * length * 5 // 8
    return pl.pallas_call(
        backward_kernel,
        in_specs=[scalars] * 4 + [whole] * (parts + 9),
        out_specs=[whole] * 4,
        out_shape=[
            jax.ShapeDtypeStruct((length, 3 * width), BF16),
            jax.ShapeDtypeStruct((8, 128), F32),
            jax.ShapeDtypeStruct((parts // 2, length // parts, depth), BF16),
            jax.ShapeDtypeStruct((parts // 2, length // parts, depth), BF16),
        ],
        scratch_shapes=[
            pltpu.VMEM((length, width), BF16),
            pltpu.VMEM((8, length), F32),
            pltpu.VMEM((length, width), F32),
            pltpu.VMEM((length, width), F32),
            pltpu.VMEM((length, width), F32),
            pltpu.VMEM((depth, 3 * width), BF16),
        ],
        compiler_params=pltpu.CompilerParams(vmem_limit_bytes=VMEM_LIMIT),
        cost_estimate=pl.CostEstimate(
            flops=heads * pairs * 10 * 256 + 2 * length * depth * 3 * width,
            bytes_accessed=16 << 20,
            transcendentals=heads * pairs,
        ),
        name="attend_backward",
    )(
        places.tensor_places,
        places.dp_places,
        jnp.array(opened, jnp.int32),
        jnp.array(edges, jnp.int32),
        *grads,
        queries,
        keys,
        values,
        mixture,
        logsum,
        seg_column,
        seg_row,
        *pieces,
    )


def local(
    layer_input,
    segment_ids,
    ln_attn_gain,
    w_query,
    w_key,
    w_value,
    head_scale,
    w_out,
    ln_post_gain,
    ln_ffn_gain,
    w_up,
    ln_mid_gain,
    w_down,
    out_cotangent,
):
    places = Places()
    tensor_size = places.tensor_size
    tensor_order = places.tensor_order
    tensor_masks = places.tensor_masks
    local_heads = H // tensor_size
    width = local_heads * HD
    parts = range(tensor_size)

    seg_row = segment_ids[0][None, :]
    seg_column = segment_ids[0][:, None]
    prompt = jnp.zeros((PROMPT,), jnp.int32)
    long_row = jnp.concatenate([prompt, segment_ids[0]])[None, :]
    long_column = jnp.concatenate([prompt, segment_ids[0]])[:, None]

    attn_shards, matrix_set = [], []
    for layer in range(LAYERS):
        packed = jnp.concatenate([w_query[layer], w_key[layer], w_value[layer]], axis=1)
        attn_shards.append(packed.astype(BF16))
        packed = jnp.concatenate([w_up[layer], w_down[layer].T, w_out[layer].T], axis=1)
        packed = packed.astype(BF16)
        whole = lax.all_gather(packed, ("dp", "tensor"), axis=0, tiled=False)
        matrix_set.append(whole.reshape(places.dp_size, tensor_size, *packed.shape))
    attn_set = [gather_near(gather_far(attn_shards[0], places), places)]

    def exchange(blocks):
        return [
            block if at == 0 else swap(block, "tensor", tensor_order[at])
            for at, block in enumerate(blocks)
        ]

    stream = layer_input
    normed_one, _ = normalize(stream)
    h_attn = (normed_one * ln_attn_gain[0]).astype(BF16)
    saved = []
    for layer in range(LAYERS):
        last = layer == LAYERS - 1
        if layer > 0:
            shard, _ = lax.optimization_barrier((attn_shards[layer], logsum))
            attn_set.append(gather_near(gather_far(shard, places), places))
        h_parts = gather_tensor([h_attn], tensor_masks)
        scale_all = head_scale[layer].reshape(tensor_size, local_heads)
        scale_rel = jnp.repeat(scale_all[places.tensor_places], HD, axis=1)
        queries, keys, values, mixture, logsum, *a_parts = attend_forward(
            places, h_parts, attn_set[layer], seg_column, seg_row, scale_rel[:1]
        )
        a_parts = exchange(a_parts)
        gain_mid = ln_mid_gain[layer].reshape(tensor_size, -1)[places.tensor_places]
        stream_in = stream
        attn_out, middle, stream, h_ffn, mean, factor, pre, h_mid, *h_next = ffn_forward(
            places, stream, a_parts, matrix_set[layer], ln_post_gain[layer], ln_ffn_gain[layer],
            gain_mid, ln_attn_gain[(layer + 1) % LAYERS], last,
        )
        if not last:
            h_attn = h_next[0]
        saved.append(
            (
                stream_in, h_parts, queries, keys, values, mixture, logsum, scale_rel, a_parts,
                attn_out, middle, h_ffn, mean, factor, gain_mid, pre, h_mid,
            )
        )

    grad_stream = out_cotangent
    matrix_grads = [None] * LAYERS
    small_grads = [None] * LAYERS
    core_hop = ("tensor", tensor_masks[-1])
    side_hops = [("tensor", mask) for mask in reversed(tensor_masks[:-1])]
    near_hop = ("dp", places.near_mask)
    for layer in reversed(range(LAYERS)):
        (
            stream_in, h_parts, queries, keys, values, mixture, logsum, scale_rel, a_parts,
            attn_out, middle, h_ffn, mean, factor, gain_mid, pre, h_mid,
        ) = saved[layer]
        grad_low, grad_middle, grad_out, *rest = ffn_backward(
            places, grad_stream, attn_out, middle, mean, factor, pre, matrix_set[layer],
            ln_post_gain[layer], ln_ffn_gain[layer], gain_mid, scale_rel,
        )
        dout_parts = exchange(rest[:tensor_size])
        grad_pre, mid_sum, ffn_sum, post_sum = rest[tensor_size:]
        wide = h_mid.shape[2]
        if layer > 0:
            whole = whole_grads(places, grad_low, h_ffn, grad_out, grad_pre, h_mid, a_parts)
            dout_parts, whole = lax.optimization_barrier((dout_parts, whole))
            whole = whole.reshape(-1, *whole.shape[2:])
            rows = lax.psum_scatter(whole, ("dp", "tensor"), scatter_dimension=0, tiled=False)
            rows = rows.astype(F32)
            up_rows, down_rows, out_rows = (
                rows[:, :wide], rows[:, wide : 2 * wide], rows[:, 2 * wide :]
            )
        else:
            up_keep, up_send, down_keep, down_send = matrix_grads_of(
                places, grad_low, h_ffn, grad_out, grad_pre, h_mid, a_parts
            )
            dout_parts, up_send, down_send = lax.optimization_barrier(
                (dout_parts, up_send, down_send)
            )
            hops = [core_hop] + side_hops + [near_hop]
            upper_rows = scatter_pair(up_keep, up_send, hops, places)
            up_rows, out_rows = upper_rows[:, :wide], upper_rows[:, wide:]
            hops = [core_hop, near_hop] + side_hops
            down_rows = scatter_pair(down_keep, down_send, hops, places)
        packed, inner_sum, keep, send = attend_backward(
            places, dout_parts, queries, keys, values, mixture, logsum, long_column, long_row,
            attn_set[layer],
        )
        grad_head = jnp.sum(inner_sum[:local_heads], 1) / scale_rel[0, ::HD]
        arrived = swap(send, *core_hop)
        for hop in side_hops:
            keep, send = add_halves(keep, arrived)
            arrived = swap(send, *hop)
        grad_h = keep.astype(F32) + arrived.astype(F32)
        attn_keep, attn_send = attn_grads(places, h_parts, packed)
        normed_one, factor_one = normalize(stream_in)
        grad_attn_gain = jnp.sum(grad_h * normed_one, 0)
        grad_stream = grad_middle + norm_back(
            grad_h * ln_attn_gain[layer], normed_one, factor_one
        )
        attn_rows = scatter_pair(attn_keep, attn_send, [near_hop], places)
        matrix_grads[layer] = (
            attn_rows[:, :width],
            attn_rows[:, width : 2 * width],
            attn_rows[:, 2 * width :],
            out_rows.T,
            up_rows,
            down_rows.T,
        )
        grad_head_all = lax.dynamic_update_slice_in_dim(
            jnp.zeros((H,), F32), grad_head, places.tensor_index * local_heads, 0
        )
        grad_mid_all = jnp.sum(mid_sum, 1)[places.tensor_sources].reshape(-1)
        small_grads[layer] = (
            grad_attn_gain, grad_head_all, jnp.sum(post_sum, 0), jnp.sum(ffn_sum, 0),
            grad_mid_all,
        )
    sizes = [part.shape[0] for part in small_grads[0]]
    vector = jnp.concatenate([part for layer in range(LAYERS) for part in small_grads[layer]])
    count = vector.shape[0]
    vector = jnp.pad(vector, (0, -count % 1024)).reshape(-1, 128)
    vector = sum_everywhere(vector).reshape(-1)
    smalls, start = [], 0
    for layer in range(LAYERS):
        found = []
        for size in sizes:
            found.append(lax.slice_in_dim(vector, start, start + size))
            start += size
        smalls.append(found)
    small = [jnp.stack([smalls[layer][at] for layer in range(LAYERS)]) for at in range(5)]
    stacked = [
        jnp.stack([matrix_grads[layer][at] for layer in range(LAYERS)]) for at in range(6)
    ]
    return (
        stream, grad_stream, small[0], stacked[0], stacked[1], stacked[2], small[1], stacked[3],
        small[2], small[3], stacked[4], small[4], stacked[5],
    )


def solution(mesh):
    rows = P(("dp", "tensor"), None)
    first = P(None, "dp", "tensor")
    second = P(None, "tensor", "dp")
    in_specs = (
        rows, P("dp", None), P(), first, first, first, P(), second, P(), P(), first, P(), second,
        rows,
    )
    out_specs = (
        rows, rows, P(), first, first, first, P(), second, P(), P(), first, P(), second,
    )
    return jax.shard_map(local, mesh=mesh, in_specs=in_specs, out_specs=out_specs, check_vma=False)
```

time: 2220 us -> 949 us (0.43)
  waiting for transfers between devices: 902 us -> 318 us
  matrix products: 549 us -> 0 us
  Pallas kernels: 0 us -> 443 us
  blocking collectives: 338 us -> 0 us
  other arithmetic: 257 us -> 63.6 us
  local copies, waits for them, and re-layouts: 94.1 us -> 28 us
  starting transfers between devices: 20.7 us -> 75.1 us
  loops' own time: 32.7 us -> 0 us
    reduce_scatter x12 -> x1, waiting for transfers between devices: 594 us -> 0.02 us  [local(): lax.psum_scatter(whole, ('dp', 'tensor'), scatter_dimension=0, tiled=False)]
    dot_general x92 -> x0, matrix products: 549 us -> none  [the longest x8 93 us: one_block(): jnp.einsum('qhd,khd->hqk', grad_block, values, preferred_element_type=jnp...]
    pallas_call x0 -> x12, Pallas kernels: none -> 443 us  [the longest x2 110 us: ffn_backward(): pl.pallas_call(functools.partial(ffn_backward_kernel, parts), in_specs=[p...]
    ppermute x0 -> x55, waiting for transfers between devices: none -> 278 us  [swap(): return lax.ppermute(array, axis, [(i, i ^ mask) for i in range(size)])]
    all_gather x8 -> x0, blocking collectives: 254 us -> none  [the longest x2 66.9 us: local(): lax.all_gather(w_key[layer_index].astype(jnp.bfloat16), 'dp', axis=0, til...]
    all_gather x12 -> x2, waiting for transfers between devices: 226 us -> 39.6 us  [local(): whole = lax.all_gather(packed, ('dp', 'tensor'), axis=0, tiled=False)]
    convert_element_type x22 -> x12, other arithmetic: 130 us -> 24.6 us  [the longest x10 23.1 us: add_low(): return (kept.astype(F32) + arrived.astype(F32)).astype(BF16)]
    psum x5 -> x0, blocking collectives: 83.8 us -> none  [the longest x1 40.5 us: local(): lax.psum((jnp.stack(attn_gain_grads), head_full, jnp.stack(post_gain_grad...]
  transfers between devices with their start and end apart: 28 -> 58, of which waited for: 19 -> 26; matrix products, arithmetic and copies ran while one was open for 17% -> 8% of each run, Pallas kernels for 0% -> 36%
where the time goes in v1:
time: 949 us; the launch traced here: 942 us
  Pallas kernels  443 us (47%)
  waiting for transfers between devices  318 us (34%)
  starting transfers between devices  75.1 us (8%)
  other arithmetic  63.6 us (7%)
  local copies, waits for them, and re-layouts  28 us (3%)
  between operations  14.9 us (2%)
    ppermute x55, waiting for transfers between devices, swap(): return lax.ppermute(array, axis, [(i, i ^ mask) for i in range(size)])  278 us
    pallas_call x2, Pallas kernels, ffn_backward(): pl.pallas_call(functools.partial(ffn_backward_kernel, parts), in_specs=[p...  110 us
    pallas_call x2, Pallas kernels, ffn_forward(): pl.pallas_call(functools.partial(ffn_forward_kernel, parts, last), in_spe...  105 us
    pallas_call x2, Pallas kernels, attend_backward(): pl.pallas_call(backward_kernel, in_specs=[scalars] * 4 + [whole] * (parts...  100 us
    ppermute x55, starting transfers between devices, swap(): return lax.ppermute(array, axis, [(i, i ^ mask) for i in range(size)])  74.9 us
    pallas_call x2, Pallas kernels, attend_forward(): pl.pallas_call(forward_kernel, in_specs=[pl.BlockSpec(memory_space=pltpu....  74 us
    all_gather x2, waiting for transfers between devices, local(): whole = lax.all_gather(packed, ('dp', 'tensor'), axis=0, tiled=False)  39.6 us
    convert_element_type x10, other arithmetic, add_low(): return (kept.astype(F32) + arrived.astype(F32)).astype(BF16)  23.1 us
  transfers between devices with their start and end apart: 58, of which 26 were waited for; matrix products, arithmetic and copies ran while one was open for 8% of the time, Pallas kernels for 36%

profile of v1, /device:TPU:0, one launch (start us, length us, event | category | flops | bytes accessed | tf_op | source)
XLA Modules:
  0.0 941.9 jit_solution(6202902877129626738)
XLA Ops:
  22.6 21.7 %collective-permute-done.refs_1_ = bf16[512,1024]{1,0:T(8,128)(2,1)} collective-permute-done((bf16[512,1024]{1,0:T(8,128)(2,1)S(1)}, bf16[512,1024]{1,0:T(8,128)(2,1)}, u32[]{:S(2)}, u32[]{:S(2)}) %collective-permute-start) | collective-permute-done | bytes 1048608 | tf_op jit(solution)/shard_map/ppermute | solution.py:74
  50.1 21.6 %collective-permute-done.6.refs_5_.refs_12_ = bf16[4,128,768]{2,1,0:T(8,128)(2,1)S(1)} collective-permute-done((bf16[4,128,768]{2,1,0:T(8,128)(2,1)S(1)}, bf16[4,128,768]{2,1,0:T(8,128)(2,1)S(1)}, u32[]{:S(2)}, u32[]{:S(2)}) %collective-permute-start.6) | collective-permute-done | bytes 786464 | tf_op jit(solution)/shard_map/ppermute | solution.py:74
  72.6 36.9 %attend_forward.2 = (bf16[2048,256]{1,0:T(8,128)(2,1)}, bf16[2048,256]{1,0:T(8,128)(2,1)}, bf16[2048,256]{1,0:T(8,128)(2,1)}, f32[2048,256]{1,0:T(8,128)}, f32[8...) custom-call(s32[4]{0:T(128)} %get-tuple-element.290.block_ref.place_, ...), custom_call_target="tpu_custom_call" | custom-call | flops 13958643712 | bytes 20971520 | tf_op jit(solution)/shard_map/attend_forward/pallas_call | solution.py:795
  115.1 9.4 %collective-permute-done.7.refs_2_ = bf16[512,256]{1,0:T(8,128)(2,1)} collective-permute-done((bf16[512,256]{1,0:T(8,128)(2,1)}, bf16[512,256]{1,0:T(8,128)(2,1)}, u32[]{:S(2)}, u32[]{:S(2)}) %collective-permute-start.7) | collective-permute-done | bytes 262176 | tf_op jit(solution)/shard_map/ppermute | solution.py:74
  124.6 9.5 %collective-permute-done.9.refs_4_ = bf16[512,256]{1,0:T(8,128)(2,1)} collective-permute-done((bf16[512,256]{1,0:T(8,128)(2,1)}, bf16[512,256]{1,0:T(8,128)(2,1)}, u32[]{:S(2)}, u32[]{:S(2)}) %collective-permute-start.9) | collective-permute-done | bytes 262176 | tf_op jit(solution)/shard_map/ppermute | solution.py:74
  134.0 39.6 %all-gather.3.cloned.1.call-done = bf16[32,128,2304]{2,1,0:T(8,128)(2,1)} async-done(((bf16[1,128,2304]{2,1,0:T(8,128)(2,1)}), bf16[32,128,2304]{2,1,0:T(8,128)(2,1)}) %all-gather.3.cloned.1.call-update) | async-done | bytes 18874384 | tf_op jit(solution)/shard_map/all_gather | solution.py:1001
  173.6 55.7 %ffn_forward.2 = (f32[512,1024]{1,0:T(8,128)}, f32[512,1024]{1,0:T(8,128)}, f32[512,1024]{1,0:T(8,128)}, bf16[512,1024]{1,0:T(8,128)(2,1)}, f32[512,128]{1,0:T(8...) custom-call(s32[4]{0:T(128)} %get-tuple-element.290.block_ref.place_, ...), custom_call_target="tpu_custom_call" | custom-call | flops 9663676416 | bytes 41943040 | tf_op jit(solution)/shard_map/ffn_forward/pallas_call | solution.py:308
  235.3 27.5 %collective-permute-done.10.refs_1_ = bf16[512,1024]{1,0:T(8,128)(2,1)S(1)} collective-permute-done((bf16[512,1024]{1,0:T(8,128)(2,1)}, bf16[512,1024]{1,0:T(8,128)(2,1)S(1)}, u32[]{:S(2)}, u32[]{:S(2)}) %collective-permute-start.10) | collective-permute-done | bytes 1048608 | tf_op jit(solution)/shard_map/ppermute | solution.py:74
  266.8 31.3 %collective-permute-done.16.refs_5_.refs_12_ = bf16[4,128,768]{2,1,0:T(8,128)(2,1)} collective-permute-done((bf16[4,128,768]{2,1,0:T(8,128)(2,1)S(1)}, bf16[4,128,768]{2,1,0:T(8,128)(2,1)}, u32[]{:S(2)}, u32[]{:S(2)}) %collective-permute-start.16) | collective-permute-done | bytes 786464 | tf_op jit(solution)/shard_map/ppermute | solution.py:74
  299.2 37.1 %attend_forward.3 = (bf16[2048,256]{1,0:T(8,128)(2,1)}, bf16[2048,256]{1,0:T(8,128)(2,1)}, bf16[2048,256]{1,0:T(8,128)(2,1)}, f32[2048,256]{1,0:T(8,128)}, f32[8...) custom-call(s32[4]{0:T(128)} %get-tuple-element.290.block_ref.place_, ...), custom_call_target="tpu_custom_call" | custom-call | flops 13958643712 | bytes 20971520 | tf_op jit(solution)/shard_map/attend_forward/pallas_call | solution.py:795
  340.3 5.4 collective-permute-done.17.refs_2_
  349.3 49.4 %ffn_forward.3 = (f32[512,1024]{1,0:T(8,128)}, f32[512,1024]{1,0:T(8,128)}, f32[512,1024]{1,0:T(8,128)}, bf16[512,1024]{1,0:T(8,128)(2,1)}, f32[512,128]{1,0:T(8...) custom-call(s32[4]{0:T(128)} %get-tuple-element.290.block_ref.place_ref, ...), custom_call_target="tpu_custom_call" | custom-call | flops 9663676416 | bytes 41943040 | tf_op jit(solution)/shard_map/ffn_forward/pallas_call | solution.py:308
  398.7 54.8 %ffn_backward.2 = (bf16[512,1024]{1,0:T(8,128)(2,1)}, f32[512,1024]{1,0:T(8,128)}, bf16[512,1024]{1,0:T(8,128)(2,1)}, bf16[512,256]{1,0:T(8,128)(2,1)}, bf16[512...) custom-call(s32[4]{0:T(128)} %get-tuple-element.290.block_ref.place_, ...), custom_call_target="tpu_custom_call" | custom-call | flops 9663676416 | bytes 46137344 | tf_op jit(solution)/shard_map/ffn_backward/pallas_call | solution.py:470
  458.0 17.9 %whole_grads.1 = bf16[8,4,128,2304]{3,2,1,0:T(8,128)(2,1)} custom-call(s32[4]{0:T(128)} %get-tuple-element.290.block_ref.place_ref, bf16[512,1024]{1,0:T(8,128)(2,1)} %get-tuple-element.121.refs_0_, bf16[512,1024]{1,0:T(8,128)(2,1)} %get-tuple-element.122.refs_1_, bf16[512,1024]{1,0:T(8,128)(2,1)} %get-tuple-element.123.refs_2_, ...), custom_call_target="tpu_custom_call" | custom-call | flops 9663676416 | bytes 31457280 | tf_op jit(solution)/shard_map/whole_grads/pallas_call | solution.py:640
  478.1 50.2 %attend_backward.2 = (bf16[2048,768]{1,0:T(8,128)(2,1)}, f32[8,128]{1,0:T(8,128)}, bf16[2,512,1024]{2,1,0:T(8,128)(2,1)}, bf16[2,512,1024]{2,1,0:T(8,128)(2,1)}) custom-call(s32[4]{0:T(128)} %get-tuple-element.290.block_ref.place_ref, s32[8]{0:T(128)} %broadcast_xor_fusion.place_ref, s32[10]{0:T(128)} %constant.44.clone.open_ref, ...), custom_call_target="tpu_custom_call" | custom-call | flops 30064771072 | bytes 16777216 | tf_op jit(solution)/shard_map/attend_backward/pallas_call | solution.py:923
  538.3 8.0 attn_grads.3
  549.6 17.9 %collective-permute-done.39 = bf16[4,128,768]{2,1,0:T(8,128)(2,1)} collective-permute-done((bf16[4,128,768]{2,1,0:T(8,128)(2,1)}, bf16[4,128,768]{2,1,0:T(8,128)(2,1)}, u32[]{:S(2)}, u32[]{:S(2)}) %collective-permute-start.39) | collective-permute-done | bytes 786464 | tf_op jit(solution)/shard_map/ppermute | solution.py:74
  581.9 55.1 %ffn_backward.3 = (bf16[512,1024]{1,0:T(8,128)(2,1)}, f32[512,1024]{1,0:T(8,128)}, bf16[512,1024]{1,0:T(8,128)(2,1)}, bf16[512,256]{1,0:T(8,128)(2,1)}, bf16[512...) custom-call(s32[4]{0:T(128)} %get-tuple-element.290.block_ref.place_, ...), custom_call_target="tpu_custom_call" | custom-call | flops 9663676416 | bytes 46137344 | tf_op jit(solution)/shard_map/ffn_backward/pallas_call | solution.py:470
  639.2 19.8 %matrix_grads.1 = (bf16[2,2,4,128,1280]{4,3,2,1,0:T(8,128)(2,1)}, bf16[2,2,4,128,1280]{4,3,2,1,0:T(8,128)(2,1)}, bf16[2,2,4,128,1024]{4,3,2,1,0:T(8,128)(2,1)}, bf16[2,2,4,128,1024]{4,3,2,1,0:T(8,128)(2,1)}) custom-call(s32[8]{0:T(128)} %broadcast_xor_fusion.place_ref, bf16[512,1024]{1,0:T(8,128)(2,1)} %get-tuple-element.147.refs_0_, ...), custom_call_target="tpu_custom_call" | custom-call | flops 9663676416 | bytes 31457280 | tf_op jit(solution)/shard_map/matrix_grads/pallas_call | solution.py:578
  659.6 49.9 %attend_backward.3 = (bf16[2048,768]{1,0:T(8,128)(2,1)}, f32[8,128]{1,0:T(8,128)}, bf16[2,512,1024]{2,1,0:T(8,128)(2,1)}, bf16[2,512,1024]{2,1,0:T(8,128)(2,1)}) custom-call(s32[4]{0:T(128)} %get-tuple-element.290.block_ref.place_ref, s32[8]{0:T(128)} %broadcast_xor_fusion.place_ref, s32[10]{0:T(128)} %constant.44.clone.open_ref, ...), custom_call_target="tpu_custom_call" | custom-call | flops 30064771072 | bytes 16777216 | tf_op jit(solution)/shard_map/attend_backward/pallas_call | solution.py:923
  709.5 7.9 attn_grads.2
  726.8 4.5 collective-permute-start.42
  738.9 4.7 collective-permute-start.36
  744.5 7.1 collective-permute-done.36
  764.2 5.5 add_convert_fusion.3
  771.6 4.8 add_convert_fusion.1
  777.9 11.9 %collective-permute-done.29 = bf16[512,1024]{1,0:T(8,128)(2,1)S(1)} collective-permute-done((bf16[512,1024]{1,0:T(8,128)(2,1)S(1)}, bf16[512,1024]{1,0:T(8,128)(2,1)S(1)}, u32[]{:S(2)}, u32[]{:S(2)}) %collective-permute-start.29) | collective-permute-done | bytes 1048608 | tf_op jit(solution)/shard_map/ppermute | solution.py:74
  797.2 46.3 %collective-permute-done.31 = f32[120,128]{1,0:T(8,128)S(1)} collective-permute-done((f32[120,128]{1,0:T(8,128)S(1)}, f32[120,128]{1,0:T(8,128)S(1)}, u32[]{:S(2)}, u32[]{:S(2)}) %collective-permute-start.31) | collective-permute-done | bytes 61472 | tf_op jit(solution)/shard_map/ppermute | solution.py:74
  871.2 13.4 %collective-permute-done.51 = bf16[4,128,1024]{2,1,0:T(8,128)(2,1)S(1)} collective-permute-done((bf16[4,128,1024]{2,1,0:T(8,128)(2,1)S(1)}, bf16[4,128,1024]{2,1,0:T(8,128)(2,1)S(1)}, u32[]{:S(2)}, u32[]{:S(2)}) %collective-permute-start.51) | collective-permute-done | bytes 1048608 | tf_op jit(solution)/shard_map/ppermute | solution.py:74
  896.9 9.6 %collective-permute-done.52 = bf16[128,1024]{1,0:T(8,128)(2,1)S(1)} collective-permute-done((bf16[128,1024]{1,0:T(8,128)(2,1)S(1)}, bf16[128,1024]{1,0:T(8,128)(2,1)S(1)}, u32[]{:S(2)}, u32[]{:S(2)}) %collective-permute-start.52) | collective-permute-done | bytes 262176 | tf_op jit(solution)/shard_map/ppermute | solution.py:74
  906.5 4.5 collective-permute-start.48
  911.8 18.4 %collective-permute-done.46 = bf16[128,1280]{1,0:T(8,128)(2,1)S(1)} collective-permute-done((bf16[128,1280]{1,0:T(8,128)(2,1)S(1)}, bf16[128,1280]{1,0:T(8,128)(2,1)S(1)}, u32[]{:S(2)}, u32[]{:S(2)}) %collective-permute-start.46) | collective-permute-done | bytes 327712 | tf_op jit(solution)/shard_map/ppermute | solution.py:74
  (331 shorter events, 169.8 us)
Async XLA Ops:
  7.2 166.4 %all-gather.3.cloned.1.call-start = ((), (), s32[]{:S(2)}) async-start(), calls=%async_computation.1 | async-start | bytes 19464192 | tf_op jit(solution)/shard_map/all_gather | solution.py:1001
  11.1 329.2 %all-gather.5.cloned.1.call-start = ((), (), s32[]{:S(2)}) async-start(), calls=%async_computation.2 | async-start | bytes 19464192 | tf_op jit(solution)/shard_map/all_gather | solution.py:1001
  12.0 918.5 %reduce-scatter.2.cloned.1.call-start = ((), (), s32[]{:S(2)}) async-start(), calls=%async_computation.3 | async-start | bytes 19464192 | tf_op jit(solution)/shard_map/reduce_scatter | solution.py:1064
  13.7 30.5 %collective-permute-start = (bf16[512,1024]{1,0:T(8,128)(2,1)S(1)}, bf16[512,1024]{1,0:T(8,128)(2,1)}, u32[]{:S(2)}, u32[]{:S(2)}) collective-permute-start(bf16[512,1024]{1,0:T(8,128)(2,1)S(1)} %multiply_convert_fusion.refs_0_), channel_id=1, source_target_pairs={{0,2},{1,3},{2,0},{3,1},{4,6},{5,7},{6,4},{7,5},{8,10},{9,11},{10,... | collective-permute-start | bytes 3145736 | tf_op jit(solution)/shard_map/ppermute | solution.py:74
  18.1 26.1 %collective-permute-start.3 = (bf16[128,768]{1,0:T(8,128)(2,1)S(1)}, bf16[128,768]{1,0:T(8,128)(2,1)S(1)}, u32[]{:S(2)}, u32[]{:S(2)}) collective-permute-start(bf16[128,768]{1,0:T(8,128)(2,1)S(1)} %pad_maximum_fusion.12), channel_id=1, source_target_pairs={{0,16},{4,20},{8,24},{12,28},{16,0},{20,4},{24,8},{28,12},{1,17},{... | collective-permute-start | bytes 589832 | tf_op jit(solution)/shard_map/ppermute | solution.py:74
  20.8 23.5 %collective-permute-start.4 = (bf16[128,768]{1,0:T(8,128)(2,1)S(1)}, bf16[128,768]{1,0:T(8,128)(2,1)S(1)}, u32[]{:S(2)}, u32[]{:S(2)}) collective-permute-start(bf16[128,768]{1,0:T(8,128)(2,1)S(1)} %pad_maximum_fusion.12), channel_id=1, source_target_pairs={{0,8},{4,12},{8,0},{12,4},{16,24},{20,28},{24,16},{28,20},{1,9},{5... | collective-permute-start | bytes 589832 | tf_op jit(solution)/shard_map/ppermute | solution.py:74
  22.6 49.2 %collective-permute-start.1 = (bf16[512,1024]{1,0:T(8,128)(2,1)S(1)}, bf16[512,1024]{1,0:T(8,128)(2,1)}, u32[]{:S(2)}, u32[]{:S(2)}) collective-permute-start(bf16[512,1024]{1,0:T(8,128)(2,1)S(1)} %multiply_convert_fusion.refs_0_), channel_id=1, source_target_pairs={{0,1},{1,0},{2,3},{3,2},{4,5},{5,4},{6,7},{7,6},{8,9},{9,8},{10,11... | collective-permute-start | bytes 3145736 | tf_op jit(solution)/shard_map/ppermute | solution.py:74
  44.2 27.5 %collective-permute-start.2 = (bf16[512,1024]{1,0:T(8,128)(2,1)}, bf16[512,1024]{1,0:T(8,128)(2,1)}, u32[]{:S(2)}, u32[]{:S(2)}) collective-permute-start(bf16[512,1024]{1,0:T(8,128)(2,1)} %collective-permute-done.refs_1_), channel_id=1, source_target_pairs={{0,1},{1,0},{2,3},{3,2},{4,5},{5,4},{6,7},{7,6},{8,9},{9,8},{10,11... | collective-permute-start | bytes 3145736 | tf_op jit(solution)/shard_map/ppermute | solution.py:74
  44.3 27.4 %collective-permute-start.6 = (bf16[4,128,768]{2,1,0:T(8,128)(2,1)S(1)}, bf16[4,128,768]{2,1,0:T(8,128)(2,1)S(1)}, u32[]{:S(2)}, u32[]{:S(2)}) collective-permute-start(bf16[4,128,768]{2,1,0:T(8,128)(2,1)S(1)} %pad_maximum_fusion.4.refs_4_.refs_11_), channel_id=1, source_target_pairs={{0,4},{4,0},{8,12},{12,8},{16,20},{20,16},{24,28},{28,24},{1,5},{5... | collective-permute-start | bytes 2359304 | tf_op jit(solution)/shard_map/ppermute | solution.py:74
  110.9 23.2 %collective-permute-start.9 = (bf16[512,256]{1,0:T(8,128)(2,1)}, bf16[512,256]{1,0:T(8,128)(2,1)}, u32[]{:S(2)}, u32[]{:S(2)}) collective-permute-start(bf16[512,256]{1,0:T(8,128)(2,1)} %get-tuple-element.101), channel_id=1, source_target_pairs={{0,3},{1,2},{2,1},{3,0},{4,7},{5,6},{6,5},{7,4},{8,11},{9,10},{10,... | collective-permute-start | bytes 786440 | tf_op jit(solution)/shard_map/ppermute | solution.py:74
  229.3 33.5 %collective-permute-start.10 = (bf16[512,1024]{1,0:T(8,128)(2,1)}, bf16[512,1024]{1,0:T(8,128)(2,1)S(1)}, u32[]{:S(2)}, u32[]{:S(2)}) collective-permute-start(bf16[512,1024]{1,0:T(8,128)(2,1)} %get-tuple-element.103.refs_0_), channel_id=1, source_target_pairs={{0,2},{1,3},{2,0},{3,1},{4,6},{5,7},{6,4},{7,5},{8,10},{9,11},{10,... | collective-permute-start | bytes 3145736 | tf_op jit(solution)/shard_map/ppermute | solution.py:74
  230.8 32.0 %collective-permute-start.13 = (bf16[128,768]{1,0:T(8,128)(2,1)S(1)}, bf16[128,768]{1,0:T(8,128)(2,1)S(1)}, u32[]{:S(2)}, u32[]{:S(2)}) collective-permute-start(bf16[128,768]{1,0:T(8,128)(2,1)S(1)} %pad_maximum_fusion.13), channel_id=1, source_target_pairs={{0,16},{4,20},{8,24},{12,28},{16,0},{20,4},{24,8},{28,12},{1,17},{... | collective-permute-start | bytes 589832 | tf_op jit(solution)/shard_map/ppermute | solution.py:74
  232.4 30.4 %collective-permute-start.14 = (bf16[128,768]{1,0:T(8,128)(2,1)S(1)}, bf16[128,768]{1,0:T(8,128)(2,1)S(1)}, u32[]{:S(2)}, u32[]{:S(2)}) collective-permute-start(bf16[128,768]{1,0:T(8,128)(2,1)S(1)} %pad_maximum_fusion.13), channel_id=1, source_target_pairs={{0,8},{4,12},{8,0},{12,4},{16,24},{20,28},{24,16},{28,20},{1,9},{5... | collective-permute-start | bytes 589832 | tf_op jit(solution)/shard_map/ppermute | solution.py:74
  232.9 29.9 %collective-permute-start.15 = (bf16[128,768]{1,0:T(8,128)(2,1)S(1)}, bf16[128,768]{1,0:T(8,128)(2,1)S(1)}, u32[]{:S(2)}, u32[]{:S(2)}) collective-permute-start(bf16[128,768]{1,0:T(8,128)(2,1)S(1)} %pad_maximum_fusion.13), channel_id=1, source_target_pairs={{0,24},{4,28},{8,16},{12,20},{16,8},{20,12},{24,0},{28,4},{1,25},{... | collective-permute-start | bytes 589832 | tf_op jit(solution)/shard_map/ppermute | solution.py:74
  235.3 62.9 %collective-permute-start.11 = (bf16[512,1024]{1,0:T(8,128)(2,1)}, bf16[512,1024]{1,0:T(8,128)(2,1)S(1)}, u32[]{:S(2)}, u32[]{:S(2)}) collective-permute-start(bf16[512,1024]{1,0:T(8,128)(2,1)} %get-tuple-element.103.refs_0_), channel_id=1, source_target_pairs={{0,1},{1,0},{2,3},{3,2},{4,5},{5,4},{6,7},{7,6},{8,9},{9,8},{10,11... | collective-permute-start | bytes 3145736 | tf_op jit(solution)/shard_map/ppermute | solution.py:74
  262.8 36.4 %collective-permute-start.12 = (bf16[512,1024]{1,0:T(8,128)(2,1)S(1)}, bf16[512,1024]{1,0:T(8,128)(2,1)}, u32[]{:S(2)}, u32[]{:S(2)}) collective-permute-start(bf16[512,1024]{1,0:T(8,128)(2,1)S(1)} %collective-permute-done.10.refs_1_), channel_id=1, source_target_pairs={{0,1},{1,0},{2,3},{3,2},{4,5},{5,4},{6,7},{7,6},{8,9},{9,8},{10,11... | collective-permute-start | bytes 3145736 | tf_op jit(solution)/shard_map/ppermute | solution.py:74
  263.9 34.2 %collective-permute-start.16 = (bf16[4,128,768]{2,1,0:T(8,128)(2,1)S(1)}, bf16[4,128,768]{2,1,0:T(8,128)(2,1)}, u32[]{:S(2)}, u32[]{:S(2)}) collective-permute-start(bf16[4,128,768]{2,1,0:T(8,128)(2,1)S(1)} %pad_maximum_fusion.5.refs_4_.refs_11_), channel_id=1, source_target_pairs={{0,4},{4,0},{8,12},{12,8},{16,20},{20,16},{24,28},{28,24},{1,5},{5... | collective-permute-start | bytes 2359304 | tf_op jit(solution)/shard_map/ppermute | solution.py:74
  536.7 39.0 %collective-permute-start.24 = (bf16[512,1024]{1,0:T(8,128)(2,1)}, bf16[512,1024]{1,0:T(8,128)(2,1)}, u32[]{:S(2)}, u32[]{:S(2)}) collective-permute-start(bf16[512,1024]{1,0:T(8,128)(2,1)} %fusion.12), channel_id=1, source_target_pairs={{0,2},{1,3},{2,0},{3,1},{4,6},{5,7},{6,4},{7,5},{8,10},{9,11},{10,... | collective-permute-start | bytes 3145736 | tf_op jit(solution)/shard_map/ppermute | solution.py:74
  569.5 152.0 %collective-permute-start.40 = (bf16[128,768]{1,0:T(8,128)(2,1)}, bf16[128,768]{1,0:T(8,128)(2,1)}, u32[]{:S(2)}, u32[]{:S(2)}) collective-permute-start(bf16[128,768]{1,0:T(8,128)(2,1)} %get-tuple-element.251), channel_id=1, source_target_pairs={{0,16},{4,20},{8,24},{12,28},{16,0},{20,4},{24,8},{28,12},{1,17},{... | collective-permute-start | bytes 589832 | tf_op jit(solution)/shard_map/ppermute | solution.py:74
  659.0 105.2 %collective-permute-start.49 = (bf16[2,2,4,128,1024]{4,3,2,1,0:T(8,128)(2,1)}, bf16[2,2,4,128,1024]{4,3,2,1,0:T(8,128)(2,1)}, u32[]{:S(2)}, u32[]{:S(2)}) collective-permute-start(bf16[2,2,4,128,1024]{4,3,2,1,0:T(8,128)(2,1)} %get-tuple-element.182), channel_id=1, source_target_pairs={{0,1},{1,0},{2,3},{3,2},{4,5},{5,4},{6,7},{7,6},{8,9},{9,8},{10,11... | collective-permute-start | bytes 12582920 | tf_op jit(solution)/shard_map/ppermute | solution.py:74
  659.1 112.4 %collective-permute-start.43 = (bf16[2,2,4,128,1280]{4,3,2,1,0:T(8,128)(2,1)}, bf16[2,2,4,128,1280]{4,3,2,1,0:T(8,128)(2,1)}, u32[]{:S(2)}, u32[]{:S(2)}) collective-permute-start(bf16[2,2,4,128,1280]{4,3,2,1,0:T(8,128)(2,1)} %get-tuple-element.179), channel_id=1, source_target_pairs={{0,1},{1,0},{2,3},{3,2},{4,5},{5,4},{6,7},{7,6},{8,9},{9,8},{10,11... | collective-permute-start | bytes 15728648 | tf_op jit(solution)/shard_map/ppermute | solution.py:74
  721.5 40.5 %collective-permute-start.28 = (bf16[2,512,1024]{2,1,0:T(8,128)(2,1)}, bf16[2,512,1024]{2,1,0:T(8,128)(2,1)}, u32[]{:S(2)}, u32[]{:S(2)}) collective-permute-start(bf16[2,512,1024]{2,1,0:T(8,128)(2,1)} %get-tuple-element.163), channel_id=1, source_target_pairs={{0,1},{1,0},{2,3},{3,2},{4,5},{5,4},{6,7},{7,6},{8,9},{9,8},{10,11... | collective-permute-start | bytes 6291464 | tf_op jit(solution)/shard_map/ppermute | solution.py:74
  763.6 26.2 %collective-permute-start.29 = (bf16[512,1024]{1,0:T(8,128)(2,1)S(1)}, bf16[512,1024]{1,0:T(8,128)(2,1)S(1)}, u32[]{:S(2)}, u32[]{:S(2)}) collective-permute-start(bf16[512,1024]{1,0:T(8,128)(2,1)S(1)} %fusion.14), channel_id=1, source_target_pairs={{0,2},{1,3},{2,0},{3,1},{4,6},{5,7},{6,4},{7,5},{8,10},{9,11},{10,... | collective-permute-start | bytes 3145736 | tf_op jit(solution)/shard_map/ppermute | solution.py:74
  769.7 91.0 %collective-permute-start.50 = (bf16[2,4,128,1024]{3,2,1,0:T(8,128)(2,1)}, bf16[2,4,128,1024]{3,2,1,0:T(8,128)(2,1)}, u32[]{:S(2)}, u32[]{:S(2)}) collective-permute-start(bf16[2,4,128,1024]{3,2,1,0:T(8,128)(2,1)} %get-tuple-element.237), channel_id=1, source_target_pairs={{0,4},{4,0},{8,12},{12,8},{16,20},{20,16},{24,28},{28,24},{1,5},{5... | collective-permute-start | bytes 6291464 | tf_op jit(solution)/shard_map/ppermute | solution.py:74
  776.4 87.6 %collective-permute-start.44 = (bf16[2,4,128,1280]{3,2,1,0:T(8,128)(2,1)}, bf16[2,4,128,1280]{3,2,1,0:T(8,128)(2,1)}, u32[]{:S(2)}, u32[]{:S(2)}) collective-permute-start(bf16[2,4,128,1280]{3,2,1,0:T(8,128)(2,1)} %get-tuple-element.235), channel_id=1, source_target_pairs={{0,2},{1,3},{2,0},{3,1},{4,6},{5,7},{6,4},{7,5},{8,10},{9,11},{10,... | collective-permute-start | bytes 7864328 | tf_op jit(solution)/shard_map/ppermute | solution.py:74
  795.0 48.5 %collective-permute-start.31 = (f32[120,128]{1,0:T(8,128)S(1)}, f32[120,128]{1,0:T(8,128)S(1)}, u32[]{:S(2)}, u32[]{:S(2)}) collective-permute-start(f32[120,128]{1,0:T(8,128)S(1)} %fusion.56), channel_id=1, source_target_pairs={{0,2},{1,3},{2,0},{3,1},{4,6},{5,7},{6,4},{7,5},{8,10},{9,11},{10,... | collective-permute-start | bytes 184328 | tf_op jit(solution)/shard_map/ppermute | solution.py:74
  866.4 26.5 %collective-permute-start.45 = (bf16[4,128,1280]{2,1,0:T(8,128)(2,1)S(1)}, bf16[4,128,1280]{2,1,0:T(8,128)(2,1)S(1)}, u32[]{:S(2)}, u32[]{:S(2)}) collective-permute-start(bf16[4,128,1280]{2,1,0:T(8,128)(2,1)S(1)} %get-tuple-element.239), channel_id=1, source_target_pairs={{0,4},{4,0},{8,12},{12,8},{16,20},{20,16},{24,28},{28,24},{1,5},{5... | collective-permute-start | bytes 3932168 | tf_op jit(solution)/shard_map/ppermute | solution.py:74
  887.0 24.6 %collective-permute-start.53 = (bf16[128,1024]{1,0:T(8,128)(2,1)S(1)}, bf16[128,1024]{1,0:T(8,128)(2,1)S(1)}, u32[]{:S(2)}, u32[]{:S(2)}) collective-permute-start(bf16[128,1024]{1,0:T(8,128)(2,1)S(1)} %get-tuple-element.247), channel_id=1, source_target_pairs={{0,8},{4,12},{8,0},{12,4},{16,24},{20,28},{24,16},{28,20},{1,9},{5... | collective-permute-start | bytes 786440 | tf_op jit(solution)/shard_map/ppermute | solution.py:74
  888.7 22.9 %collective-permute-start.54 = (bf16[128,1024]{1,0:T(8,128)(2,1)S(1)}, bf16[128,1024]{1,0:T(8,128)(2,1)S(1)}, u32[]{:S(2)}, u32[]{:S(2)}) collective-permute-start(bf16[128,1024]{1,0:T(8,128)(2,1)S(1)} %get-tuple-element.246), channel_id=1, source_target_pairs={{0,24},{4,28},{8,16},{12,20},{16,8},{20,12},{24,0},{28,4},{1,25},{... | collective-permute-start | bytes 786440 | tf_op jit(solution)/shard_map/ppermute | solution.py:74
  893.1 37.1 %collective-permute-start.46 = (bf16[128,1280]{1,0:T(8,128)(2,1)S(1)}, bf16[128,1280]{1,0:T(8,128)(2,1)S(1)}, u32[]{:S(2)}, u32[]{:S(2)}) collective-permute-start(bf16[128,1280]{1,0:T(8,128)(2,1)S(1)} %get-tuple-element.242), channel_id=1, source_target_pairs={{0,16},{4,20},{8,24},{12,28},{16,0},{20,4},{24,8},{28,12},{1,17},{... | collective-permute-start | bytes 983048 | tf_op jit(solution)/shard_map/ppermute | solution.py:74
  895.2 35.0 %collective-permute-start.47 = (bf16[128,1280]{1,0:T(8,128)(2,1)S(1)}, bf16[128,1280]{1,0:T(8,128)(2,1)S(1)}, u32[]{:S(2)}, u32[]{:S(2)}) collective-permute-start(bf16[128,1280]{1,0:T(8,128)(2,1)S(1)} %get-tuple-element.244), channel_id=1, source_target_pairs={{0,8},{4,12},{8,0},{12,4},{16,24},{20,28},{24,16},{28,20},{1,9},{5... | collective-permute-start | bytes 983048 | tf_op jit(solution)/shard_map/ppermute | solution.py:74
  906.5 23.7 %collective-permute-start.48 = (bf16[128,1280]{1,0:T(8,128)(2,1)S(1)}, bf16[128,1280]{1,0:T(8,128)(2,1)S(1)}, u32[]{:S(2)}, u32[]{:S(2)}) collective-permute-start(bf16[128,1280]{1,0:T(8,128)(2,1)S(1)} %get-tuple-element.243), channel_id=1, source_target_pairs={{0,24},{4,28},{8,16},{12,20},{16,8},{20,12},{24,0},{28,4},{1,25},{... | collective-permute-start | bytes 983048 | tf_op jit(solution)/shard_map/ppermute | solution.py:74
  (77 other events, 1155.6 us)
Sparse Core Ops, SparseCore 0:
  11.5 162.0 all-gather.2
  176.5 141.6 all-gather.4
  476.2 217.6 reduce-scatter.1

commit v2 on v1

--- a/solution.py
+++ b/solution.py
@@ -84,6 +84,7 @@
         masks = bit_masks(self.dp_size)
         self.far_masks = relative_order(masks[:-1])
         self.near_mask = masks[-1]
+        self.far_hops = [("dp", mask) for mask in reversed(masks[:-1])]
         dp_order = self.far_masks + [mask | self.near_mask for mask in self.far_masks]
         self.tensor_order = relative_order(self.tensor_masks)
         tensor_inverse = [self.tensor_order.index(i) for i in range(self.tensor_size)]
@@ -124,27 +125,18 @@
 
 
 def add_halves(kept, arrived):
-    return add_low(kept[0], arrived[0]), add_low(kept[1], arrived[1])
-
-
-def sum_far(kept, arrived, places):
-    blocks = [add_low(kept[i], arrived[i]) for i in range(kept.shape[0])]
-    return sum_blocks(blocks, places)
-
-
-def sum_blocks(blocks, places):
-    total = blocks[0].astype(F32)
-    for block, mask in zip(blocks[1:], places.far_masks[1:]):
-        total = total + swap(block, "dp", mask).astype(F32)
-    return total
-
-
-def scatter_pair(kept, sent, hops, places):
-    arrived = swap(sent, *hops[0])
-    for hop in hops[1:]:
+    half = kept.shape[0] // 2
+    return add_low(kept[:half], arrived[:half]), add_low(kept[half:], arrived[half:])
+
+
+def scatter_rest(kept, arrived, hops):
+    for hop in hops:
+        if kept.shape[0] == 1:
+            kept, arrived = kept[0], arrived[0]
         kept, sent = add_halves(kept, arrived)
         arrived = swap(sent, *hop)
-    return sum_far(kept, arrived, places)
+    total = kept.astype(F32) + arrived.astype(F32)
+    return total.reshape(total.shape[-2:])
 
 
 def sum_everywhere(vector):
@@ -171,11 +163,12 @@
 
 
 def each_rows(total, chunk, body):
-    def step(at, carry):
-        body(pl.ds(pl.multiple_of(at * chunk, chunk), chunk))
-        return carry
-
-    lax.fori_loop(0, total // chunk, step, 0)
+    for start in range(0, total, chunk):
+        body(pl.ds(start, chunk))
+
+
+def lanes(values, width):
+    return jnp.concatenate([values] * (width // 128), axis=1)
 
 
 def fold_lanes(values):
@@ -235,18 +228,25 @@
     each_rows(rows, CHUNK, middle_rows)
     sums[...] = jnp.zeros_like(sums)
     squares[...] = jnp.zeros_like(squares)
+
+    def write_pre(at):
+        return pltpu.make_async_copy(pre_buf.at[at % 2], pre_ref.at[at], pre_sem.at[at % 2])
+
+    def write_mid(at):
+        return pltpu.make_async_copy(mid_buf.at[at % 2], h_mid_ref.at[at], mid_sem.at[at % 2])
+
+    wait_whole(w_up.at[0], up_sem.at[0])
+    pre_buf[0] = dot_nn(h_ffn_ref[...], w_up[0])
     for at in range(parts):
-        slot = at % 2
-        wait_whole(w_up.at[at], up_sem.at[at])
-        if at >= 2:
-            pltpu.make_async_copy(
-                pre_buf.at[slot], pre_ref.at[at - 2], pre_sem.at[slot]
-            ).wait()
-        pre_buf[slot] = dot_nn(h_ffn_ref[...], w_up[at])
-        pltpu.make_async_copy(pre_buf.at[slot], pre_ref.at[at], pre_sem.at[slot]).start()
-
-        def active_rows(here, at=at, slot=slot):
-            value = tanh_gelu(pre_buf[slot, here, :])
+        write_pre(at).start()
+        if at + 1 < parts:
+            wait_whole(w_up.at[at + 1], up_sem.at[at + 1])
+            if at >= 1:
+                write_pre(at - 1).wait()
+            pre_buf[(at + 1) % 2] = dot_nn(h_ffn_ref[...], w_up[at + 1])
+
+        def active_rows(here, at=at):
+            value = tanh_gelu(pre_buf[at % 2, here, :])
             active[at, here, :] = value
             sums[here, :] += fold_lanes(value)
             squares[here, :] += fold_lanes(value * value)
@@ -256,25 +256,28 @@
     spread = jnp.sum(squares[...], axis=1, keepdims=True) / hidden - mean * mean
     mean_ref[...] = jnp.broadcast_to(mean, mean_ref.shape)
     factor_ref[...] = jnp.broadcast_to(lax.rsqrt(spread + NORM_EPSILON), factor_ref.shape)
+
+    def mid_part(at):
+        def mid_rows(here):
+            normed = active[at, here, :] - lanes(mean_ref[here, :], wide)
+            normed = normed * lanes(factor_ref[here, :], wide)
+            mid_buf[at % 2, here, :] = (normed * mid_ref[at : at + 1, :]).astype(BF16)
+
+        each_rows(rows, CHUNK, mid_rows)
+
+    mid_part(0)
     for at in range(parts):
-        slot = at % 2
-        if at >= 2:
-            pltpu.make_async_copy(
-                mid_buf.at[slot], h_mid_ref.at[at - 2], mid_sem.at[slot]
-            ).wait()
-
-        def mid_rows(here, at=at, slot=slot):
-            normed = (active[at, here, :] - mean_ref[here, :1]) * factor_ref[here, :1]
-            mid_buf[slot, here, :] = (normed * mid_ref[at : at + 1, :]).astype(BF16)
-
-        each_rows(rows, CHUNK, mid_rows)
-        pltpu.make_async_copy(mid_buf.at[slot], h_mid_ref.at[at], mid_sem.at[slot]).start()
+        write_mid(at).start()
         wait_whole(w_down.at[at], down_sem.at[at])
-        product = dot_nt(mid_buf[slot], w_down[at])
+        if 1 <= at < parts - 1:
+            write_mid(at - 1).wait()
+        product = dot_nt(mid_buf[at % 2], w_down[at])
         if at == 0:
             next_stream_ref[...] = middle_ref[...] + product
         else:
             next_stream_ref[...] += product
+        if at + 1 < parts:
+            mid_part(at + 1)
     if not last:
 
         def next_rows(here):
@@ -283,9 +286,8 @@
 
         each_rows(rows, CHUNK, next_rows)
     for at in range(max(parts - 2, 0), parts):
-        slot = at % 2
-        pltpu.make_async_copy(pre_buf.at[slot], pre_ref.at[at], pre_sem.at[slot]).wait()
-        pltpu.make_async_copy(mid_buf.at[slot], h_mid_ref.at[at], mid_sem.at[slot]).wait()
+        write_pre(at).wait()
+        write_mid(at).wait()
 
 
 def ffn_forward(places, stream, a_parts, matrices, post, ffn, mid, following, last):
@@ -386,22 +388,26 @@
     mid_sum_ref[...] = jnp.zeros_like(mid_sum_ref)
     ffn_sum_ref[...] = jnp.zeros_like(ffn_sum_ref)
     post_sum_ref[...] = jnp.zeros_like(post_sum_ref)
+    wait_whole(weights.at[0], weight_sem.at[0])
+    product[0] = dot_nn(low_ref[...], weights[0])
     for at in range(parts):
-        wait_whole(weights.at[at], weight_sem.at[at])
-        product[...] = dot_nn(low_ref[...], weights[at])
         start_rows(place_ref[at], matrix_ref, up_columns, weights.at[at], weight_sem.at[at])
         read_pre(at).wait()
+        if at + 1 < parts:
+            wait_whole(weights.at[at + 1], weight_sem.at[at + 1])
+            product[(at + 1) % 2] = dot_nn(low_ref[...], weights[at + 1])
 
         def hidden_rows(here, at=at):
             value = pre_buf[at % 2, here, :]
             squared = value * value
-            bend = jnp.tanh(0.7978845608028654 * (value + 0.044715 * squared * value))
-            raised = 0.5 * (1.0 + bend)
-            normed = (value * raised - mean_ref[here, :1]) * factor_ref[here, :1]
-            steep = 0.7978845608028654 * (1.0 + 0.134145 * squared)
-            slope[at, here, :] = raised + 0.5 * value * (1.0 - bend * bend) * steep
-            normed_four[at, here, :] = normed
-            grad = product[here, :]
+            bend = jnp.tanh(value * (0.7978845608028654 + 0.035677408136300125 * squared))
+            raised = 0.5 + 0.5 * bend
+            normed = value * raised - lanes(mean_ref[here, :], wide)
+            normed = normed * lanes(factor_ref[here, :], wide)
+            steep = value * (0.7978845608028654 + 0.10703222440890037 * squared)
+            slope[at, here, :] = raised + 0.5 * steep * (1.0 - bend * bend)
+            normed_four[at, here, :] = normed.astype(BF16)
+            grad = product[at % 2, here, :]
             mid_sum_ref[at] += fold_rows(grad * normed)
             grad = grad * mid_ref[at : at + 1, :]
             grad_normed[at, here, :] = grad
@@ -421,26 +427,32 @@
     def write_low(at):
         return pltpu.make_async_copy(low_buf.at[at % 2], grad_pre_ref.at[at], low_sem.at[at % 2])
 
+    def low_part(at):
+        def pre_rows(here):
+            normed = normed_four[at, here, :].astype(F32)
+            grad = grad_normed[at, here, :] - lanes(first[here, :], wide)
+            grad = grad - normed * lanes(second[here, :], wide)
+            grad = grad * slope[at, here, :] * lanes(factor_ref[here, :], wide)
+            low_buf[at % 2, here, :] = grad.astype(BF16)
+
+        each_rows(rows, CHUNK, pre_rows)
+
+    low_part(0)
     for at in range(parts):
-        if at >= 2:
-            write_low(at - 2).wait()
-
-        def pre_rows(here, at=at):
-            grad = grad_normed[at, here, :] - first[here, :1]
-            grad = factor_ref[here, :1] * (grad - normed_four[at, here, :] * second[here, :1])
-            low_buf[at % 2, here, :] = (grad * slope[at, here, :]).astype(BF16)
-
-        each_rows(rows, CHUNK, pre_rows)
         write_low(at).start()
         wait_whole(weights.at[at], weight_sem.at[at])
+        if 1 <= at < parts - 1:
+            write_low(at - 1).wait()
         part = dot_nt(low_buf[at % 2], weights[at])
         if at == 0:
-            product[...] = part
+            product[0] = part
         else:
-            product[...] += part
+            product[0] += part
+        if at + 1 < parts:
+            low_part(at + 1)
 
     def middle_rows(here):
-        grad = product[here, :]
+        grad = product[0, here, :]
         normed, factor = normalize(middle_ref[here, :])
         ffn_sum_ref[...] += fold_rows(grad * normed)
         grad = grad_ref[here, :] + norm_back(grad * ffn_ref[...], normed, factor)
@@ -486,10 +498,10 @@
             pltpu.VMEM((parts, depth, wide), BF16),
             pltpu.VMEM((parts, depth, narrow), BF16),
             pltpu.VMEM((parts, rows, wide), F32),
-            pltpu.VMEM((parts, rows, wide), F32),
+            pltpu.VMEM((parts, rows, wide), BF16),
             pltpu.VMEM((parts, rows, wide), F32),
             pltpu.VMEM((2, rows, wide), F32),
-            pltpu.VMEM((rows, depth), F32),
+            pltpu.VMEM((2, rows, depth), F32),
             pltpu.VMEM((2, rows, wide), BF16),
             pltpu.VMEM((rows, 128), F32),
             pltpu.VMEM((rows, 128), F32),
@@ -522,89 +534,110 @@
 
 
 def turned(place_ref, source, plain, target, rows):
-    plain[...] = source[...].astype(F32).T.astype(BF16)
+    plain[...] = source[...].astype(BF16).astype(F32).T.astype(BF16)
     for at in range(target.shape[0] // rows):
         target[at * rows : (at + 1) * rows, :] = plain[block_rows(place_ref, at, rows), :]
 
 
-def matrix_grads_kernel(parts, place_ref, *refs):
-    low_ref, h_ffn_ref, grad_out_ref = refs[:3]
-    grad_pre_ref, h_mid_ref, a_ref = refs[3:6]
-    up_keep, up_send, down_keep, down_send = refs[6:10]
-    low_turned, h_turned, out_turned, low_plain, h_plain, out_plain = refs[10:]
+def up_grads_kernel(parts, place_ref, *refs):
+    h_ffn_ref, grad_out_ref, grad_pre_ref, a_ref, keep_ref, send_ref = refs[:6]
+    h_turned, out_turned, h_plain, out_plain = refs[6:]
     step = pl.program_id(0)
-    depth = low_turned.shape[0]
-    count, rows = up_keep.shape[2:4]
-    wide = h_mid_ref.shape[2]
+    count, rows = keep_ref.shape[2:4]
+    wide = grad_pre_ref.shape[2]
 
     @pl.when(step == 0)
     def _():
-        turned(place_ref, low_ref, low_plain, low_turned, rows)
         turned(place_ref, h_ffn_ref, h_plain, h_turned, rows)
         turned(place_ref, grad_out_ref, out_plain, out_turned, rows)
 
-    def fill(up_ref, down_ref):
+    def fill(target):
         shape = (2, count, rows, -1)
         grad = dot_nn(h_turned[...], grad_pre_ref[0]).astype(BF16)
-        up_ref[0, :, :, :, :wide] = grad.reshape(shape)
+        target[0, :, :, :, :wide] = grad.reshape(shape)
         grad = dot_nn(out_turned[...], a_ref[0]).astype(BF16)
-        up_ref[0, :, :, :, wide:] = grad.reshape(shape)
-        grad = dot_nn(low_turned[...], h_mid_ref[0]).astype(BF16)
-        down_ref[:, 0] = grad.reshape(shape)
+        target[0, :, :, :, wide:] = grad.reshape(shape)
 
     @pl.when(step < parts // 2)
     def _():
-        fill(up_keep, down_keep)
+        fill(keep_ref)
 
     @pl.when(step >= parts // 2)
     def _():
-        fill(up_send, down_send)
-
-
-def matrix_grads_of(places, low, h_ffn, grad_out, grad_pre, h_mid, a_parts):
-    rows, depth = low.shape
-    parts, _, wide = h_mid.shape
-    narrow = a_parts[0].shape[1]
+        fill(send_ref)
+
+
+def down_grads_kernel(parts, place_ref, *refs):
+    grad_ref, h_mid_ref, keep_ref, send_ref, low_turned, low_plain = refs
+    step = pl.program_id(0)
+    count, rows = keep_ref.shape[2:4]
+
+    @pl.when(step == 0)
+    def _():
+        turned(place_ref, grad_ref, low_plain, low_turned, rows)
+
+    def fill(target):
+        grad = dot_nn(low_turned[...], h_mid_ref[0]).astype(BF16)
+        target[:, 0] = grad.reshape(2, count, rows, -1)
+
+    @pl.when(step < parts // 2)
+    def _():
+        fill(keep_ref)
+
+    @pl.when(step >= parts // 2)
+    def _():
+        fill(send_ref)
+
+
+def split_grads(kernel, name, places, turns, sides, block, outside, at_part):
+    parts, rows, _ = sides[0].shape
+    depth = turns[0].shape[1]
     half = parts // 2
-    count = places.dp_size // 2
-    block = depth // places.dp_size
-    a_all = jnp.stack(a_parts)
+    columns = sum(side.shape[2] for side in sides)
     whole = pl.BlockSpec((rows, depth), lambda i, place: (0, 0))
-    each = pl.BlockSpec((1, rows, wide), lambda i, place: (i, 0, 0))
-    up = (half, 2, count, block, wide + narrow)
-    down = (2, half, count, block, wide)
-    up_block = (1, 2, count, block, wide + narrow)
-    down_block = (2, 1, count, block, wide)
     return pl.pallas_call(
-        functools.partial(matrix_grads_kernel, parts),
+        functools.partial(kernel, parts),
         grid_spec=pltpu.PrefetchScalarGridSpec(
             num_scalar_prefetch=1,
             grid=(parts,),
-            in_specs=[whole] * 3
-            + [each] * 2
-            + [pl.BlockSpec((1, rows, narrow), lambda i, place: (i, 0, 0))],
+            in_specs=[whole] * len(turns)
+            + [pl.BlockSpec((1,) + side.shape[1:], lambda i, place: (i, 0, 0)) for side in sides],
             out_specs=[
-                pl.BlockSpec(up_block, lambda i, p: (jnp.minimum(i, half - 1), 0, 0, 0, 0)),
-                pl.BlockSpec(up_block, lambda i, p: (jnp.maximum(i - half, 0), 0, 0, 0, 0)),
-                pl.BlockSpec(down_block, lambda i, p: (0, jnp.minimum(i, half - 1), 0, 0, 0)),
-                pl.BlockSpec(down_block, lambda i, p: (0, jnp.maximum(i - half, 0), 0, 0, 0)),
+                pl.BlockSpec(block, lambda i, place: at_part(jnp.minimum(i, half - 1))),
+                pl.BlockSpec(block, lambda i, place: at_part(jnp.maximum(i - half, 0))),
             ],
-            scratch_shapes=[pltpu.VMEM((depth, rows), BF16)] * 6,
+            scratch_shapes=[pltpu.VMEM((depth, rows), BF16)] * (2 * len(turns)),
         ),
-        out_shape=[
-            jax.ShapeDtypeStruct(up, BF16),
-            jax.ShapeDtypeStruct(up, BF16),
-            jax.ShapeDtypeStruct(down, BF16),
-            jax.ShapeDtypeStruct(down, BF16),
-        ],
+        out_shape=[jax.ShapeDtypeStruct(outside, BF16)] * 2,
         compiler_params=pltpu.CompilerParams(vmem_limit_bytes=VMEM_LIMIT),
         cost_estimate=pl.CostEstimate(
-            flops=2 * rows * depth * parts * (2 * wide + narrow),
-            bytes_accessed=30 << 20,
+            flops=2 * rows * depth * parts * columns,
+            bytes_accessed=16 << 20,
             transcendentals=0,
         ),
-        name="matrix_grads",
-    )(places.dp_places, low, h_ffn, grad_out, grad_pre, h_mid, a_all)
+        name=name,
+    )(places.dp_places, *turns, *sides)
+
+
+def up_grads(places, h_ffn, grad_out, grad_pre, a_parts):
+    a_all = jnp.stack(a_parts)
+    half = len(a_parts) // 2
+    count = places.dp_size // 2
+    tail = (count, h_ffn.shape[1] // places.dp_size, grad_pre.shape[2] + a_all.shape[2])
+    return split_grads(
+        up_grads_kernel, "up_grads", places, [h_ffn, grad_out], [grad_pre, a_all],
+        (1, 2) + tail, (half, 2) + tail, lambda part: (part, 0, 0, 0, 0),
+    )
+
+
+def down_grads(places, grad, h_mid):
+    half = h_mid.shape[0] // 2
+    count = places.dp_size // 2
+    tail = (count, grad.shape[1] // places.dp_size, h_mid.shape[2])
+    return split_grads(
+        down_grads_kernel, "down_grads", places, [grad], [h_mid],
+        (2, 1) + tail, (2, half) + tail, lambda part: (0, part, 0, 0, 0),
+    )
 
 
 def whole_grads_kernel(parts, place_ref, *refs):
@@ -1050,6 +1083,12 @@
             stream_in, h_parts, queries, keys, values, mixture, logsum, scale_rel, a_parts,
             attn_out, middle, h_ffn, mean, factor, gain_mid, pre, h_mid,
         ) = saved[layer]
+        if layer == 0:
+            down_keep, down_send = down_grads(places, grad_stream, h_mid)
+            grad_stream, down_keep, down_send = lax.optimization_barrier(
+                (grad_stream, down_keep, down_send)
+            )
+            down_arrived = swap(down_send, *core_hop)
         grad_low, grad_middle, grad_out, *rest = ffn_backward(
             places, grad_stream, attn_out, middle, mean, factor, pre, matrix_set[layer],
             ln_post_gain[layer], ln_ffn_gain[layer], gain_mid, scale_rel,
@@ -1067,34 +1106,44 @@
                 rows[:, :wide], rows[:, wide : 2 * wide], rows[:, 2 * wide :]
             )
         else:
-            up_keep, up_send, down_keep, down_send = matrix_grads_of(
-                places, grad_low, h_ffn, grad_out, grad_pre, h_mid, a_parts
+            up_keep, up_send = up_grads(places, h_ffn, grad_out, grad_pre, a_parts)
+            ups = add_halves(up_keep, swap(up_send, *core_hop))
+            downs = add_halves(down_keep, down_arrived)
+            dout_parts, ups, downs, above = lax.optimization_barrier(
+                (dout_parts, ups, downs, matrix_grads[1][:3])
             )
-            dout_parts, up_send, down_send = lax.optimization_barrier(
-                (dout_parts, up_send, down_send)
-            )
-            hops = [core_hop] + side_hops + [near_hop]
-            upper_rows = scatter_pair(up_keep, up_send, hops, places)
-            up_rows, out_rows = upper_rows[:, :wide], upper_rows[:, wide:]
-            hops = [core_hop, near_hop] + side_hops
-            down_rows = scatter_pair(down_keep, down_send, hops, places)
+            matrix_grads[1] = above + matrix_grads[1][3:]
+            side_arrived = swap(ups[1], *side_hops[0])
+            near_arrived = swap(downs[1], *near_hop)
         packed, inner_sum, keep, send = attend_backward(
             places, dout_parts, queries, keys, values, mixture, logsum, long_column, long_row,
             attn_set[layer],
         )
+        if layer == 0:
+            packed, send, side_arrived, near_arrived = lax.optimization_barrier(
+                (packed, send, side_arrived, near_arrived)
+            )
         grad_head = jnp.sum(inner_sum[:local_heads], 1) / scale_rel[0, ::HD]
         arrived = swap(send, *core_hop)
         for hop in side_hops:
             keep, send = add_halves(keep, arrived)
             arrived = swap(send, *hop)
-        grad_h = keep.astype(F32) + arrived.astype(F32)
         attn_keep, attn_send = attn_grads(places, h_parts, packed)
+        attn_arrived = swap(attn_send, *near_hop)
+        if layer > 0:
+            arrived, attn_arrived = lax.optimization_barrier((arrived, attn_arrived))
+        grad_h = (keep.astype(F32) + arrived.astype(F32)).reshape(stream_in.shape)
         normed_one, factor_one = normalize(stream_in)
         grad_attn_gain = jnp.sum(grad_h * normed_one, 0)
         grad_stream = grad_middle + norm_back(
             grad_h * ln_attn_gain[layer], normed_one, factor_one
         )
-        attn_rows = scatter_pair(attn_keep, attn_send, [near_hop], places)
+        attn_rows = scatter_rest(attn_keep, attn_arrived, places.far_hops)
+        if layer == 0:
+            hops = side_hops[1:] + [near_hop] + places.far_hops
+            upper_rows = scatter_rest(ups[0], side_arrived, hops)
+            up_rows, out_rows = upper_rows[:, :wide], upper_rows[:, wide:]
+            down_rows = scatter_rest(downs[0], near_arrived, side_hops + places.far_hops)
         matrix_grads[layer] = (
             attn_rows[:, :width],
             attn_rows[:, width : 2 * width],

time: 949 us -> 826 us (0.87)
  Pallas kernels: 443 us -> 353 us
  starting transfers between devices: 75.1 us -> 50.8 us
  waiting for transfers between devices: 318 us -> 305 us
    pallas_call x2, Pallas kernels: 105 us -> 56.1 us  [ffn_forward(): pl.pallas_call(functools.partial(ffn_forward_kernel, parts, last), in_spe...]
    pallas_call x2, Pallas kernels: 110 us -> 65.2 us  [ffn_backward(): pl.pallas_call(functools.partial(ffn_backward_kernel, parts), in_specs=[p...]
    ppermute x55 -> x51, waiting for transfers between devices: 278 us -> 248 us  [swap(): return lax.ppermute(array, axis, [(i, i ^ mask) for i in range(size)])]
    ppermute x55 -> x51, starting transfers between devices: 74.9 us -> 50.7 us  [swap(): return lax.ppermute(array, axis, [(i, i ^ mask) for i in range(size)])]
    all_gather x2, waiting for transfers between devices: 39.6 us -> 56.2 us  [local(): whole = lax.all_gather(packed, ('dp', 'tensor'), axis=0, tiled=False)]
    convert_element_type x10 -> x14, other arithmetic: 23.1 us -> 29.1 us  [add_low(): return (kept.astype(F32) + arrived.astype(F32)).astype(BF16)]
    pallas_call x1 -> x2, Pallas kernels: 19.8 us -> 24.3 us  [split_grads(): pl.pallas_call(functools.partial(kernel, parts), grid_spec=pltpu.Prefetch...]
  transfers between devices with their start and end apart: 58 -> 54, of which waited for: 26 -> 23; matrix products, arithmetic and copies ran while one was open for 8% -> 10% of each run, Pallas kernels for 36% -> 30%
where the time goes in v2:
time: 826 us; the launch traced here: 818 us
  Pallas kernels  353 us (43%)
  waiting for transfers between devices  305 us (37%)
  other arithmetic  63.3 us (8%)
  starting transfers between devices  50.8 us (6%)
  local copies, waits for them, and re-layouts  30.7 us (4%)
  between operations  15 us (2%)
    ppermute x51, waiting for transfers between devices, swap(): return lax.ppermute(array, axis, [(i, i ^ mask) for i in range(size)])  248 us
    pallas_call x2, Pallas kernels, attend_backward(): pl.pallas_call(backward_kernel, in_specs=[scalars] * 4 + [whole] * (parts...  99.5 us
    pallas_call x2, Pallas kernels, attend_forward(): pl.pallas_call(forward_kernel, in_specs=[pl.BlockSpec(memory_space=pltpu....  73.4 us
    pallas_call x2, Pallas kernels, ffn_backward(): pl.pallas_call(functools.partial(ffn_backward_kernel, parts), in_specs=[p...  65.2 us
    all_gather x2, waiting for transfers between devices, local(): whole = lax.all_gather(packed, ('dp', 'tensor'), axis=0, tiled=False)  56.2 us
    pallas_call x2, Pallas kernels, ffn_forward(): pl.pallas_call(functools.partial(ffn_forward_kernel, parts, last), in_spe...  56.1 us
    ppermute x51, starting transfers between devices, swap(): return lax.ppermute(array, axis, [(i, i ^ mask) for i in range(size)])  50.7 us
    convert_element_type x14, other arithmetic, add_low(): return (kept.astype(F32) + arrived.astype(F32)).astype(BF16)  29.1 us
  transfers between devices with their start and end apart: 54, of which 23 were waited for; matrix products, arithmetic and copies ran while one was open for 10% of the time, Pallas kernels for 30%

profile of v2, /device:TPU:0, one launch (start us, length us, event | category | flops | bytes accessed | tf_op | source)
XLA Modules:
  0.0 817.6 jit_solution(3063453480188326638)
XLA Ops:
  22.6 21.6 %collective-permute-done.refs_1_ = bf16[512,1024]{1,0:T(8,128)(2,1)} collective-permute-done((bf16[512,1024]{1,0:T(8,128)(2,1)S(1)}, bf16[512,1024]{1,0:T(8,128)(2,1)}, u32[]{:S(2)}, u32[]{:S(2)}) %collective-permute-start) | collective-permute-done | bytes 1048608 | tf_op jit(solution)/shard_map/ppermute | solution.py:74
  50.2 21.5 %collective-permute-done.6.refs_5_.refs_12_ = bf16[4,128,768]{2,1,0:T(8,128)(2,1)S(1)} collective-permute-done((bf16[4,128,768]{2,1,0:T(8,128)(2,1)S(1)}, bf16[4,128,768]{2,1,0:T(8,128)(2,1)S(1)}, u32[]{:S(2)}, u32[]{:S(2)}) %collective-permute-start.6) | collective-permute-done | bytes 786464 | tf_op jit(solution)/shard_map/ppermute | solution.py:74
  72.6 36.7 %attend_forward.2 = (bf16[2048,256]{1,0:T(8,128)(2,1)}, bf16[2048,256]{1,0:T(8,128)(2,1)}, bf16[2048,256]{1,0:T(8,128)(2,1)}, f32[2048,256]{1,0:T(8,128)}, f32[8...) custom-call(s32[4]{0:T(128)} %get-tuple-element.312.block_ref.place_, ...), custom_call_target="tpu_custom_call" | custom-call | flops 13958643712 | bytes 20971520 | tf_op jit(solution)/shard_map/attend_forward/pallas_call | solution.py:828
  115.0 9.4 %collective-permute-done.7.refs_2_ = bf16[512,256]{1,0:T(8,128)(2,1)} collective-permute-done((bf16[512,256]{1,0:T(8,128)(2,1)}, bf16[512,256]{1,0:T(8,128)(2,1)}, u32[]{:S(2)}, u32[]{:S(2)}) %collective-permute-start.7) | collective-permute-done | bytes 262176 | tf_op jit(solution)/shard_map/ppermute | solution.py:74
  124.4 9.5 %collective-permute-done.9.refs_4_ = bf16[512,256]{1,0:T(8,128)(2,1)} collective-permute-done((bf16[512,256]{1,0:T(8,128)(2,1)}, bf16[512,256]{1,0:T(8,128)(2,1)}, u32[]{:S(2)}, u32[]{:S(2)}) %collective-permute-start.9) | collective-permute-done | bytes 262176 | tf_op jit(solution)/shard_map/ppermute | solution.py:74
  133.9 39.7 %all-gather.3.cloned.1.call-done = bf16[32,128,2304]{2,1,0:T(8,128)(2,1)} async-done(((bf16[1,128,2304]{2,1,0:T(8,128)(2,1)}), bf16[32,128,2304]{2,1,0:T(8,128)(2,1)}) %all-gather.3.cloned.1.call-update) | async-done | bytes 18874384 | tf_op jit(solution)/shard_map/all_gather | solution.py:1034
  173.6 28.4 %ffn_forward.2 = (f32[512,1024]{1,0:T(8,128)}, f32[512,1024]{1,0:T(8,128)}, f32[512,1024]{1,0:T(8,128)}, bf16[512,1024]{1,0:T(8,128)(2,1)}, f32[512,128]{1,0:T(8...) custom-call(s32[4]{0:T(128)} %get-tuple-element.312.block_ref.place_, ...), custom_call_target="tpu_custom_call" | custom-call | flops 9663676416 | bytes 41943040 | tf_op jit(solution)/shard_map/ffn_forward/pallas_call | solution.py:310
  208.1 28.0 %collective-permute-done.10.refs_1_ = bf16[512,1024]{1,0:T(8,128)(2,1)S(1)} collective-permute-done((bf16[512,1024]{1,0:T(8,128)(2,1)}, bf16[512,1024]{1,0:T(8,128)(2,1)S(1)}, u32[]{:S(2)}, u32[]{:S(2)}) %collective-permute-start.10) | collective-permute-done | bytes 1048608 | tf_op jit(solution)/shard_map/ppermute | solution.py:74
  240.1 18.3 %collective-permute-done.16.refs_5_.refs_12_ = bf16[4,128,768]{2,1,0:T(8,128)(2,1)} collective-permute-done((bf16[4,128,768]{2,1,0:T(8,128)(2,1)S(1)}, bf16[4,128,768]{2,1,0:T(8,128)(2,1)}, u32[]{:S(2)}, u32[]{:S(2)}) %collective-permute-start.16) | collective-permute-done | bytes 786464 | tf_op jit(solution)/shard_map/ppermute | solution.py:74
  259.4 36.7 %attend_forward.3 = (bf16[2048,256]{1,0:T(8,128)(2,1)}, bf16[2048,256]{1,0:T(8,128)(2,1)}, bf16[2048,256]{1,0:T(8,128)(2,1)}, f32[2048,256]{1,0:T(8,128)}, f32[8...) custom-call(s32[4]{0:T(128)} %get-tuple-element.312.block_ref.place_, ...), custom_call_target="tpu_custom_call" | custom-call | flops 13958643712 | bytes 20971520 | tf_op jit(solution)/shard_map/attend_forward/pallas_call | solution.py:828
  301.6 16.4 %all-gather.5.cloned.1.call-done = bf16[32,128,2304]{2,1,0:T(8,128)(2,1)} async-done(((bf16[1,128,2304]{2,1,0:T(8,128)(2,1)}), bf16[32,128,2304]{2,1,0:T(8,128)(2,1)}) %all-gather.5.cloned.1.call-update) | async-done | bytes 18874384 | tf_op jit(solution)/shard_map/all_gather | solution.py:1034
  318.0 27.6 %ffn_forward.3 = (f32[512,1024]{1,0:T(8,128)}, f32[512,1024]{1,0:T(8,128)}, f32[512,1024]{1,0:T(8,128)}, bf16[512,1024]{1,0:T(8,128)(2,1)}, f32[512,128]{1,0:T(8...) custom-call(s32[4]{0:T(128)} %get-tuple-element.312.block_ref.place_ref, ...), custom_call_target="tpu_custom_call" | custom-call | flops 9663676416 | bytes 41943040 | tf_op jit(solution)/shard_map/ffn_forward/pallas_call | solution.py:310
  345.7 32.2 %ffn_backward.2 = (bf16[512,1024]{1,0:T(8,128)(2,1)}, f32[512,1024]{1,0:T(8,128)}, bf16[512,1024]{1,0:T(8,128)(2,1)}, bf16[512,256]{1,0:T(8,128)(2,1)}, bf16[512...) custom-call(s32[4]{0:T(128)} %get-tuple-element.312.block_ref.place_, ...), custom_call_target="tpu_custom_call" | custom-call | flops 9663676416 | bytes 46137344 | tf_op jit(solution)/shard_map/ffn_backward/pallas_call | solution.py:482
  382.5 17.9 %whole_grads.1 = bf16[8,4,128,2304]{3,2,1,0:T(8,128)(2,1)} custom-call(s32[4]{0:T(128)} %get-tuple-element.312.block_ref.place_ref, bf16[512,1024]{1,0:T(8,128)(2,1)} %get-tuple-element.134.refs_0_, bf16[512,1024]{1,0:T(8,128)(2,1)} %get-tuple-element.135.refs_1_, bf16[512,1024]{1,0:T(8,128)(2,1)} %get-tuple-element.136.refs_2_, ...), custom_call_target="tpu_custom_call" | custom-call | flops 9663676416 | bytes 31457280 | tf_op jit(solution)/shard_map/whole_grads/pallas_call | solution.py:673
  400.4 49.7 %attend_backward.2 = (bf16[2048,768]{1,0:T(8,128)(2,1)}, f32[8,128]{1,0:T(8,128)}, bf16[2,512,1024]{2,1,0:T(8,128)(2,1)}, bf16[2,512,1024]{2,1,0:T(8,128)(2,1)}) custom-call(s32[4]{0:T(128)} %get-tuple-element.312.block_ref.place_ref, s32[8]{0:T(128)} %broadcast_xor_fusion.place_ref, s32[10]{0:T(128)} %constant.44.clone.open_ref, ...), custom_call_target="tpu_custom_call" | custom-call | flops 30064771072 | bytes 16777216 | tf_op jit(solution)/shard_map/attend_backward/pallas_call | solution.py:956
  458.8 8.6 %attn_grads.2 = (bf16[4,128,768]{2,1,0:T(8,128)(2,1)}, bf16[4,128,768]{2,1,0:T(8,128)(2,1)}) custom-call(s32[8]{0:T(128)} %broadcast_xor_fusion.place_ref, bf16[512,1024]{1,0:T(8,128)(2,1)} %get-tuple-element.116.refs_0_, bf16[512,1024]{1,0:T(8,128)(2,1)} %copy-done.47, bf16[512,1024]{1,0:T(8,128)(2,1)} %copy-done.48, ...), custom_call_target="tpu_custom_call" | custom-call | flops 3221225472 | bytes 8388608 | tf_op jit(solution)/shard_map/attn_grads/pallas_call | solution.py:721
  472.5 14.8 %collective-permute-done.25 = bf16[4,128,768]{2,1,0:T(8,128)(2,1)S(1)} collective-permute-done((bf16[4,128,768]{2,1,0:T(8,128)(2,1)}, bf16[4,128,768]{2,1,0:T(8,128)(2,1)S(1)}, u32[]{:S(2)}, u32[]{:S(2)}) %collective-permute-start.25) | collective-permute-done | bytes 786464 | tf_op jit(solution)/shard_map/ppermute | solution.py:74
  494.8 11.3 %down_grads.1 = (bf16[2,2,4,128,1024]{4,3,2,1,0:T(8,128)(2,1)}, bf16[2,2,4,128,1024]{4,3,2,1,0:T(8,128)(2,1)}) custom-call(s32[8]{0:T(128)} %broadcast_xor_fusion.place_ref, f32[512,1024]{1,0:T(8,128)} %multiply_add_fusion.1.refs_0_, bf16[4,512,1024]{2,1,0:T(8,128)(2,1)} %get-tuple-element.153.refs_1_), custom_call_target="tpu_custom_call" | custom-call | flops 4294967296 | bytes 16777216 | tf_op jit(solution)/shard_map/down_grads/pallas_call | solution.py:598
  506.2 33.0 %ffn_backward.3 = (bf16[512,1024]{1,0:T(8,128)(2,1)}, f32[512,1024]{1,0:T(8,128)}, bf16[512,1024]{1,0:T(8,128)(2,1)}, bf16[512,256]{1,0:T(8,128)(2,1)}, bf16[512...) custom-call(s32[4]{0:T(128)} %get-tuple-element.312.block_ref.place_, ...), custom_call_target="tpu_custom_call" | custom-call | flops 9663676416 | bytes 46137344 | tf_op jit(solution)/shard_map/ffn_backward/pallas_call | solution.py:482
  539.2 13.0 %up_grads.1 = (bf16[2,2,4,128,1280]{4,3,2,1,0:T(8,128)(2,1)}, bf16[2,2,4,128,1280]{4,3,2,1,0:T(8,128)(2,1)}) custom-call(s32[8]{0:T(128)} %broadcast_xor_fusion.place_ref, bf16[512,1024]{1,0:T(8,128)(2,1)} %get-tuple-element.167.refs_0_, bf16[512,1024]{1,0:T(8,128)(2,1)} %get-tuple-element.168.refs_1_, bf16[4,512,1024]{2,1,0:T(8,128)(2,1)} %get-tuple-element.169.refs_2_, ...), custom_call_target="tpu_custom_call" | custom-call | flops 5368709120 | bytes 16777216 | tf_op jit(solution)/shard_map/up_grads/pallas_call | solution.py:598
  560.6 13.1 %collective-permute-done.31 = bf16[2,128,768]{2,1,0:T(8,128)(2,1)S(1)} collective-permute-done((bf16[2,128,768]{2,1,0:T(8,128)(2,1)S(1)}, bf16[2,128,768]{2,1,0:T(8,128)(2,1)S(1)}, u32[]{:S(2)}, u32[]{:S(2)}) %collective-permute-start.31) | collective-permute-done | bytes 393248 | tf_op jit(solution)/shard_map/ppermute | solution.py:74
  578.3 7.5 collective-permute-done.32
  587.7 6.3 add_convert_fusion.2
  602.2 49.8 %attend_backward.3 = (bf16[2048,768]{1,0:T(8,128)(2,1)}, f32[8,128]{1,0:T(8,128)}, bf16[2,512,1024]{2,1,0:T(8,128)(2,1)}, bf16[2,512,1024]{2,1,0:T(8,128)(2,1)}) custom-call(s32[4]{0:T(128)} %get-tuple-element.312.block_ref.place_ref, s32[8]{0:T(128)} %broadcast_xor_fusion.place_ref, s32[10]{0:T(128)} %constant.44.clone.open_ref, ...), custom_call_target="tpu_custom_call" | custom-call | flops 30064771072 | bytes 16777216 | tf_op jit(solution)/shard_map/attend_backward/pallas_call | solution.py:956
  652.0 5.2 collective-permute-done.34
  657.2 23.6 %collective-permute-done.33 = bf16[1,2,4,128,1280]{4,3,2,1,0:T(8,128)(2,1)} collective-permute-done((bf16[1,2,4,128,1280]{4,3,2,1,0:T(8,128)(2,1)}, bf16[1,2,4,128,1280]{4,3,2,1,0:T(8,128)(2,1)}, u32[]{:S(2)}, u32[]{:S(2)}) %collective-permute-start.33) | collective-permute-done | bytes 2621472 | tf_op jit(solution)/shard_map/ppermute | solution.py:74
  686.0 8.0 attn_grads.3
  701.3 13.6 %collective-permute-done.42 = bf16[4,128,768]{2,1,0:T(8,128)(2,1)} collective-permute-done((bf16[4,128,768]{2,1,0:T(8,128)(2,1)}, bf16[4,128,768]{2,1,0:T(8,128)(2,1)}, u32[]{:S(2)}, u32[]{:S(2)}) %collective-permute-start.42) | collective-permute-done | bytes 786464 | tf_op jit(solution)/shard_map/ppermute | solution.py:74
  720.4 10.1 %collective-permute-done.43 = bf16[2,128,768]{2,1,0:T(8,128)(2,1)S(1)} collective-permute-done((bf16[2,128,768]{2,1,0:T(8,128)(2,1)S(1)}, bf16[2,128,768]{2,1,0:T(8,128)(2,1)S(1)}, u32[]{:S(2)}, u32[]{:S(2)}) %collective-permute-start.43) | collective-permute-done | bytes 393248 | tf_op jit(solution)/shard_map/ppermute | solution.py:74
  731.2 10.2 %collective-permute-done.45 = bf16[1,4,128,1280]{3,2,1,0:T(8,128)(2,1)} collective-permute-done((bf16[1,4,128,1280]{3,2,1,0:T(8,128)(2,1)}, bf16[1,4,128,1280]{3,2,1,0:T(8,128)(2,1)}, u32[]{:S(2)}, u32[]{:S(2)}) %collective-permute-start.45) | collective-permute-done | bytes 1310752 | tf_op jit(solution)/shard_map/ppermute | solution.py:74
  749.2 14.6 %collective-permute-done.46 = bf16[2,128,1280]{2,1,0:T(8,128)(2,1)S(1)} collective-permute-done((bf16[2,128,1280]{2,1,0:T(8,128)(2,1)S(1)}, bf16[2,128,1280]{2,1,0:T(8,128)(2,1)S(1)}, u32[]{:S(2)}, u32[]{:S(2)}) %collective-permute-start.46) | collective-permute-done | bytes 655392 | tf_op jit(solution)/shard_map/ppermute | solution.py:74
  766.9 12.4 %collective-permute-done.47 = bf16[1,128,1280]{2,1,0:T(8,128)(2,1)S(1)} collective-permute-done((bf16[1,128,1280]{2,1,0:T(8,128)(2,1)S(1)}, bf16[1,128,1280]{2,1,0:T(8,128)(2,1)S(1)}, u32[]{:S(2)}, u32[]{:S(2)}) %collective-permute-start.47) | collective-permute-done | bytes 327712 | tf_op jit(solution)/shard_map/ppermute | solution.py:74
  (344 shorter events, 153.3 us)
Async XLA Ops:
  7.2 166.4 %all-gather.3.cloned.1.call-start = ((), (), s32[]{:S(2)}) async-start(), calls=%async_computation.1 | async-start | bytes 19464192 | tf_op jit(solution)/shard_map/all_gather | solution.py:1034
  11.1 306.9 %all-gather.5.cloned.1.call-start = ((), (), s32[]{:S(2)}) async-start(), calls=%async_computation.2 | async-start | bytes 19464192 | tf_op jit(solution)/shard_map/all_gather | solution.py:1034
  12.1 794.1 %reduce-scatter.2.cloned.1.call-start = ((), (), s32[]{:S(2)}) async-start(), calls=%async_computation.3 | async-start | bytes 19464192 | tf_op jit(solution)/shard_map/reduce_scatter | solution.py:1103
  13.7 30.5 %collective-permute-start = (bf16[512,1024]{1,0:T(8,128)(2,1)S(1)}, bf16[512,1024]{1,0:T(8,128)(2,1)}, u32[]{:S(2)}, u32[]{:S(2)}) collective-permute-start(bf16[512,1024]{1,0:T(8,128)(2,1)S(1)} %multiply_convert_fusion.refs_0_), channel_id=1, source_target_pairs={{0,2},{1,3},{2,0},{3,1},{4,6},{5,7},{6,4},{7,5},{8,10},{9,11},{10,... | collective-permute-start | bytes 3145736 | tf_op jit(solution)/shard_map/ppermute | solution.py:74
  18.2 26.1 %collective-permute-start.3 = (bf16[128,768]{1,0:T(8,128)(2,1)S(1)}, bf16[128,768]{1,0:T(8,128)(2,1)S(1)}, u32[]{:S(2)}, u32[]{:S(2)}) collective-permute-start(bf16[128,768]{1,0:T(8,128)(2,1)S(1)} %pad_maximum_fusion.12), channel_id=1, source_target_pairs={{0,16},{4,20},{8,24},{12,28},{16,0},{20,4},{24,8},{28,12},{1,17},{... | collective-permute-start | bytes 589832 | tf_op jit(solution)/shard_map/ppermute | solution.py:74
  20.8 23.5 %collective-permute-start.4 = (bf16[128,768]{1,0:T(8,128)(2,1)S(1)}, bf16[128,768]{1,0:T(8,128)(2,1)S(1)}, u32[]{:S(2)}, u32[]{:S(2)}) collective-permute-start(bf16[128,768]{1,0:T(8,128)(2,1)S(1)} %pad_maximum_fusion.12), channel_id=1, source_target_pairs={{0,8},{4,12},{8,0},{12,4},{16,24},{20,28},{24,16},{28,20},{1,9},{5... | collective-permute-start | bytes 589832 | tf_op jit(solution)/shard_map/ppermute | solution.py:74
  22.4 21.9 %collective-permute-start.5 = (bf16[128,768]{1,0:T(8,128)(2,1)S(1)}, bf16[128,768]{1,0:T(8,128)(2,1)S(1)}, u32[]{:S(2)}, u32[]{:S(2)}) collective-permute-start(bf16[128,768]{1,0:T(8,128)(2,1)S(1)} %pad_maximum_fusion.12), channel_id=1, source_target_pairs={{0,24},{4,28},{8,16},{12,20},{16,8},{20,12},{24,0},{28,4},{1,25},{... | collective-permute-start | bytes 589832 | tf_op jit(solution)/shard_map/ppermute | solution.py:74
  22.6 49.1 %collective-permute-start.1 = (bf16[512,1024]{1,0:T(8,128)(2,1)S(1)}, bf16[512,1024]{1,0:T(8,128)(2,1)}, u32[]{:S(2)}, u32[]{:S(2)}) collective-permute-start(bf16[512,1024]{1,0:T(8,128)(2,1)S(1)} %multiply_convert_fusion.refs_0_), channel_id=1, source_target_pairs={{0,1},{1,0},{2,3},{3,2},{4,5},{5,4},{6,7},{7,6},{8,9},{9,8},{10,11... | collective-permute-start | bytes 3145736 | tf_op jit(solution)/shard_map/ppermute | solution.py:74
  44.3 27.5 %collective-permute-start.2 = (bf16[512,1024]{1,0:T(8,128)(2,1)}, bf16[512,1024]{1,0:T(8,128)(2,1)}, u32[]{:S(2)}, u32[]{:S(2)}) collective-permute-start(bf16[512,1024]{1,0:T(8,128)(2,1)} %collective-permute-done.refs_1_), channel_id=1, source_target_pairs={{0,1},{1,0},{2,3},{3,2},{4,5},{5,4},{6,7},{7,6},{8,9},{9,8},{10,11... | collective-permute-start | bytes 3145736 | tf_op jit(solution)/shard_map/ppermute | solution.py:74
  44.4 27.4 %collective-permute-start.6 = (bf16[4,128,768]{2,1,0:T(8,128)(2,1)S(1)}, bf16[4,128,768]{2,1,0:T(8,128)(2,1)S(1)}, u32[]{:S(2)}, u32[]{:S(2)}) collective-permute-start(bf16[4,128,768]{2,1,0:T(8,128)(2,1)S(1)} %pad_maximum_fusion.4.refs_4_.refs_11_), channel_id=1, source_target_pairs={{0,4},{4,0},{8,12},{12,8},{16,20},{20,16},{24,28},{28,24},{1,5},{5... | collective-permute-start | bytes 2359304 | tf_op jit(solution)/shard_map/ppermute | solution.py:74
  110.7 23.2 %collective-permute-start.9 = (bf16[512,256]{1,0:T(8,128)(2,1)}, bf16[512,256]{1,0:T(8,128)(2,1)}, u32[]{:S(2)}, u32[]{:S(2)}) collective-permute-start(bf16[512,256]{1,0:T(8,128)(2,1)} %get-tuple-element.114), channel_id=1, source_target_pairs={{0,3},{1,2},{2,1},{3,0},{4,7},{5,6},{6,5},{7,4},{8,11},{9,10},{10,... | collective-permute-start | bytes 786440 | tf_op jit(solution)/shard_map/ppermute | solution.py:74
  202.1 34.0 %collective-permute-start.10 = (bf16[512,1024]{1,0:T(8,128)(2,1)}, bf16[512,1024]{1,0:T(8,128)(2,1)S(1)}, u32[]{:S(2)}, u32[]{:S(2)}) collective-permute-start(bf16[512,1024]{1,0:T(8,128)(2,1)} %get-tuple-element.116.refs_0_), channel_id=1, source_target_pairs={{0,2},{1,3},{2,0},{3,1},{4,6},{5,7},{6,4},{7,5},{8,10},{9,11},{10,... | collective-permute-start | bytes 3145736 | tf_op jit(solution)/shard_map/ppermute | solution.py:74
  203.6 32.5 %collective-permute-start.13 = (bf16[128,768]{1,0:T(8,128)(2,1)S(1)}, bf16[128,768]{1,0:T(8,128)(2,1)S(1)}, u32[]{:S(2)}, u32[]{:S(2)}) collective-permute-start(bf16[128,768]{1,0:T(8,128)(2,1)S(1)} %pad_maximum_fusion.13), channel_id=1, source_target_pairs={{0,16},{4,20},{8,24},{12,28},{16,0},{20,4},{24,8},{28,12},{1,17},{... | collective-permute-start | bytes 589832 | tf_op jit(solution)/shard_map/ppermute | solution.py:74
  205.2 30.9 %collective-permute-start.14 = (bf16[128,768]{1,0:T(8,128)(2,1)S(1)}, bf16[128,768]{1,0:T(8,128)(2,1)S(1)}, u32[]{:S(2)}, u32[]{:S(2)}) collective-permute-start(bf16[128,768]{1,0:T(8,128)(2,1)S(1)} %pad_maximum_fusion.13), channel_id=1, source_target_pairs={{0,8},{4,12},{8,0},{12,4},{16,24},{20,28},{24,16},{28,20},{1,9},{5... | collective-permute-start | bytes 589832 | tf_op jit(solution)/shard_map/ppermute | solution.py:74
  205.7 30.5 %collective-permute-start.15 = (bf16[128,768]{1,0:T(8,128)(2,1)S(1)}, bf16[128,768]{1,0:T(8,128)(2,1)S(1)}, u32[]{:S(2)}, u32[]{:S(2)}) collective-permute-start(bf16[128,768]{1,0:T(8,128)(2,1)S(1)} %pad_maximum_fusion.13), channel_id=1, source_target_pairs={{0,24},{4,28},{8,16},{12,20},{16,8},{20,12},{24,0},{28,4},{1,25},{... | collective-permute-start | bytes 589832 | tf_op jit(solution)/shard_map/ppermute | solution.py:74
  208.1 50.4 %collective-permute-start.11 = (bf16[512,1024]{1,0:T(8,128)(2,1)}, bf16[512,1024]{1,0:T(8,128)(2,1)S(1)}, u32[]{:S(2)}, u32[]{:S(2)}) collective-permute-start(bf16[512,1024]{1,0:T(8,128)(2,1)} %get-tuple-element.116.refs_0_), channel_id=1, source_target_pairs={{0,1},{1,0},{2,3},{3,2},{4,5},{5,4},{6,7},{7,6},{8,9},{9,8},{10,11... | collective-permute-start | bytes 3145736 | tf_op jit(solution)/shard_map/ppermute | solution.py:74
  236.1 23.3 %collective-permute-start.12 = (bf16[512,1024]{1,0:T(8,128)(2,1)S(1)}, bf16[512,1024]{1,0:T(8,128)(2,1)}, u32[]{:S(2)}, u32[]{:S(2)}) collective-permute-start(bf16[512,1024]{1,0:T(8,128)(2,1)S(1)} %collective-permute-done.10.refs_1_), channel_id=1, source_target_pairs={{0,1},{1,0},{2,3},{3,2},{4,5},{5,4},{6,7},{7,6},{8,9},{9,8},{10,11... | collective-permute-start | bytes 3145736 | tf_op jit(solution)/shard_map/ppermute | solution.py:74
  296.1 21.9 %collective-permute-start.17 = (bf16[512,256]{1,0:T(8,128)(2,1)}, bf16[512,256]{1,0:T(8,128)(2,1)}, u32[]{:S(2)}, u32[]{:S(2)}) collective-permute-start(bf16[512,256]{1,0:T(8,128)(2,1)} %get-tuple-element.120), channel_id=1, source_target_pairs={{0,2},{1,3},{2,0},{3,1},{4,6},{5,7},{6,4},{7,5},{8,10},{9,11},{10,... | collective-permute-start | bytes 786440 | tf_op jit(solution)/shard_map/ppermute | solution.py:74
  296.2 21.9 %collective-permute-start.18 = (bf16[512,256]{1,0:T(8,128)(2,1)}, bf16[512,256]{1,0:T(8,128)(2,1)}, u32[]{:S(2)}, u32[]{:S(2)}) collective-permute-start(bf16[512,256]{1,0:T(8,128)(2,1)} %get-tuple-element.121), channel_id=1, source_target_pairs={{0,1},{1,0},{2,3},{3,2},{4,5},{5,4},{6,7},{7,6},{8,9},{9,8},{10,11... | collective-permute-start | bytes 786440 | tf_op jit(solution)/shard_map/ppermute | solution.py:74
  296.2 21.8 %collective-permute-start.19 = (bf16[512,256]{1,0:T(8,128)(2,1)}, bf16[512,256]{1,0:T(8,128)(2,1)}, u32[]{:S(2)}, u32[]{:S(2)}) collective-permute-start(bf16[512,256]{1,0:T(8,128)(2,1)} %get-tuple-element.122), channel_id=1, source_target_pairs={{0,3},{1,2},{2,1},{3,0},{4,7},{5,6},{6,5},{7,4},{8,11},{9,10},{10,... | collective-permute-start | bytes 786440 | tf_op jit(solution)/shard_map/ppermute | solution.py:74
  377.9 22.5 %collective-permute-start.20 = (bf16[512,256]{1,0:T(8,128)(2,1)}, bf16[512,256]{1,0:T(8,128)(2,1)}, u32[]{:S(2)}, u32[]{:S(2)}) collective-permute-start(bf16[512,256]{1,0:T(8,128)(2,1)} %get-tuple-element.131), channel_id=1, source_target_pairs={{0,2},{1,3},{2,0},{3,1},{4,6},{5,7},{6,4},{7,5},{8,10},{9,11},{10,... | collective-permute-start | bytes 786440 | tf_op jit(solution)/shard_map/ppermute | solution.py:74
  457.2 30.1 %collective-permute-start.24 = (bf16[1,512,1024]{2,1,0:T(8,128)(2,1)}, bf16[1,512,1024]{2,1,0:T(8,128)(2,1)}, u32[]{:S(2)}, u32[]{:S(2)}) collective-permute-start(bf16[1,512,1024]{2,1,0:T(8,128)(2,1)} %add_convert_fusion.10), channel_id=1, source_target_pairs={{0,2},{1,3},{2,0},{3,1},{4,6},{5,7},{6,4},{7,5},{8,10},{9,11},{10,... | collective-permute-start | bytes 3145736 | tf_op jit(solution)/shard_map/ppermute | solution.py:74
  552.3 41.8 %collective-permute-start.29 = (bf16[2,2,4,128,1280]{4,3,2,1,0:T(8,128)(2,1)}, bf16[2,2,4,128,1280]{4,3,2,1,0:T(8,128)(2,1)}, u32[]{:S(2)}, u32[]{:S(2)}) collective-permute-start(bf16[2,2,4,128,1280]{4,3,2,1,0:T(8,128)(2,1)} %get-tuple-element.171), channel_id=1, source_target_pairs={{0,1},{1,0},{2,3},{3,2},{4,5},{5,4},{6,7},{7,6},{8,9},{9,8},{10,11... | collective-permute-start | bytes 15728648 | tf_op jit(solution)/shard_map/ppermute | solution.py:74
  552.3 35.4 %collective-permute-start.30 = (bf16[2,2,4,128,1024]{4,3,2,1,0:T(8,128)(2,1)}, bf16[2,2,4,128,1024]{4,3,2,1,0:T(8,128)(2,1)}, u32[]{:S(2)}, u32[]{:S(2)}) collective-permute-start(bf16[2,2,4,128,1024]{4,3,2,1,0:T(8,128)(2,1)} %get-tuple-element.173), channel_id=1, source_target_pairs={{0,1},{1,0},{2,3},{3,2},{4,5},{5,4},{6,7},{7,6},{8,9},{9,8},{10,11... | collective-permute-start | bytes 12582920 | tf_op jit(solution)/shard_map/ppermute | solution.py:74
  577.1 21.7 %collective-permute-start.26 = (bf16[512,256]{1,0:T(8,128)(2,1)S(1)}, bf16[512,256]{1,0:T(8,128)(2,1)S(1)}, u32[]{:S(2)}, u32[]{:S(2)}) collective-permute-start(bf16[512,256]{1,0:T(8,128)(2,1)S(1)} %copy-done.52), channel_id=1, source_target_pairs={{0,2},{1,3},{2,0},{3,1},{4,6},{5,7},{6,4},{7,5},{8,10},{9,11},{10,... | collective-permute-start | bytes 786440 | tf_op jit(solution)/shard_map/ppermute | solution.py:74
  600.2 80.6 %collective-permute-start.33 = (bf16[1,2,4,128,1280]{4,3,2,1,0:T(8,128)(2,1)}, bf16[1,2,4,128,1280]{4,3,2,1,0:T(8,128)(2,1)}, u32[]{:S(2)}, u32[]{:S(2)}) collective-permute-start(bf16[1,2,4,128,1280]{4,3,2,1,0:T(8,128)(2,1)} %get-tuple-element.187), channel_id=1, source_target_pairs={{0,2},{1,3},{2,0},{3,1},{4,6},{5,7},{6,4},{7,5},{8,10},{9,11},{10,... | collective-permute-start | bytes 7864328 | tf_op jit(solution)/shard_map/ppermute | solution.py:74
  600.8 56.5 %collective-permute-start.34 = (bf16[1,2,4,128,1024]{4,3,2,1,0:T(8,128)(2,1)}, bf16[1,2,4,128,1024]{4,3,2,1,0:T(8,128)(2,1)}, u32[]{:S(2)}, u32[]{:S(2)}) collective-permute-start(bf16[1,2,4,128,1024]{4,3,2,1,0:T(8,128)(2,1)} %get-tuple-element.188), channel_id=1, source_target_pairs={{0,4},{4,0},{8,12},{12,8},{16,20},{20,16},{24,28},{28,24},{1,5},{5... | collective-permute-start | bytes 6291464 | tf_op jit(solution)/shard_map/ppermute | solution.py:74
  685.4 31.5 %collective-permute-start.48 = (bf16[1,4,128,1024]{3,2,1,0:T(8,128)(2,1)}, bf16[1,4,128,1024]{3,2,1,0:T(8,128)(2,1)}, u32[]{:S(2)}, u32[]{:S(2)}) collective-permute-start(bf16[1,4,128,1024]{3,2,1,0:T(8,128)(2,1)} %get-tuple-element.267), channel_id=1, source_target_pairs={{0,2},{1,3},{2,0},{3,1},{4,6},{5,7},{6,4},{7,5},{8,10},{9,11},{10,... | collective-permute-start | bytes 3145736 | tf_op jit(solution)/shard_map/ppermute | solution.py:74
  699.9 41.5 %collective-permute-start.45 = (bf16[1,4,128,1280]{3,2,1,0:T(8,128)(2,1)}, bf16[1,4,128,1280]{3,2,1,0:T(8,128)(2,1)}, u32[]{:S(2)}, u32[]{:S(2)}) collective-permute-start(bf16[1,4,128,1280]{3,2,1,0:T(8,128)(2,1)} %get-tuple-element.265), channel_id=1, source_target_pairs={{0,4},{4,0},{8,12},{12,8},{16,20},{20,16},{24,28},{28,24},{1,5},{5... | collective-permute-start | bytes 3932168 | tf_op jit(solution)/shard_map/ppermute | solution.py:74
  701.3 47.0 %collective-permute-start.35 = (bf16[2,512,1024]{2,1,0:T(8,128)(2,1)}, bf16[2,512,1024]{2,1,0:T(8,128)(2,1)S(1)}, u32[]{:S(2)}, u32[]{:S(2)}) collective-permute-start(bf16[2,512,1024]{2,1,0:T(8,128)(2,1)} %get-tuple-element.189), channel_id=1, source_target_pairs={{0,1},{1,0},{2,3},{3,2},{4,5},{5,4},{6,7},{7,6},{8,9},{9,8},{10,11... | collective-permute-start | bytes 6291464 | tf_op jit(solution)/shard_map/ppermute | solution.py:74
  718.5 26.2 %collective-permute-start.49 = (bf16[2,128,1024]{2,1,0:T(8,128)(2,1)S(1)}, bf16[2,128,1024]{2,1,0:T(8,128)(2,1)S(1)}, u32[]{:S(2)}, u32[]{:S(2)}) collective-permute-start(bf16[2,128,1024]{2,1,0:T(8,128)(2,1)S(1)} %get-tuple-element.271), channel_id=1, source_target_pairs={{0,8},{4,12},{8,0},{12,4},{16,24},{20,28},{24,16},{28,20},{1,9},{5... | collective-permute-start | bytes 1572872 | tf_op jit(solution)/shard_map/ppermute | solution.py:74
  748.6 31.6 %collective-permute-start.36 = (bf16[1,512,1024]{2,1,0:T(8,128)(2,1)S(1)}, bf16[1,512,1024]{2,1,0:T(8,128)(2,1)S(1)}, u32[]{:S(2)}, u32[]{:S(2)}) collective-permute-start(bf16[1,512,1024]{2,1,0:T(8,128)(2,1)S(1)} %add_convert_fusion.8), channel_id=1, source_target_pairs={{0,2},{1,3},{2,0},{3,1},{4,6},{5,7},{6,4},{7,5},{8,10},{9,11},{10,... | collective-permute-start | bytes 3145736 | tf_op jit(solution)/shard_map/ppermute | solution.py:74
  (81 other events, 1175.0 us)
Sparse Core Ops, SparseCore 0:
  11.5 162.0 all-gather.2
  176.5 141.4 all-gather.4
  450.3 239.8 reduce-scatter.1

commit v3 on v2

--- a/solution.py
+++ b/solution.py
@@ -129,11 +129,15 @@
     return add_low(kept[:half], arrived[:half]), add_low(kept[half:], arrived[half:])
 
 
+def split_add(kept, arrived):
+    while kept.shape[0] == 1:
+        kept, arrived = kept[0], arrived[0]
+    return add_halves(kept, arrived)
+
+
 def scatter_rest(kept, arrived, hops):
     for hop in hops:
-        if kept.shape[0] == 1:
-            kept, arrived = kept[0], arrived[0]
-        kept, sent = add_halves(kept, arrived)
+        kept, sent = split_add(kept, arrived)
         arrived = swap(sent, *hop)
     total = kept.astype(F32) + arrived.astype(F32)
     return total.reshape(total.shape[-2:])
@@ -1047,9 +1051,6 @@
     saved = []
     for layer in range(LAYERS):
         last = layer == LAYERS - 1
-        if layer > 0:
-            shard, _ = lax.optimization_barrier((attn_shards[layer], logsum))
-            attn_set.append(gather_near(gather_far(shard, places), places))
         h_parts = gather_tensor([h_attn], tensor_masks)
         scale_all = head_scale[layer].reshape(tensor_size, local_heads)
         scale_rel = jnp.repeat(scale_all[places.tensor_places], HD, axis=1)
@@ -1057,6 +1058,11 @@
             places, h_parts, attn_set[layer], seg_column, seg_row, scale_rel[:1]
         )
         a_parts = exchange(a_parts)
+        if not last:
+            shard, _ = lax.optimization_barrier((attn_shards[layer + 1], h_parts))
+            pieces = gather_near(gather_far(shard, places), places)
+            a_parts, pieces = lax.optimization_barrier((a_parts, pieces))
+            attn_set.append(pieces)
         gain_mid = ln_mid_gain[layer].reshape(tensor_size, -1)[places.tensor_places]
         stream_in = stream
         attn_out, middle, stream, h_ffn, mean, factor, pre, h_mid, *h_next = ffn_forward(
@@ -1093,6 +1099,11 @@
             places, grad_stream, attn_out, middle, mean, factor, pre, matrix_set[layer],
             ln_post_gain[layer], ln_ffn_gain[layer], gain_mid, scale_rel,
         )
+        if layer == 0:
+            rest, down_arrived, above = lax.optimization_barrier(
+                (rest, down_arrived, matrix_grads[1][:3])
+            )
+            matrix_grads[1] = above + matrix_grads[1][3:]
         dout_parts = exchange(rest[:tensor_size])
         grad_pre, mid_sum, ffn_sum, post_sum = rest[tensor_size:]
         wide = h_mid.shape[2]
@@ -1109,10 +1120,7 @@
             up_keep, up_send = up_grads(places, h_ffn, grad_out, grad_pre, a_parts)
             ups = add_halves(up_keep, swap(up_send, *core_hop))
             downs = add_halves(down_keep, down_arrived)
-            dout_parts, ups, downs, above = lax.optimization_barrier(
-                (dout_parts, ups, downs, matrix_grads[1][:3])
-            )
-            matrix_grads[1] = above + matrix_grads[1][3:]
+            dout_parts, ups, downs = lax.optimization_barrier((dout_parts, ups, downs))
             side_arrived = swap(ups[1], *side_hops[0])
             near_arrived = swap(downs[1], *near_hop)
         packed, inner_sum, keep, send = attend_backward(
@@ -1120,11 +1128,15 @@
             attn_set[layer],
         )
         if layer == 0:
-            packed, send, side_arrived, near_arrived = lax.optimization_barrier(
-                (packed, send, side_arrived, near_arrived)
+            send, side_arrived, near_arrived = lax.optimization_barrier(
+                (send, side_arrived, near_arrived)
             )
+            ups = split_add(ups[0], side_arrived)
+            downs = split_add(downs[0], near_arrived)
         grad_head = jnp.sum(inner_sum[:local_heads], 1) / scale_rel[0, ::HD]
         arrived = swap(send, *core_hop)
+        if layer == 0:
+            packed, arrived, ups, downs = lax.optimization_barrier((packed, arrived, ups, downs))
         for hop in side_hops:
             keep, send = add_halves(keep, arrived)
             arrived = swap(send, *hop)
@@ -1141,9 +1153,10 @@
         attn_rows = scatter_rest(attn_keep, attn_arrived, places.far_hops)
         if layer == 0:
             hops = side_hops[1:] + [near_hop] + places.far_hops
-            upper_rows = scatter_rest(ups[0], side_arrived, hops)
+            upper_rows = scatter_rest(ups[0], swap(ups[1], *hops[0]), hops[1:])
             up_rows, out_rows = upper_rows[:, :wide], upper_rows[:, wide:]
-            down_rows = scatter_rest(downs[0], near_arrived, side_hops + places.far_hops)
+            hops = side_hops + places.far_hops
+            down_rows = scatter_rest(downs[0], swap(downs[1], *hops[0]), hops[1:])
         matrix_grads[layer] = (
             attn_rows[:, :width],
             attn_rows[:, width : 2 * width],

time: 826 us -> 818 us (level)
  waiting for transfers between devices: 305 us -> 270 us
  other arithmetic: 63.3 us -> 82.1 us
  starting transfers between devices: 50.8 us -> 61.5 us
    ppermute x51, waiting for transfers between devices: 248 us -> 226 us  [swap(): return lax.ppermute(array, axis, [(i, i ^ mask) for i in range(size)])]
    all_gather x2, waiting for transfers between devices: 56.2 us -> 44.3 us  [local(): whole = lax.all_gather(packed, ('dp', 'tensor'), axis=0, tiled=False)]
    ppermute x51, starting transfers between devices: 50.7 us -> 61.4 us  [swap(): return lax.ppermute(array, axis, [(i, i ^ mask) for i in range(size)])]
  transfers between devices with their start and end apart: 54 -> 54, of which waited for: 23 -> 27; matrix products, arithmetic and copies ran while one was open for 10% -> 12% of each run, Pallas kernels for 30% -> 30%
where the time goes in v3:
time: 818 us; the launch traced here: 809 us
  Pallas kernels  353 us (43%)
  waiting for transfers between devices  270 us (33%)
  other arithmetic  82.1 us (10%)
  starting transfers between devices  61.5 us (8%)
  local copies, waits for them, and re-layouts  27.5 us (3%)
  between operations  14.8 us (2%)
    ppermute x51, waiting for transfers between devices, swap(): return lax.ppermute(array, axis, [(i, i ^ mask) for i in range(size)])  226 us
    pallas_call x2, Pallas kernels, attend_backward(): pl.pallas_call(backward_kernel, in_specs=[scalars] * 4 + [whole] * (parts...  100 us
    pallas_call x2, Pallas kernels, attend_forward(): pl.pallas_call(forward_kernel, in_specs=[pl.BlockSpec(memory_space=pltpu....  73.3 us
    pallas_call x2, Pallas kernels, ffn_backward(): pl.pallas_call(functools.partial(ffn_backward_kernel, parts), in_specs=[p...  64.5 us
    ppermute x51, starting transfers between devices, swap(): return lax.ppermute(array, axis, [(i, i ^ mask) for i in range(size)])  61.4 us
    pallas_call x2, Pallas kernels, ffn_forward(): pl.pallas_call(functools.partial(ffn_forward_kernel, parts, last), in_spe...  56.4 us
    all_gather x2, waiting for transfers between devices, local(): whole = lax.all_gather(packed, ('dp', 'tensor'), axis=0, tiled=False)  44.3 us
    convert_element_type x14, other arithmetic, add_low(): return (kept.astype(F32) + arrived.astype(F32)).astype(BF16)  33.5 us
  transfers between devices with their start and end apart: 54, of which 27 were waited for; matrix products, arithmetic and copies ran while one was open for 12% of the time, Pallas kernels for 30%

profile of v3, /device:TPU:0, one launch (start us, length us, event | category | flops | bytes accessed | tf_op | source)
XLA Modules:
  0.0 808.7 jit_solution(16775496667884621652)
XLA Ops:
  16.3 27.4 %collective-permute-done.refs_1_ = bf16[512,1024]{1,0:T(8,128)(2,1)} collective-permute-done((bf16[512,1024]{1,0:T(8,128)(2,1)S(1)}, bf16[512,1024]{1,0:T(8,128)(2,1)}, u32[]{:S(2)}, u32[]{:S(2)}) %collective-permute-start) | collective-permute-done | bytes 1048608 | tf_op jit(solution)/shard_map/ppermute | solution.py:74
  49.0 14.3 %collective-permute-done.3 = bf16[128,768]{1,0:T(8,128)(2,1)S(1)} collective-permute-done((bf16[128,768]{1,0:T(8,128)(2,1)S(1)}, bf16[128,768]{1,0:T(8,128)(2,1)S(1)}, u32[]{:S(2)}, u32[]{:S(2)}) %collective-permute-start.3) | collective-permute-done | bytes 196640 | tf_op jit(solution)/shard_map/ppermute | solution.py:74
  65.6 7.0 collective-permute-done.5
  76.6 15.0 %collective-permute-start.10 = (bf16[128,768]{1,0:T(8,128)(2,1)S(1)}, bf16[128,768]{1,0:T(8,128)(2,1)S(1)}, u32[]{:S(2)}, u32[]{:S(2)}) collective-permute-start(bf16[128,768]{1,0:T(8,128)(2,1)S(1)} %pad_maximum_fusion.13), channel_id=1, source_target_pairs={{0,16},{4,20},{8,24},{12,28},{16,0},{20,4},{24,8},{28,12},{1,17},{... | collective-permute-start | bytes 589832 | tf_op jit(solution)/shard_map/ppermute | solution.py:74
  93.7 8.6 %collective-permute-done.10 = bf16[128,768]{1,0:T(8,128)(2,1)S(1)} collective-permute-done((bf16[128,768]{1,0:T(8,128)(2,1)S(1)}, bf16[128,768]{1,0:T(8,128)(2,1)S(1)}, u32[]{:S(2)}, u32[]{:S(2)}) %collective-permute-start.10) | collective-permute-done | bytes 196640 | tf_op jit(solution)/shard_map/ppermute | solution.py:74
  102.3 5.7 collective-permute-done.11
  109.1 36.7 %attend_forward.2 = (bf16[2048,256]{1,0:T(8,128)(2,1)}, bf16[2048,256]{1,0:T(8,128)(2,1)}, bf16[2048,256]{1,0:T(8,128)(2,1)}, f32[2048,256]{1,0:T(8,128)}, f32[8...) custom-call(s32[4]{0:T(128)} %get-tuple-element.352.block_ref.place_, ...), custom_call_target="tpu_custom_call" | custom-call | flops 13958643712 | bytes 20971520 | tf_op jit(solution)/shard_map/attend_forward/pallas_call | solution.py:832
  157.1 21.6 %all-gather.3.cloned.1.call-done = bf16[32,128,2304]{2,1,0:T(8,128)(2,1)} async-done(((bf16[1,128,2304]{2,1,0:T(8,128)(2,1)}), bf16[32,128,2304]{2,1,0:T(8,128)(2,1)}) %all-gather.3.cloned.1.call-update) | async-done | bytes 18874384 | tf_op jit(solution)/shard_map/all_gather | solution.py:1038
  178.7 28.6 %ffn_forward.2 = (f32[512,1024]{1,0:T(8,128)}, f32[512,1024]{1,0:T(8,128)}, f32[512,1024]{1,0:T(8,128)}, bf16[512,1024]{1,0:T(8,128)(2,1)}, f32[512,128]{1,0:T(8...) custom-call(s32[4]{0:T(128)} %get-tuple-element.352.block_ref.place_, ...), custom_call_target="tpu_custom_call" | custom-call | flops 9663676416 | bytes 41943040 | tf_op jit(solution)/shard_map/ffn_forward/pallas_call | solution.py:314
  208.9 32.4 %collective-permute-done.14.refs_1_ = bf16[512,1024]{1,0:T(8,128)(2,1)S(1)} collective-permute-done((bf16[512,1024]{1,0:T(8,128)(2,1)}, bf16[512,1024]{1,0:T(8,128)(2,1)S(1)}, u32[]{:S(2)}, u32[]{:S(2)}) %collective-permute-start.14) | collective-permute-done | bytes 1048608 | tf_op jit(solution)/shard_map/ppermute | solution.py:74
  244.1 36.6 %attend_forward.3 = (bf16[2048,256]{1,0:T(8,128)(2,1)}, bf16[2048,256]{1,0:T(8,128)(2,1)}, bf16[2048,256]{1,0:T(8,128)(2,1)}, f32[2048,256]{1,0:T(8,128)}, f32[8...) custom-call(s32[4]{0:T(128)} %get-tuple-element.352.block_ref.place_, ...), custom_call_target="tpu_custom_call" | custom-call | flops 13958643712 | bytes 20971520 | tf_op jit(solution)/shard_map/attend_forward/pallas_call | solution.py:832
  286.2 22.6 %all-gather.5.cloned.1.call-done = bf16[32,128,2304]{2,1,0:T(8,128)(2,1)} async-done(((bf16[1,128,2304]{2,1,0:T(8,128)(2,1)}), bf16[32,128,2304]{2,1,0:T(8,128)(2,1)}) %all-gather.5.cloned.1.call-update) | async-done | bytes 18874384 | tf_op jit(solution)/shard_map/all_gather | solution.py:1038
  308.8 27.9 %ffn_forward.3 = (f32[512,1024]{1,0:T(8,128)}, f32[512,1024]{1,0:T(8,128)}, f32[512,1024]{1,0:T(8,128)}, bf16[512,1024]{1,0:T(8,128)(2,1)}, f32[512,128]{1,0:T(8...) custom-call(s32[4]{0:T(128)} %get-tuple-element.352.block_ref.place_ref, ...), custom_call_target="tpu_custom_call" | custom-call | flops 9663676416 | bytes 41943040 | tf_op jit(solution)/shard_map/ffn_forward/pallas_call | solution.py:314
  336.7 32.0 %ffn_backward.2 = (bf16[512,1024]{1,0:T(8,128)(2,1)}, f32[512,1024]{1,0:T(8,128)}, bf16[512,1024]{1,0:T(8,128)(2,1)}, bf16[512,256]{1,0:T(8,128)(2,1)}, bf16[512...) custom-call(s32[4]{0:T(128)} %get-tuple-element.352.block_ref.place_, ...), custom_call_target="tpu_custom_call" | custom-call | flops 9663676416 | bytes 46137344 | tf_op jit(solution)/shard_map/ffn_backward/pallas_call | solution.py:486
  373.2 17.9 %whole_grads.1 = bf16[8,4,128,2304]{3,2,1,0:T(8,128)(2,1)} custom-call(s32[4]{0:T(128)} %get-tuple-element.352.block_ref.place_ref, bf16[512,1024]{1,0:T(8,128)(2,1)} %get-tuple-element.159.refs_0_, bf16[512,1024]{1,0:T(8,128)(2,1)} %get-tuple-element.160.refs_1_, bf16[512,1024]{1,0:T(8,128)(2,1)} %get-tuple-element.161.refs_2_, ...), custom_call_target="tpu_custom_call" | custom-call | flops 9663676416 | bytes 31457280 | tf_op jit(solution)/shard_map/whole_grads/pallas_call | solution.py:677
  391.2 50.0 %attend_backward.2 = (bf16[2048,768]{1,0:T(8,128)(2,1)}, f32[8,128]{1,0:T(8,128)}, bf16[2,512,1024]{2,1,0:T(8,128)(2,1)}, bf16[2,512,1024]{2,1,0:T(8,128)(2,1)}) custom-call(s32[4]{0:T(128)} %get-tuple-element.352.block_ref.place_ref, s32[8]{0:T(128)} %broadcast_xor_fusion.place_ref, s32[10]{0:T(128)} %constant.44.clone.open_ref, ...), custom_call_target="tpu_custom_call" | custom-call | flops 30064771072 | bytes 16777216 | tf_op jit(solution)/shard_map/attend_backward/pallas_call | solution.py:960
  449.7 7.9 attn_grads.2
  462.6 15.8 %collective-permute-done.25 = bf16[4,128,768]{2,1,0:T(8,128)(2,1)S(1)} collective-permute-done((bf16[4,128,768]{2,1,0:T(8,128)(2,1)}, bf16[4,128,768]{2,1,0:T(8,128)(2,1)S(1)}, u32[]{:S(2)}, u32[]{:S(2)}) %collective-permute-start.25) | collective-permute-done | bytes 786464 | tf_op jit(solution)/shard_map/ppermute | solution.py:74
  485.5 11.4 %down_grads.1 = (bf16[2,2,4,128,1024]{4,3,2,1,0:T(8,128)(2,1)}, bf16[2,2,4,128,1024]{4,3,2,1,0:T(8,128)(2,1)}) custom-call(s32[8]{0:T(128)} %broadcast_xor_fusion.place_ref, f32[512,1024]{1,0:T(8,128)} %multiply_add_fusion.1.refs_0_, bf16[4,512,1024]{2,1,0:T(8,128)(2,1)} %get-tuple-element.178.refs_1_), custom_call_target="tpu_custom_call" | custom-call | flops 4294967296 | bytes 16777216 | tf_op jit(solution)/shard_map/down_grads/pallas_call | solution.py:602
  503.1 7.2 collective-permute-done.27
  513.4 32.5 %ffn_backward.3 = (bf16[512,1024]{1,0:T(8,128)(2,1)}, f32[512,1024]{1,0:T(8,128)}, bf16[512,1024]{1,0:T(8,128)(2,1)}, bf16[512,256]{1,0:T(8,128)(2,1)}, bf16[512...) custom-call(s32[4]{0:T(128)} %get-tuple-element.352.block_ref.place_, ...), custom_call_target="tpu_custom_call" | custom-call | flops 9663676416 | bytes 46137344 | tf_op jit(solution)/shard_map/ffn_backward/pallas_call | solution.py:486
  547.9 13.3 %up_grads.1 = (bf16[2,2,4,128,1280]{4,3,2,1,0:T(8,128)(2,1)}, bf16[2,2,4,128,1280]{4,3,2,1,0:T(8,128)(2,1)}) custom-call(s32[8]{0:T(128)} %broadcast_xor_fusion.place_ref, bf16[512,1024]{1,0:T(8,128)(2,1)} %get-tuple-element.203.refs_0_, bf16[512,1024]{1,0:T(8,128)(2,1)} %get-tuple-element.204.refs_1_, bf16[4,512,1024]{2,1,0:T(8,128)(2,1)} %get-tuple-element.205.refs_2_, ...), custom_call_target="tpu_custom_call" | custom-call | flops 5368709120 | bytes 16777216 | tf_op jit(solution)/shard_map/up_grads/pallas_call | solution.py:602
  563.4 6.1 add_convert_fusion.2
  578.3 50.1 %attend_backward.3 = (bf16[2048,768]{1,0:T(8,128)(2,1)}, f32[8,128]{1,0:T(8,128)}, bf16[2,512,1024]{2,1,0:T(8,128)(2,1)}, bf16[2,512,1024]{2,1,0:T(8,128)(2,1)}) custom-call(s32[4]{0:T(128)} %get-tuple-element.352.block_ref.place_ref, s32[8]{0:T(128)} %broadcast_xor_fusion.place_ref, s32[10]{0:T(128)} %constant.44.clone.open_ref, ...), custom_call_target="tpu_custom_call" | custom-call | flops 30064771072 | bytes 16777216 | tf_op jit(solution)/shard_map/attend_backward/pallas_call | solution.py:960
  628.4 18.0 %collective-permute-done.34 = bf16[1,2,4,128,1024]{4,3,2,1,0:T(8,128)(2,1)} collective-permute-done((bf16[1,2,4,128,1024]{4,3,2,1,0:T(8,128)(2,1)}, bf16[1,2,4,128,1024]{4,3,2,1,0:T(8,128)(2,1)}, u32[]{:S(2)}, u32[]{:S(2)}) %collective-permute-start.34) | collective-permute-done | bytes 2097184 | tf_op jit(solution)/shard_map/ppermute | solution.py:74
  646.4 12.1 %collective-permute-done.33 = bf16[1,2,4,128,1280]{4,3,2,1,0:T(8,128)(2,1)} collective-permute-done((bf16[1,2,4,128,1280]{4,3,2,1,0:T(8,128)(2,1)}, bf16[1,2,4,128,1280]{4,3,2,1,0:T(8,128)(2,1)}, u32[]{:S(2)}, u32[]{:S(2)}) %collective-permute-start.33) | collective-permute-done | bytes 2621472 | tf_op jit(solution)/shard_map/ppermute | solution.py:74
  677.0 7.9 attn_grads.3
  695.8 10.0 %collective-permute-done.42 = bf16[4,128,768]{2,1,0:T(8,128)(2,1)S(1)} collective-permute-done((bf16[4,128,768]{2,1,0:T(8,128)(2,1)}, bf16[4,128,768]{2,1,0:T(8,128)(2,1)S(1)}, u32[]{:S(2)}, u32[]{:S(2)}) %collective-permute-start.42) | collective-permute-done | bytes 786464 | tf_op jit(solution)/shard_map/ppermute | solution.py:74
  711.7 15.7 %collective-permute-done.36 = bf16[1,512,1024]{2,1,0:T(8,128)(2,1)S(1)} collective-permute-done((bf16[1,512,1024]{2,1,0:T(8,128)(2,1)}, bf16[1,512,1024]{2,1,0:T(8,128)(2,1)S(1)}, u32[]{:S(2)}, u32[]{:S(2)}) %collective-permute-start.36) | collective-permute-done | bytes 1048608 | tf_op jit(solution)/shard_map/ppermute | solution.py:74
  756.5 5.7 collective-permute-done.41
  774.8 15.3 %collective-permute-done.50 = bf16[1,128,1024]{2,1,0:T(8,128)(2,1)S(1)} collective-permute-done((bf16[1,128,1024]{2,1,0:T(8,128)(2,1)S(1)}, bf16[1,128,1024]{2,1,0:T(8,128)(2,1)S(1)}, u32[]{:S(2)}, u32[]{:S(2)}) %collective-permute-start.50) | collective-permute-done | bytes 262176 | tf_op jit(solution)/shard_map/ppermute | solution.py:74
  791.2 5.9 collective-permute-done.47
  (333 shorter events, 174.7 us)
Async XLA Ops:
  7.2 171.5 %all-gather.3.cloned.1.call-start = ((), (), s32[]{:S(2)}) async-start(), calls=%async_computation.1 | async-start | bytes 19464192 | tf_op jit(solution)/shard_map/all_gather | solution.py:1038
  10.6 298.2 %all-gather.5.cloned.1.call-start = ((), (), s32[]{:S(2)}) async-start(), calls=%async_computation.2 | async-start | bytes 19464192 | tf_op jit(solution)/shard_map/all_gather | solution.py:1038
  11.5 785.7 %reduce-scatter.2.cloned.1.call-start = ((), (), s32[]{:S(2)}) async-start(), calls=%async_computation.3 | async-start | bytes 19464192 | tf_op jit(solution)/shard_map/reduce_scatter | solution.py:1114
  13.2 30.5 %collective-permute-start = (bf16[512,1024]{1,0:T(8,128)(2,1)S(1)}, bf16[512,1024]{1,0:T(8,128)(2,1)}, u32[]{:S(2)}, u32[]{:S(2)}) collective-permute-start(bf16[512,1024]{1,0:T(8,128)(2,1)S(1)} %multiply_convert_fusion.refs_0_), channel_id=1, source_target_pairs={{0,2},{1,3},{2,0},{3,1},{4,6},{5,7},{6,4},{7,5},{8,10},{9,11},{10,... | collective-permute-start | bytes 3145736 | tf_op jit(solution)/shard_map/ppermute | solution.py:74
  16.2 60.4 %collective-permute-start.1 = (bf16[512,1024]{1,0:T(8,128)(2,1)S(1)}, bf16[512,1024]{1,0:T(8,128)(2,1)}, u32[]{:S(2)}, u32[]{:S(2)}) collective-permute-start(bf16[512,1024]{1,0:T(8,128)(2,1)S(1)} %multiply_convert_fusion.refs_0_), channel_id=1, source_target_pairs={{0,1},{1,0},{2,3},{3,2},{4,5},{5,4},{6,7},{7,6},{8,9},{9,8},{10,11... | collective-permute-start | bytes 3145736 | tf_op jit(solution)/shard_map/ppermute | solution.py:74
  43.7 32.9 %collective-permute-start.2 = (bf16[512,1024]{1,0:T(8,128)(2,1)}, bf16[512,1024]{1,0:T(8,128)(2,1)}, u32[]{:S(2)}, u32[]{:S(2)}) collective-permute-start(bf16[512,1024]{1,0:T(8,128)(2,1)} %collective-permute-done.refs_1_), channel_id=1, source_target_pairs={{0,1},{1,0},{2,3},{3,2},{4,5},{5,4},{6,7},{7,6},{8,9},{9,8},{10,11... | collective-permute-start | bytes 3145736 | tf_op jit(solution)/shard_map/ppermute | solution.py:74
  48.2 24.4 %collective-permute-start.5 = (bf16[128,768]{1,0:T(8,128)(2,1)S(1)}, bf16[128,768]{1,0:T(8,128)(2,1)S(1)}, u32[]{:S(2)}, u32[]{:S(2)}) collective-permute-start(bf16[128,768]{1,0:T(8,128)(2,1)S(1)} %pad_maximum_fusion.12), channel_id=1, source_target_pairs={{0,24},{4,28},{8,16},{12,20},{16,8},{20,12},{24,0},{28,4},{1,25},{... | collective-permute-start | bytes 589832 | tf_op jit(solution)/shard_map/ppermute | solution.py:74
  72.7 36.3 %collective-permute-start.6 = (bf16[4,128,768]{2,1,0:T(8,128)(2,1)S(1)}, bf16[4,128,768]{2,1,0:T(8,128)(2,1)}, u32[]{:S(2)}, u32[]{:S(2)}) collective-permute-start(bf16[4,128,768]{2,1,0:T(8,128)(2,1)S(1)} %pad_maximum_fusion.4.refs_4_.refs_11_), channel_id=1, source_target_pairs={{0,4},{4,0},{8,12},{12,8},{16,20},{20,16},{24,28},{28,24},{1,5},{5... | collective-permute-start | bytes 2359304 | tf_op jit(solution)/shard_map/ppermute | solution.py:74
  76.6 25.7 %collective-permute-start.10 = (bf16[128,768]{1,0:T(8,128)(2,1)S(1)}, bf16[128,768]{1,0:T(8,128)(2,1)S(1)}, u32[]{:S(2)}, u32[]{:S(2)}) collective-permute-start(bf16[128,768]{1,0:T(8,128)(2,1)S(1)} %pad_maximum_fusion.13), channel_id=1, source_target_pairs={{0,16},{4,20},{8,24},{12,28},{16,0},{20,4},{24,8},{28,12},{1,17},{... | collective-permute-start | bytes 589832 | tf_op jit(solution)/shard_map/ppermute | solution.py:74
  109.1 48.0 %collective-permute-start.13 = (bf16[4,128,768]{2,1,0:T(8,128)(2,1)}, bf16[4,128,768]{2,1,0:T(8,128)(2,1)}, u32[]{:S(2)}, u32[]{:S(2)}) collective-permute-start(bf16[4,128,768]{2,1,0:T(8,128)(2,1)} %pad_maximum_fusion.5.refs_4_.refs_11_), channel_id=1, source_target_pairs={{0,4},{4,0},{8,12},{12,8},{16,20},{20,16},{24,28},{28,24},{1,5},{5... | collective-permute-start | bytes 2359304 | tf_op jit(solution)/shard_map/ppermute | solution.py:74
  207.3 34.0 %collective-permute-start.14 = (bf16[512,1024]{1,0:T(8,128)(2,1)}, bf16[512,1024]{1,0:T(8,128)(2,1)S(1)}, u32[]{:S(2)}, u32[]{:S(2)}) collective-permute-start(bf16[512,1024]{1,0:T(8,128)(2,1)} %get-tuple-element.141.refs_0_), channel_id=1, source_target_pairs={{0,2},{1,3},{2,0},{3,1},{4,6},{5,7},{6,4},{7,5},{8,10},{9,11},{10,... | collective-permute-start | bytes 3145736 | tf_op jit(solution)/shard_map/ppermute | solution.py:74
  208.9 33.8 %collective-permute-start.15 = (bf16[512,1024]{1,0:T(8,128)(2,1)}, bf16[512,1024]{1,0:T(8,128)(2,1)S(1)}, u32[]{:S(2)}, u32[]{:S(2)}) collective-permute-start(bf16[512,1024]{1,0:T(8,128)(2,1)} %get-tuple-element.141.refs_0_), channel_id=1, source_target_pairs={{0,1},{1,0},{2,3},{3,2},{4,5},{5,4},{6,7},{7,6},{8,9},{9,8},{10,11... | collective-permute-start | bytes 3145736 | tf_op jit(solution)/shard_map/ppermute | solution.py:74
  280.8 28.1 %collective-permute-start.17 = (bf16[512,256]{1,0:T(8,128)(2,1)}, bf16[512,256]{1,0:T(8,128)(2,1)}, u32[]{:S(2)}, u32[]{:S(2)}) collective-permute-start(bf16[512,256]{1,0:T(8,128)(2,1)} %get-tuple-element.145), channel_id=1, source_target_pairs={{0,2},{1,3},{2,0},{3,1},{4,6},{5,7},{6,4},{7,5},{8,10},{9,11},{10,... | collective-permute-start | bytes 786440 | tf_op jit(solution)/shard_map/ppermute | solution.py:74
  282.3 26.5 %collective-permute-start.18 = (bf16[512,256]{1,0:T(8,128)(2,1)}, bf16[512,256]{1,0:T(8,128)(2,1)}, u32[]{:S(2)}, u32[]{:S(2)}) collective-permute-start(bf16[512,256]{1,0:T(8,128)(2,1)} %get-tuple-element.146), channel_id=1, source_target_pairs={{0,1},{1,0},{2,3},{3,2},{4,5},{5,4},{6,7},{7,6},{8,9},{9,8},{10,11... | collective-permute-start | bytes 786440 | tf_op jit(solution)/shard_map/ppermute | solution.py:74
  282.3 26.5 %collective-permute-start.19 = (bf16[512,256]{1,0:T(8,128)(2,1)}, bf16[512,256]{1,0:T(8,128)(2,1)}, u32[]{:S(2)}, u32[]{:S(2)}) collective-permute-start(bf16[512,256]{1,0:T(8,128)(2,1)} %get-tuple-element.147), channel_id=1, source_target_pairs={{0,3},{1,2},{2,1},{3,0},{4,7},{5,6},{6,5},{7,4},{8,11},{9,10},{10,... | collective-permute-start | bytes 786440 | tf_op jit(solution)/shard_map/ppermute | solution.py:74
  368.7 22.5 %collective-permute-start.20 = (bf16[512,256]{1,0:T(8,128)(2,1)}, bf16[512,256]{1,0:T(8,128)(2,1)}, u32[]{:S(2)}, u32[]{:S(2)}) collective-permute-start(bf16[512,256]{1,0:T(8,128)(2,1)} %get-tuple-element.156), channel_id=1, source_target_pairs={{0,2},{1,3},{2,0},{3,1},{4,6},{5,7},{6,4},{7,5},{8,10},{9,11},{10,... | collective-permute-start | bytes 786440 | tf_op jit(solution)/shard_map/ppermute | solution.py:74
  368.8 22.4 %collective-permute-start.21 = (bf16[512,256]{1,0:T(8,128)(2,1)}, bf16[512,256]{1,0:T(8,128)(2,1)}, u32[]{:S(2)}, u32[]{:S(2)}) collective-permute-start(bf16[512,256]{1,0:T(8,128)(2,1)} %get-tuple-element.157), channel_id=1, source_target_pairs={{0,1},{1,0},{2,3},{3,2},{4,5},{5,4},{6,7},{7,6},{8,9},{9,8},{10,11... | collective-permute-start | bytes 786440 | tf_op jit(solution)/shard_map/ppermute | solution.py:74
  369.1 22.1 %collective-permute-start.22 = (bf16[512,256]{1,0:T(8,128)(2,1)}, bf16[512,256]{1,0:T(8,128)(2,1)}, u32[]{:S(2)}, u32[]{:S(2)}) collective-permute-start(bf16[512,256]{1,0:T(8,128)(2,1)} %get-tuple-element.158), channel_id=1, source_target_pairs={{0,3},{1,2},{2,1},{3,0},{4,7},{5,6},{6,5},{7,4},{8,11},{9,10},{10,... | collective-permute-start | bytes 786440 | tf_op jit(solution)/shard_map/ppermute | solution.py:74
  449.6 28.8 %collective-permute-start.24 = (bf16[1,512,1024]{2,1,0:T(8,128)(2,1)}, bf16[1,512,1024]{2,1,0:T(8,128)(2,1)}, u32[]{:S(2)}, u32[]{:S(2)}) collective-permute-start(bf16[1,512,1024]{2,1,0:T(8,128)(2,1)} %add_convert_fusion.10), channel_id=1, source_target_pairs={{0,2},{1,3},{2,0},{3,1},{4,6},{5,7},{6,4},{7,5},{8,10},{9,11},{10,... | collective-permute-start | bytes 3145736 | tf_op jit(solution)/shard_map/ppermute | solution.py:74
  457.6 20.8 %collective-permute-start.25 = (bf16[4,128,768]{2,1,0:T(8,128)(2,1)}, bf16[4,128,768]{2,1,0:T(8,128)(2,1)S(1)}, u32[]{:S(2)}, u32[]{:S(2)}) collective-permute-start(bf16[4,128,768]{2,1,0:T(8,128)(2,1)} %get-tuple-element.176), channel_id=1, source_target_pairs={{0,4},{4,0},{8,12},{12,8},{16,20},{20,16},{24,28},{28,24},{1,5},{5... | collective-permute-start | bytes 2359304 | tf_op jit(solution)/shard_map/ppermute | solution.py:74
  497.0 50.9 %collective-permute-start.26 = (bf16[2,2,4,128,1024]{4,3,2,1,0:T(8,128)(2,1)}, bf16[2,2,4,128,1024]{4,3,2,1,0:T(8,128)(2,1)}, u32[]{:S(2)}, u32[]{:S(2)}) collective-permute-start(bf16[2,2,4,128,1024]{4,3,2,1,0:T(8,128)(2,1)} %get-tuple-element.196), channel_id=1, source_target_pairs={{0,1},{1,0},{2,3},{3,2},{4,5},{5,4},{6,7},{7,6},{8,9},{9,8},{10,11... | collective-permute-start | bytes 12582920 | tf_op jit(solution)/shard_map/ppermute | solution.py:74
  511.1 34.8 %collective-permute-start.28 = (bf16[1,128,768]{2,1,0:T(8,128)(2,1)}, bf16[1,128,768]{2,1,0:T(8,128)(2,1)}, u32[]{:S(2)}, u32[]{:S(2)}) collective-permute-start(bf16[1,128,768]{2,1,0:T(8,128)(2,1)} %add_convert_fusion.22), channel_id=1, source_target_pairs={{0,16},{4,20},{8,24},{12,28},{16,0},{20,4},{24,8},{28,12},{1,17},{... | collective-permute-start | bytes 589832 | tf_op jit(solution)/shard_map/ppermute | solution.py:74
  575.7 82.8 %collective-permute-start.33 = (bf16[1,2,4,128,1280]{4,3,2,1,0:T(8,128)(2,1)}, bf16[1,2,4,128,1280]{4,3,2,1,0:T(8,128)(2,1)}, u32[]{:S(2)}, u32[]{:S(2)}) collective-permute-start(bf16[1,2,4,128,1280]{4,3,2,1,0:T(8,128)(2,1)} %get-tuple-element.222), channel_id=1, source_target_pairs={{0,2},{1,3},{2,0},{3,1},{4,6},{5,7},{6,4},{7,5},{8,10},{9,11},{10,... | collective-permute-start | bytes 7864328 | tf_op jit(solution)/shard_map/ppermute | solution.py:74
  577.1 69.3 %collective-permute-start.34 = (bf16[1,2,4,128,1024]{4,3,2,1,0:T(8,128)(2,1)}, bf16[1,2,4,128,1024]{4,3,2,1,0:T(8,128)(2,1)}, u32[]{:S(2)}, u32[]{:S(2)}) collective-permute-start(bf16[1,2,4,128,1024]{4,3,2,1,0:T(8,128)(2,1)} %get-tuple-element.223), channel_id=1, source_target_pairs={{0,4},{4,0},{8,12},{12,8},{16,20},{20,16},{24,28},{28,24},{1,5},{5... | collective-permute-start | bytes 6291464 | tf_op jit(solution)/shard_map/ppermute | solution.py:74
  675.4 31.8 %collective-permute-start.48 = (bf16[1,4,128,1024]{3,2,1,0:T(8,128)(2,1)}, bf16[1,4,128,1024]{3,2,1,0:T(8,128)(2,1)}, u32[]{:S(2)}, u32[]{:S(2)}) collective-permute-start(bf16[1,4,128,1024]{3,2,1,0:T(8,128)(2,1)} %get-tuple-element.248), channel_id=1, source_target_pairs={{0,2},{1,3},{2,0},{3,1},{4,6},{5,7},{6,4},{7,5},{8,10},{9,11},{10,... | collective-permute-start | bytes 3145736 | tf_op jit(solution)/shard_map/ppermute | solution.py:74
  685.0 20.7 %collective-permute-start.42 = (bf16[4,128,768]{2,1,0:T(8,128)(2,1)}, bf16[4,128,768]{2,1,0:T(8,128)(2,1)S(1)}, u32[]{:S(2)}, u32[]{:S(2)}) collective-permute-start(bf16[4,128,768]{2,1,0:T(8,128)(2,1)} %get-tuple-element.240), channel_id=1, source_target_pairs={{0,4},{4,0},{8,12},{12,8},{16,20},{20,16},{24,28},{28,24},{1,5},{5... | collective-permute-start | bytes 2359304 | tf_op jit(solution)/shard_map/ppermute | solution.py:74
  689.0 38.4 %collective-permute-start.36 = (bf16[1,512,1024]{2,1,0:T(8,128)(2,1)}, bf16[1,512,1024]{2,1,0:T(8,128)(2,1)S(1)}, u32[]{:S(2)}, u32[]{:S(2)}) collective-permute-start(bf16[1,512,1024]{2,1,0:T(8,128)(2,1)} %add_convert_fusion.6), channel_id=1, source_target_pairs={{0,2},{1,3},{2,0},{3,1},{4,6},{5,7},{6,4},{7,5},{8,10},{9,11},{10,... | collective-permute-start | bytes 3145736 | tf_op jit(solution)/shard_map/ppermute | solution.py:74
  695.6 58.3 %collective-permute-start.45 = (bf16[1,4,128,1280]{3,2,1,0:T(8,128)(2,1)}, bf16[1,4,128,1280]{3,2,1,0:T(8,128)(2,1)}, u32[]{:S(2)}, u32[]{:S(2)}) collective-permute-start(bf16[1,4,128,1280]{3,2,1,0:T(8,128)(2,1)} %get-tuple-element.245), channel_id=1, source_target_pairs={{0,4},{4,0},{8,12},{12,8},{16,20},{20,16},{24,28},{28,24},{1,5},{5... | collective-permute-start | bytes 3932168 | tf_op jit(solution)/shard_map/ppermute | solution.py:74
  706.7 41.4 %collective-permute-start.43 = (bf16[2,128,768]{2,1,0:T(8,128)(2,1)}, bf16[2,128,768]{2,1,0:T(8,128)(2,1)}, u32[]{:S(2)}, u32[]{:S(2)}) collective-permute-start(bf16[2,128,768]{2,1,0:T(8,128)(2,1)} %get-tuple-element.313), channel_id=1, source_target_pairs={{0,8},{4,12},{8,0},{12,4},{16,24},{20,28},{24,16},{28,20},{1,9},{5... | collective-permute-start | bytes 1179656 | tf_op jit(solution)/shard_map/ppermute | solution.py:74
  710.2 57.8 %collective-permute-start.49 = (bf16[2,128,1024]{2,1,0:T(8,128)(2,1)}, bf16[2,128,1024]{2,1,0:T(8,128)(2,1)}, u32[]{:S(2)}, u32[]{:S(2)}) collective-permute-start(bf16[2,128,1024]{2,1,0:T(8,128)(2,1)} %get-tuple-element.311), channel_id=1, source_target_pairs={{0,8},{4,12},{8,0},{12,4},{16,24},{20,28},{24,16},{28,20},{1,9},{5... | collective-permute-start | bytes 1572872 | tf_op jit(solution)/shard_map/ppermute | solution.py:74
  769.0 21.1 %collective-permute-start.50 = (bf16[1,128,1024]{2,1,0:T(8,128)(2,1)S(1)}, bf16[1,128,1024]{2,1,0:T(8,128)(2,1)S(1)}, u32[]{:S(2)}, u32[]{:S(2)}) collective-permute-start(bf16[1,128,1024]{2,1,0:T(8,128)(2,1)S(1)} %fusion.12), channel_id=1, source_target_pairs={{0,16},{4,20},{8,24},{12,28},{16,0},{20,4},{24,8},{28,12},{1,17},{... | collective-permute-start | bytes 786440 | tf_op jit(solution)/shard_map/ppermute | solution.py:74
  774.0 23.1 %collective-permute-start.47 = (bf16[1,128,1280]{2,1,0:T(8,128)(2,1)S(1)}, bf16[1,128,1280]{2,1,0:T(8,128)(2,1)S(1)}, u32[]{:S(2)}, u32[]{:S(2)}) collective-permute-start(bf16[1,128,1280]{2,1,0:T(8,128)(2,1)S(1)} %fusion.9), channel_id=1, source_target_pairs={{0,16},{4,20},{8,24},{12,28},{16,0},{20,4},{24,8},{28,12},{1,17},{... | collective-permute-start | bytes 983048 | tf_op jit(solution)/shard_map/ppermute | solution.py:74
  (76 other events, 1318.0 us)
Sparse Core Ops, SparseCore 0:
  11.5 167.1 all-gather.2
  181.6 127.1 all-gather.4
  462.7 234.3 reduce-scatter.1

commit v4 on v3

--- a/solution.py
+++ b/solution.py
@@ -1059,7 +1059,7 @@
         )
         a_parts = exchange(a_parts)
         if not last:
-            shard, _ = lax.optimization_barrier((attn_shards[layer + 1], h_parts))
+            shard, _ = lax.optimization_barrier((attn_shards[layer + 1], logsum))
             pieces = gather_near(gather_far(shard, places), places)
             a_parts, pieces = lax.optimization_barrier((a_parts, pieces))
             attn_set.append(pieces)
@@ -1140,6 +1140,8 @@
         for hop in side_hops:
             keep, send = add_halves(keep, arrived)
             arrived = swap(send, *hop)
+        if layer == 0:
+            packed, arrived = lax.optimization_barrier((packed, arrived))
         attn_keep, attn_send = attn_grads(places, h_parts, packed)
         attn_arrived = swap(attn_send, *near_hop)
         if layer > 0:

time: 818 us -> 833 us (1.018)
  waiting for transfers between devices: 270 us -> 301 us
    ppermute x51, waiting for transfers between devices: 226 us -> 266 us  [swap(): return lax.ppermute(array, axis, [(i, i ^ mask) for i in range(size)])]
    all_gather x2, waiting for transfers between devices: 44.3 us -> 34.7 us  [local(): whole = lax.all_gather(packed, ('dp', 'tensor'), axis=0, tiled=False)]
  transfers between devices with their start and end apart: 54 -> 54, of which waited for: 27 -> 28; matrix products, arithmetic and copies ran while one was open for 12% -> 10% of each run, Pallas kernels for 30% -> 29%
where the time goes in v4:
time: 833 us; the launch traced here: 823 us
  Pallas kernels  352 us (42%)
  waiting for transfers between devices  301 us (36%)
  other arithmetic  73.8 us (9%)
  starting transfers between devices  56.4 us (7%)
  local copies, waits for them, and re-layouts  25.4 us (3%)
  between operations  14.9 us (2%)
    ppermute x51, waiting for transfers between devices, swap(): return lax.ppermute(array, axis, [(i, i ^ mask) for i in range(size)])  266 us
    pallas_call x2, Pallas kernels, attend_backward(): pl.pallas_call(backward_kernel, in_specs=[scalars] * 4 + [whole] * (parts...  99.6 us
    pallas_call x2, Pallas kernels, attend_forward(): pl.pallas_call(forward_kernel, in_specs=[pl.BlockSpec(memory_space=pltpu....  73.4 us
    pallas_call x2, Pallas kernels, ffn_backward(): pl.pallas_call(functools.partial(ffn_backward_kernel, parts), in_specs=[p...  64.8 us
    ppermute x51, starting transfers between devices, swap(): return lax.ppermute(array, axis, [(i, i ^ mask) for i in range(size)])  56.2 us
    pallas_call x2, Pallas kernels, ffn_forward(): pl.pallas_call(functools.partial(ffn_forward_kernel, parts, last), in_spe...  55.9 us
    all_gather x2, waiting for transfers between devices, local(): whole = lax.all_gather(packed, ('dp', 'tensor'), axis=0, tiled=False)  34.7 us
    convert_element_type x14, other arithmetic, add_low(): return (kept.astype(F32) + arrived.astype(F32)).astype(BF16)  30.4 us
  transfers between devices with their start and end apart: 54, of which 28 were waited for; matrix products, arithmetic and copies ran while one was open for 10% of the time, Pallas kernels for 29%

profile of v4, /device:TPU:0, one launch (start us, length us, event | category | flops | bytes accessed | tf_op | source)
XLA Modules:
  0.0 823.4 jit_solution(2926949114704112284)
XLA Ops:
  20.8 22.9 %collective-permute-done.refs_1_ = bf16[512,1024]{1,0:T(8,128)(2,1)} collective-permute-done((bf16[512,1024]{1,0:T(8,128)(2,1)S(1)}, bf16[512,1024]{1,0:T(8,128)(2,1)}, u32[]{:S(2)}, u32[]{:S(2)}) %collective-permute-start) | collective-permute-done | bytes 1048608 | tf_op jit(solution)/shard_map/ppermute | solution.py:74
  49.9 22.7 %collective-permute-done.6.refs_5_.refs_12_ = bf16[4,128,768]{2,1,0:T(8,128)(2,1)S(1)} collective-permute-done((bf16[4,128,768]{2,1,0:T(8,128)(2,1)S(1)}, bf16[4,128,768]{2,1,0:T(8,128)(2,1)S(1)}, u32[]{:S(2)}, u32[]{:S(2)}) %collective-permute-start.6) | collective-permute-done | bytes 786464 | tf_op jit(solution)/shard_map/ppermute | solution.py:74
  73.4 36.7 %attend_forward.2 = (bf16[2048,256]{1,0:T(8,128)(2,1)}, bf16[2048,256]{1,0:T(8,128)(2,1)}, bf16[2048,256]{1,0:T(8,128)(2,1)}, f32[2048,256]{1,0:T(8,128)}, f32[8...) custom-call(s32[4]{0:T(128)} %get-tuple-element.356.block_ref.place_, ...), custom_call_target="tpu_custom_call" | custom-call | flops 13958643712 | bytes 20971520 | tf_op jit(solution)/shard_map/attend_forward/pallas_call | solution.py:832
  110.1 11.1 %collective-permute-start.10 = (bf16[128,768]{1,0:T(8,128)(2,1)}, bf16[128,768]{1,0:T(8,128)(2,1)S(1)}, u32[]{:S(2)}, u32[]{:S(2)}) collective-permute-start(bf16[128,768]{1,0:T(8,128)(2,1)} %pad_maximum_fusion.13), channel_id=1, source_target_pairs={{0,16},{4,20},{8,24},{12,28},{16,0},{20,4},{24,8},{28,12},{1,17},{... | collective-permute-start | bytes 589832 | tf_op jit(solution)/shard_map/ppermute | solution.py:74
  122.8 17.0 %collective-permute-done.10 = bf16[128,768]{1,0:T(8,128)(2,1)S(1)} collective-permute-done((bf16[128,768]{1,0:T(8,128)(2,1)}, bf16[128,768]{1,0:T(8,128)(2,1)S(1)}, u32[]{:S(2)}, u32[]{:S(2)}) %collective-permute-start.10) | collective-permute-done | bytes 196640 | tf_op jit(solution)/shard_map/ppermute | solution.py:74
  164.5 10.1 %all-gather.3.cloned.1.call-done = bf16[32,128,2304]{2,1,0:T(8,128)(2,1)} async-done(((bf16[1,128,2304]{2,1,0:T(8,128)(2,1)}), bf16[32,128,2304]{2,1,0:T(8,128)(2,1)}) %all-gather.3.cloned.1.call-update) | async-done | bytes 18874384 | tf_op jit(solution)/shard_map/all_gather | solution.py:1038
  174.6 28.3 %ffn_forward.2 = (f32[512,1024]{1,0:T(8,128)}, f32[512,1024]{1,0:T(8,128)}, f32[512,1024]{1,0:T(8,128)}, bf16[512,1024]{1,0:T(8,128)(2,1)}, f32[512,128]{1,0:T(8...) custom-call(s32[4]{0:T(128)} %get-tuple-element.356.block_ref.place_, ...), custom_call_target="tpu_custom_call" | custom-call | flops 9663676416 | bytes 41943040 | tf_op jit(solution)/shard_map/ffn_forward/pallas_call | solution.py:314
  204.4 32.5 %collective-permute-done.14.refs_1_ = bf16[512,1024]{1,0:T(8,128)(2,1)S(1)} collective-permute-done((bf16[512,1024]{1,0:T(8,128)(2,1)}, bf16[512,1024]{1,0:T(8,128)(2,1)S(1)}, u32[]{:S(2)}, u32[]{:S(2)}) %collective-permute-start.14) | collective-permute-done | bytes 1048608 | tf_op jit(solution)/shard_map/ppermute | solution.py:74
  239.7 36.7 %attend_forward.3 = (bf16[2048,256]{1,0:T(8,128)(2,1)}, bf16[2048,256]{1,0:T(8,128)(2,1)}, bf16[2048,256]{1,0:T(8,128)(2,1)}, f32[2048,256]{1,0:T(8,128)}, f32[8...) custom-call(s32[4]{0:T(128)} %get-tuple-element.356.block_ref.place_, ...), custom_call_target="tpu_custom_call" | custom-call | flops 13958643712 | bytes 20971520 | tf_op jit(solution)/shard_map/attend_forward/pallas_call | solution.py:832
  281.9 24.6 %all-gather.5.cloned.1.call-done = bf16[32,128,2304]{2,1,0:T(8,128)(2,1)} async-done(((bf16[1,128,2304]{2,1,0:T(8,128)(2,1)}), bf16[32,128,2304]{2,1,0:T(8,128)(2,1)}) %all-gather.5.cloned.1.call-update) | async-done | bytes 18874384 | tf_op jit(solution)/shard_map/all_gather | solution.py:1038
  306.5 27.6 %ffn_forward.3 = (f32[512,1024]{1,0:T(8,128)}, f32[512,1024]{1,0:T(8,128)}, f32[512,1024]{1,0:T(8,128)}, bf16[512,1024]{1,0:T(8,128)(2,1)}, f32[512,128]{1,0:T(8...) custom-call(s32[4]{0:T(128)} %get-tuple-element.356.block_ref.place_ref, ...), custom_call_target="tpu_custom_call" | custom-call | flops 9663676416 | bytes 41943040 | tf_op jit(solution)/shard_map/ffn_forward/pallas_call | solution.py:314
  334.1 32.2 %ffn_backward.2 = (bf16[512,1024]{1,0:T(8,128)(2,1)}, f32[512,1024]{1,0:T(8,128)}, bf16[512,1024]{1,0:T(8,128)(2,1)}, bf16[512,256]{1,0:T(8,128)(2,1)}, bf16[512...) custom-call(s32[4]{0:T(128)} %get-tuple-element.356.block_ref.place_, ...), custom_call_target="tpu_custom_call" | custom-call | flops 9663676416 | bytes 46137344 | tf_op jit(solution)/shard_map/ffn_backward/pallas_call | solution.py:486
  370.9 18.1 %whole_grads.1 = bf16[8,4,128,2304]{3,2,1,0:T(8,128)(2,1)} custom-call(s32[4]{0:T(128)} %get-tuple-element.356.block_ref.place_ref, bf16[512,1024]{1,0:T(8,128)(2,1)} %get-tuple-element.162.refs_0_, bf16[512,1024]{1,0:T(8,128)(2,1)} %get-tuple-element.163.refs_1_, bf16[512,1024]{1,0:T(8,128)(2,1)} %get-tuple-element.164.refs_2_, ...), custom_call_target="tpu_custom_call" | custom-call | flops 9663676416 | bytes 31457280 | tf_op jit(solution)/shard_map/whole_grads/pallas_call | solution.py:677
  389.0 49.7 %attend_backward.2 = (bf16[2048,768]{1,0:T(8,128)(2,1)}, f32[8,128]{1,0:T(8,128)}, bf16[2,512,1024]{2,1,0:T(8,128)(2,1)}, bf16[2,512,1024]{2,1,0:T(8,128)(2,1)}) custom-call(s32[4]{0:T(128)} %get-tuple-element.356.block_ref.place_ref, s32[8]{0:T(128)} %broadcast_xor_fusion.place_ref, s32[10]{0:T(128)} %constant.44.clone.open_ref, ...), custom_call_target="tpu_custom_call" | custom-call | flops 30064771072 | bytes 16777216 | tf_op jit(solution)/shard_map/attend_backward/pallas_call | solution.py:960
  447.1 7.9 attn_grads.2
  459.0 15.8 %collective-permute-done.25 = bf16[4,128,768]{2,1,0:T(8,128)(2,1)S(1)} collective-permute-done((bf16[4,128,768]{2,1,0:T(8,128)(2,1)}, bf16[4,128,768]{2,1,0:T(8,128)(2,1)S(1)}, u32[]{:S(2)}, u32[]{:S(2)}) %collective-permute-start.25) | collective-permute-done | bytes 786464 | tf_op jit(solution)/shard_map/ppermute | solution.py:74
  481.9 11.5 %down_grads.1 = (bf16[2,2,4,128,1024]{4,3,2,1,0:T(8,128)(2,1)}, bf16[2,2,4,128,1024]{4,3,2,1,0:T(8,128)(2,1)}) custom-call(s32[8]{0:T(128)} %broadcast_xor_fusion.place_ref, f32[512,1024]{1,0:T(8,128)} %multiply_add_fusion.1.refs_0_, bf16[4,512,1024]{2,1,0:T(8,128)(2,1)} %get-tuple-element.181.refs_1_), custom_call_target="tpu_custom_call" | custom-call | flops 4294967296 | bytes 16777216 | tf_op jit(solution)/shard_map/down_grads/pallas_call | solution.py:602
  497.5 9.3 %collective-permute-done.27 = bf16[2,128,768]{2,1,0:T(8,128)(2,1)S(1)} collective-permute-done((bf16[2,128,768]{2,1,0:T(8,128)(2,1)S(1)}, bf16[2,128,768]{2,1,0:T(8,128)(2,1)S(1)}, u32[]{:S(2)}, u32[]{:S(2)}) %collective-permute-start.27) | collective-permute-done | bytes 393248 | tf_op jit(solution)/shard_map/ppermute | solution.py:74
  508.7 32.6 %ffn_backward.3 = (bf16[512,1024]{1,0:T(8,128)(2,1)}, f32[512,1024]{1,0:T(8,128)}, bf16[512,1024]{1,0:T(8,128)(2,1)}, bf16[512,256]{1,0:T(8,128)(2,1)}, bf16[512...) custom-call(s32[4]{0:T(128)} %get-tuple-element.356.block_ref.place_, ...), custom_call_target="tpu_custom_call" | custom-call | flops 9663676416 | bytes 46137344 | tf_op jit(solution)/shard_map/ffn_backward/pallas_call | solution.py:486
  543.3 12.9 %up_grads.1 = (bf16[2,2,4,128,1280]{4,3,2,1,0:T(8,128)(2,1)}, bf16[2,2,4,128,1280]{4,3,2,1,0:T(8,128)(2,1)}) custom-call(s32[8]{0:T(128)} %broadcast_xor_fusion.place_ref, bf16[512,1024]{1,0:T(8,128)(2,1)} %get-tuple-element.206.refs_0_, bf16[512,1024]{1,0:T(8,128)(2,1)} %get-tuple-element.207.refs_1_, bf16[4,512,1024]{2,1,0:T(8,128)(2,1)} %get-tuple-element.208.refs_2_, ...), custom_call_target="tpu_custom_call" | custom-call | flops 5368709120 | bytes 16777216 | tf_op jit(solution)/shard_map/up_grads/pallas_call | solution.py:602
  558.4 6.0 add_convert_fusion.2
  573.6 49.9 %attend_backward.3 = (bf16[2048,768]{1,0:T(8,128)(2,1)}, f32[8,128]{1,0:T(8,128)}, bf16[2,512,1024]{2,1,0:T(8,128)(2,1)}, bf16[2,512,1024]{2,1,0:T(8,128)(2,1)}) custom-call(s32[4]{0:T(128)} %get-tuple-element.356.block_ref.place_ref, s32[8]{0:T(128)} %broadcast_xor_fusion.place_ref, s32[10]{0:T(128)} %constant.44.clone.open_ref, ...), custom_call_target="tpu_custom_call" | custom-call | flops 30064771072 | bytes 16777216 | tf_op jit(solution)/shard_map/attend_backward/pallas_call | solution.py:960
  623.5 19.6 %collective-permute-done.34 = bf16[1,2,4,128,1024]{4,3,2,1,0:T(8,128)(2,1)} collective-permute-done((bf16[1,2,4,128,1024]{4,3,2,1,0:T(8,128)(2,1)}, bf16[1,2,4,128,1024]{4,3,2,1,0:T(8,128)(2,1)}, u32[]{:S(2)}, u32[]{:S(2)}) %collective-permute-start.34) | collective-permute-done | bytes 2097184 | tf_op jit(solution)/shard_map/ppermute | solution.py:74
  643.1 11.9 %collective-permute-done.33 = bf16[1,2,4,128,1280]{4,3,2,1,0:T(8,128)(2,1)} collective-permute-done((bf16[1,2,4,128,1280]{4,3,2,1,0:T(8,128)(2,1)}, bf16[1,2,4,128,1280]{4,3,2,1,0:T(8,128)(2,1)}, u32[]{:S(2)}, u32[]{:S(2)}) %collective-permute-start.33) | collective-permute-done | bytes 2621472 | tf_op jit(solution)/shard_map/ppermute | solution.py:74
  675.8 21.0 %collective-permute-done.48 = bf16[1,4,128,1024]{3,2,1,0:T(8,128)(2,1)} collective-permute-done((bf16[1,4,128,1024]{3,2,1,0:T(8,128)(2,1)}, bf16[1,4,128,1024]{3,2,1,0:T(8,128)(2,1)}, u32[]{:S(2)}, u32[]{:S(2)}) %collective-permute-start.48) | collective-permute-done | bytes 1048608 | tf_op jit(solution)/shard_map/ppermute | solution.py:74
  700.1 18.5 %collective-permute-done.36 = bf16[1,512,1024]{2,1,0:T(8,128)(2,1)S(1)} collective-permute-done((bf16[1,512,1024]{2,1,0:T(8,128)(2,1)}, bf16[1,512,1024]{2,1,0:T(8,128)(2,1)S(1)}, u32[]{:S(2)}, u32[]{:S(2)}) %collective-permute-start.36) | collective-permute-done | bytes 1048608 | tf_op jit(solution)/shard_map/ppermute | solution.py:74
  724.0 7.9 attn_grads.3
  740.0 13.4 %collective-permute-done.39 = f32[120,128]{1,0:T(8,128)S(1)} collective-permute-done((f32[120,128]{1,0:T(8,128)S(1)}, f32[120,128]{1,0:T(8,128)S(1)}, u32[]{:S(2)}, u32[]{:S(2)}) %collective-permute-start.39) | collective-permute-done | bytes 61472 | tf_op jit(solution)/shard_map/ppermute | solution.py:74
  754.1 5.1 multiply_add_fusion
  773.0 13.1 %collective-permute-done.46 = bf16[2,128,1280]{2,1,0:T(8,128)(2,1)S(1)} collective-permute-done((bf16[2,128,1280]{2,1,0:T(8,128)(2,1)S(1)}, bf16[2,128,1280]{2,1,0:T(8,128)(2,1)S(1)}, u32[]{:S(2)}, u32[]{:S(2)}) %collective-permute-start.46) | collective-permute-done | bytes 655392 | tf_op jit(solution)/shard_map/ppermute | solution.py:74
  787.3 11.4 %collective-permute-done.43 = bf16[2,128,768]{2,1,0:T(8,128)(2,1)S(1)} collective-permute-done((bf16[2,128,768]{2,1,0:T(8,128)(2,1)S(1)}, bf16[2,128,768]{2,1,0:T(8,128)(2,1)S(1)}, u32[]{:S(2)}, u32[]{:S(2)}) %collective-permute-start.43) | collective-permute-done | bytes 393248 | tf_op jit(solution)/shard_map/ppermute | solution.py:74
  800.0 6.0 collective-permute-done.47
  (351 shorter events, 164.4 us)
Async XLA Ops:
  7.2 167.4 %all-gather.3.cloned.1.call-start = ((), (), s32[]{:S(2)}) async-start(), calls=%async_computation.1 | async-start | bytes 19464192 | tf_op jit(solution)/shard_map/all_gather | solution.py:1038
  10.6 295.9 %all-gather.5.cloned.1.call-start = ((), (), s32[]{:S(2)}) async-start(), calls=%async_computation.2 | async-start | bytes 19464192 | tf_op jit(solution)/shard_map/all_gather | solution.py:1038
  11.5 800.5 %reduce-scatter.2.cloned.1.call-start = ((), (), s32[]{:S(2)}) async-start(), calls=%async_computation.3 | async-start | bytes 19464192 | tf_op jit(solution)/shard_map/reduce_scatter | solution.py:1114
  13.2 30.5 %collective-permute-start = (bf16[512,1024]{1,0:T(8,128)(2,1)S(1)}, bf16[512,1024]{1,0:T(8,128)(2,1)}, u32[]{:S(2)}, u32[]{:S(2)}) collective-permute-start(bf16[512,1024]{1,0:T(8,128)(2,1)S(1)} %multiply_convert_fusion.refs_0_), channel_id=1, source_target_pairs={{0,2},{1,3},{2,0},{3,1},{4,6},{5,7},{6,4},{7,5},{8,10},{9,11},{10,... | collective-permute-start | bytes 3145736 | tf_op jit(solution)/shard_map/ppermute | solution.py:74
  16.4 27.9 %collective-permute-start.3 = (bf16[128,768]{1,0:T(8,128)(2,1)S(1)}, bf16[128,768]{1,0:T(8,128)(2,1)S(1)}, u32[]{:S(2)}, u32[]{:S(2)}) collective-permute-start(bf16[128,768]{1,0:T(8,128)(2,1)S(1)} %pad_maximum_fusion.12), channel_id=1, source_target_pairs={{0,16},{4,20},{8,24},{12,28},{16,0},{20,4},{24,8},{28,12},{1,17},{... | collective-permute-start | bytes 589832 | tf_op jit(solution)/shard_map/ppermute | solution.py:74
  19.0 25.2 %collective-permute-start.4 = (bf16[128,768]{1,0:T(8,128)(2,1)S(1)}, bf16[128,768]{1,0:T(8,128)(2,1)S(1)}, u32[]{:S(2)}, u32[]{:S(2)}) collective-permute-start(bf16[128,768]{1,0:T(8,128)(2,1)S(1)} %pad_maximum_fusion.12), channel_id=1, source_target_pairs={{0,8},{4,12},{8,0},{12,4},{16,24},{20,28},{24,16},{28,20},{1,9},{5... | collective-permute-start | bytes 589832 | tf_op jit(solution)/shard_map/ppermute | solution.py:74
  20.6 23.7 %collective-permute-start.5 = (bf16[128,768]{1,0:T(8,128)(2,1)S(1)}, bf16[128,768]{1,0:T(8,128)(2,1)S(1)}, u32[]{:S(2)}, u32[]{:S(2)}) collective-permute-start(bf16[128,768]{1,0:T(8,128)(2,1)S(1)} %pad_maximum_fusion.12), channel_id=1, source_target_pairs={{0,24},{4,28},{8,16},{12,20},{16,8},{20,12},{24,0},{28,4},{1,25},{... | collective-permute-start | bytes 589832 | tf_op jit(solution)/shard_map/ppermute | solution.py:74
  20.8 51.7 %collective-permute-start.1 = (bf16[512,1024]{1,0:T(8,128)(2,1)S(1)}, bf16[512,1024]{1,0:T(8,128)(2,1)}, u32[]{:S(2)}, u32[]{:S(2)}) collective-permute-start(bf16[512,1024]{1,0:T(8,128)(2,1)S(1)} %multiply_convert_fusion.refs_0_), channel_id=1, source_target_pairs={{0,1},{1,0},{2,3},{3,2},{4,5},{5,4},{6,7},{7,6},{8,9},{9,8},{10,11... | collective-permute-start | bytes 3145736 | tf_op jit(solution)/shard_map/ppermute | solution.py:74
  43.7 28.8 %collective-permute-start.2 = (bf16[512,1024]{1,0:T(8,128)(2,1)}, bf16[512,1024]{1,0:T(8,128)(2,1)}, u32[]{:S(2)}, u32[]{:S(2)}) collective-permute-start(bf16[512,1024]{1,0:T(8,128)(2,1)} %collective-permute-done.refs_1_), channel_id=1, source_target_pairs={{0,1},{1,0},{2,3},{3,2},{4,5},{5,4},{6,7},{7,6},{8,9},{9,8},{10,11... | collective-permute-start | bytes 3145736 | tf_op jit(solution)/shard_map/ppermute | solution.py:74
  44.4 28.2 %collective-permute-start.6 = (bf16[4,128,768]{2,1,0:T(8,128)(2,1)S(1)}, bf16[4,128,768]{2,1,0:T(8,128)(2,1)S(1)}, u32[]{:S(2)}, u32[]{:S(2)}) collective-permute-start(bf16[4,128,768]{2,1,0:T(8,128)(2,1)S(1)} %pad_maximum_fusion.4.refs_4_.refs_11_), channel_id=1, source_target_pairs={{0,4},{4,0},{8,12},{12,8},{16,20},{20,16},{24,28},{28,24},{1,5},{5... | collective-permute-start | bytes 2359304 | tf_op jit(solution)/shard_map/ppermute | solution.py:74
  110.1 29.6 %collective-permute-start.10 = (bf16[128,768]{1,0:T(8,128)(2,1)}, bf16[128,768]{1,0:T(8,128)(2,1)S(1)}, u32[]{:S(2)}, u32[]{:S(2)}) collective-permute-start(bf16[128,768]{1,0:T(8,128)(2,1)} %pad_maximum_fusion.13), channel_id=1, source_target_pairs={{0,16},{4,20},{8,24},{12,28},{16,0},{20,4},{24,8},{28,12},{1,17},{... | collective-permute-start | bytes 589832 | tf_op jit(solution)/shard_map/ppermute | solution.py:74
  121.2 22.3 %collective-permute-start.11 = (bf16[128,768]{1,0:T(8,128)(2,1)}, bf16[128,768]{1,0:T(8,128)(2,1)S(1)}, u32[]{:S(2)}, u32[]{:S(2)}) collective-permute-start(bf16[128,768]{1,0:T(8,128)(2,1)} %pad_maximum_fusion.13), channel_id=1, source_target_pairs={{0,8},{4,12},{8,0},{12,4},{16,24},{20,28},{24,16},{28,20},{1,9},{5... | collective-permute-start | bytes 589832 | tf_op jit(solution)/shard_map/ppermute | solution.py:74
  121.2 25.4 %collective-permute-start.12 = (bf16[128,768]{1,0:T(8,128)(2,1)}, bf16[128,768]{1,0:T(8,128)(2,1)S(1)}, u32[]{:S(2)}, u32[]{:S(2)}) collective-permute-start(bf16[128,768]{1,0:T(8,128)(2,1)} %pad_maximum_fusion.13), channel_id=1, source_target_pairs={{0,24},{4,28},{8,16},{12,20},{16,8},{20,12},{24,0},{28,4},{1,25},{... | collective-permute-start | bytes 589832 | tf_op jit(solution)/shard_map/ppermute | solution.py:74
  202.9 34.0 %collective-permute-start.14 = (bf16[512,1024]{1,0:T(8,128)(2,1)}, bf16[512,1024]{1,0:T(8,128)(2,1)S(1)}, u32[]{:S(2)}, u32[]{:S(2)}) collective-permute-start(bf16[512,1024]{1,0:T(8,128)(2,1)} %get-tuple-element.144.refs_0_), channel_id=1, source_target_pairs={{0,2},{1,3},{2,0},{3,1},{4,6},{5,7},{6,4},{7,5},{8,10},{9,11},{10,... | collective-permute-start | bytes 3145736 | tf_op jit(solution)/shard_map/ppermute | solution.py:74
  204.4 33.9 %collective-permute-start.15 = (bf16[512,1024]{1,0:T(8,128)(2,1)}, bf16[512,1024]{1,0:T(8,128)(2,1)S(1)}, u32[]{:S(2)}, u32[]{:S(2)}) collective-permute-start(bf16[512,1024]{1,0:T(8,128)(2,1)} %get-tuple-element.144.refs_0_), channel_id=1, source_target_pairs={{0,1},{1,0},{2,3},{3,2},{4,5},{5,4},{6,7},{7,6},{8,9},{9,8},{10,11... | collective-permute-start | bytes 3145736 | tf_op jit(solution)/shard_map/ppermute | solution.py:74
  276.4 30.1 %collective-permute-start.17 = (bf16[512,256]{1,0:T(8,128)(2,1)}, bf16[512,256]{1,0:T(8,128)(2,1)}, u32[]{:S(2)}, u32[]{:S(2)}) collective-permute-start(bf16[512,256]{1,0:T(8,128)(2,1)} %get-tuple-element.148), channel_id=1, source_target_pairs={{0,2},{1,3},{2,0},{3,1},{4,6},{5,7},{6,4},{7,5},{8,10},{9,11},{10,... | collective-permute-start | bytes 786440 | tf_op jit(solution)/shard_map/ppermute | solution.py:74
  277.8 28.6 %collective-permute-start.18 = (bf16[512,256]{1,0:T(8,128)(2,1)}, bf16[512,256]{1,0:T(8,128)(2,1)}, u32[]{:S(2)}, u32[]{:S(2)}) collective-permute-start(bf16[512,256]{1,0:T(8,128)(2,1)} %get-tuple-element.149), channel_id=1, source_target_pairs={{0,1},{1,0},{2,3},{3,2},{4,5},{5,4},{6,7},{7,6},{8,9},{9,8},{10,11... | collective-permute-start | bytes 786440 | tf_op jit(solution)/shard_map/ppermute | solution.py:74
  277.8 28.6 %collective-permute-start.19 = (bf16[512,256]{1,0:T(8,128)(2,1)}, bf16[512,256]{1,0:T(8,128)(2,1)}, u32[]{:S(2)}, u32[]{:S(2)}) collective-permute-start(bf16[512,256]{1,0:T(8,128)(2,1)} %get-tuple-element.150), channel_id=1, source_target_pairs={{0,3},{1,2},{2,1},{3,0},{4,7},{5,6},{6,5},{7,4},{8,11},{9,10},{10,... | collective-permute-start | bytes 786440 | tf_op jit(solution)/shard_map/ppermute | solution.py:74
  366.4 22.6 %collective-permute-start.20 = (bf16[512,256]{1,0:T(8,128)(2,1)}, bf16[512,256]{1,0:T(8,128)(2,1)}, u32[]{:S(2)}, u32[]{:S(2)}) collective-permute-start(bf16[512,256]{1,0:T(8,128)(2,1)} %get-tuple-element.159), channel_id=1, source_target_pairs={{0,2},{1,3},{2,0},{3,1},{4,6},{5,7},{6,4},{7,5},{8,10},{9,11},{10,... | collective-permute-start | bytes 786440 | tf_op jit(solution)/shard_map/ppermute | solution.py:74
  366.4 22.5 %collective-permute-start.21 = (bf16[512,256]{1,0:T(8,128)(2,1)}, bf16[512,256]{1,0:T(8,128)(2,1)}, u32[]{:S(2)}, u32[]{:S(2)}) collective-permute-start(bf16[512,256]{1,0:T(8,128)(2,1)} %get-tuple-element.160), channel_id=1, source_target_pairs={{0,1},{1,0},{2,3},{3,2},{4,5},{5,4},{6,7},{7,6},{8,9},{9,8},{10,11... | collective-permute-start | bytes 786440 | tf_op jit(solution)/shard_map/ppermute | solution.py:74
  447.1 27.7 %collective-permute-start.24 = (bf16[1,512,1024]{2,1,0:T(8,128)(2,1)}, bf16[1,512,1024]{2,1,0:T(8,128)(2,1)}, u32[]{:S(2)}, u32[]{:S(2)}) collective-permute-start(bf16[1,512,1024]{2,1,0:T(8,128)(2,1)} %add_convert_fusion.10), channel_id=1, source_target_pairs={{0,2},{1,3},{2,0},{3,1},{4,6},{5,7},{6,4},{7,5},{8,10},{9,11},{10,... | collective-permute-start | bytes 3145736 | tf_op jit(solution)/shard_map/ppermute | solution.py:74
  493.4 49.9 %collective-permute-start.26 = (bf16[2,2,4,128,1024]{4,3,2,1,0:T(8,128)(2,1)}, bf16[2,2,4,128,1024]{4,3,2,1,0:T(8,128)(2,1)}, u32[]{:S(2)}, u32[]{:S(2)}) collective-permute-start(bf16[2,2,4,128,1024]{4,3,2,1,0:T(8,128)(2,1)} %get-tuple-element.199), channel_id=1, source_target_pairs={{0,1},{1,0},{2,3},{3,2},{4,5},{5,4},{6,7},{7,6},{8,9},{9,8},{10,11... | collective-permute-start | bytes 12582920 | tf_op jit(solution)/shard_map/ppermute | solution.py:74
  507.6 33.7 %collective-permute-start.28 = (bf16[1,128,768]{2,1,0:T(8,128)(2,1)}, bf16[1,128,768]{2,1,0:T(8,128)(2,1)}, u32[]{:S(2)}, u32[]{:S(2)}) collective-permute-start(bf16[1,128,768]{2,1,0:T(8,128)(2,1)} %add_convert_fusion.22), channel_id=1, source_target_pairs={{0,16},{4,20},{8,24},{12,28},{16,0},{20,4},{24,8},{28,12},{1,17},{... | collective-permute-start | bytes 589832 | tf_op jit(solution)/shard_map/ppermute | solution.py:74
  570.3 84.7 %collective-permute-start.33 = (bf16[1,2,4,128,1280]{4,3,2,1,0:T(8,128)(2,1)}, bf16[1,2,4,128,1280]{4,3,2,1,0:T(8,128)(2,1)}, u32[]{:S(2)}, u32[]{:S(2)}) collective-permute-start(bf16[1,2,4,128,1280]{4,3,2,1,0:T(8,128)(2,1)} %get-tuple-element.224), channel_id=1, source_target_pairs={{0,2},{1,3},{2,0},{3,1},{4,6},{5,7},{6,4},{7,5},{8,10},{9,11},{10,... | collective-permute-start | bytes 7864328 | tf_op jit(solution)/shard_map/ppermute | solution.py:74
  572.0 71.1 %collective-permute-start.34 = (bf16[1,2,4,128,1024]{4,3,2,1,0:T(8,128)(2,1)}, bf16[1,2,4,128,1024]{4,3,2,1,0:T(8,128)(2,1)}, u32[]{:S(2)}, u32[]{:S(2)}) collective-permute-start(bf16[1,2,4,128,1024]{4,3,2,1,0:T(8,128)(2,1)} %get-tuple-element.225), channel_id=1, source_target_pairs={{0,4},{4,0},{8,12},{12,8},{16,20},{20,16},{24,28},{28,24},{1,5},{5... | collective-permute-start | bytes 6291464 | tf_op jit(solution)/shard_map/ppermute | solution.py:74
  666.2 30.6 %collective-permute-start.48 = (bf16[1,4,128,1024]{3,2,1,0:T(8,128)(2,1)}, bf16[1,4,128,1024]{3,2,1,0:T(8,128)(2,1)}, u32[]{:S(2)}, u32[]{:S(2)}) collective-permute-start(bf16[1,4,128,1024]{3,2,1,0:T(8,128)(2,1)} %get-tuple-element.252), channel_id=1, source_target_pairs={{0,2},{1,3},{2,0},{3,1},{4,6},{5,7},{6,4},{7,5},{8,10},{9,11},{10,... | collective-permute-start | bytes 3145736 | tf_op jit(solution)/shard_map/ppermute | solution.py:74
  668.9 49.7 %collective-permute-start.36 = (bf16[1,512,1024]{2,1,0:T(8,128)(2,1)}, bf16[1,512,1024]{2,1,0:T(8,128)(2,1)S(1)}, u32[]{:S(2)}, u32[]{:S(2)}) collective-permute-start(bf16[1,512,1024]{2,1,0:T(8,128)(2,1)} %add_convert_fusion.6), channel_id=1, source_target_pairs={{0,2},{1,3},{2,0},{3,1},{4,6},{5,7},{6,4},{7,5},{8,10},{9,11},{10,... | collective-permute-start | bytes 3145736 | tf_op jit(solution)/shard_map/ppermute | solution.py:74
  674.1 87.0 %collective-permute-start.45 = (bf16[1,4,128,1280]{3,2,1,0:T(8,128)(2,1)}, bf16[1,4,128,1280]{3,2,1,0:T(8,128)(2,1)}, u32[]{:S(2)}, u32[]{:S(2)}) collective-permute-start(bf16[1,4,128,1280]{3,2,1,0:T(8,128)(2,1)} %get-tuple-element.249), channel_id=1, source_target_pairs={{0,4},{4,0},{8,12},{12,8},{16,20},{20,16},{24,28},{28,24},{1,5},{5... | collective-permute-start | bytes 3932168 | tf_op jit(solution)/shard_map/ppermute | solution.py:74
  699.8 68.0 %collective-permute-start.49 = (bf16[2,128,1024]{2,1,0:T(8,128)(2,1)}, bf16[2,128,1024]{2,1,0:T(8,128)(2,1)}, u32[]{:S(2)}, u32[]{:S(2)}) collective-permute-start(bf16[2,128,1024]{2,1,0:T(8,128)(2,1)} %get-tuple-element.315), channel_id=1, source_target_pairs={{0,8},{4,12},{8,0},{12,4},{16,24},{20,28},{24,16},{28,20},{1,9},{5... | collective-permute-start | bytes 1572872 | tf_op jit(solution)/shard_map/ppermute | solution.py:74
  731.9 38.8 %collective-permute-start.42 = (bf16[4,128,768]{2,1,0:T(8,128)(2,1)}, bf16[4,128,768]{2,1,0:T(8,128)(2,1)S(1)}, u32[]{:S(2)}, u32[]{:S(2)}) collective-permute-start(bf16[4,128,768]{2,1,0:T(8,128)(2,1)} %get-tuple-element.244), channel_id=1, source_target_pairs={{0,4},{4,0},{8,12},{12,8},{16,20},{20,16},{24,28},{28,24},{1,5},{5... | collective-permute-start | bytes 2359304 | tf_op jit(solution)/shard_map/ppermute | solution.py:74
  762.7 23.4 %collective-permute-start.46 = (bf16[2,128,1280]{2,1,0:T(8,128)(2,1)S(1)}, bf16[2,128,1280]{2,1,0:T(8,128)(2,1)S(1)}, u32[]{:S(2)}, u32[]{:S(2)}) collective-permute-start(bf16[2,128,1280]{2,1,0:T(8,128)(2,1)S(1)} %get-tuple-element.313), channel_id=1, source_target_pairs={{0,8},{4,12},{8,0},{12,4},{16,24},{20,28},{24,16},{28,20},{1,9},{5... | collective-permute-start | bytes 1966088 | tf_op jit(solution)/shard_map/ppermute | solution.py:74
  771.0 27.8 %collective-permute-start.43 = (bf16[2,128,768]{2,1,0:T(8,128)(2,1)S(1)}, bf16[2,128,768]{2,1,0:T(8,128)(2,1)S(1)}, u32[]{:S(2)}, u32[]{:S(2)}) collective-permute-start(bf16[2,128,768]{2,1,0:T(8,128)(2,1)S(1)} %get-tuple-element.317), channel_id=1, source_target_pairs={{0,8},{4,12},{8,0},{12,4},{16,24},{20,28},{24,16},{28,20},{1,9},{5... | collective-permute-start | bytes 1179656 | tf_op jit(solution)/shard_map/ppermute | solution.py:74
  (85 other events, 1133.8 us)
Sparse Core Ops, SparseCore 0:
  11.5 163.0 all-gather.2
  177.5 128.9 all-gather.4
  459.1 235.1 reduce-scatter.1
